TPU v7x, 256 devices: a whole 4x4x8 slice. The times are simulated.
256 devices in a mesh: line: 8 (over z_hi, core), dp: 32 (over z_lo, x, y).
Axes of the slice: x: 4, y: 4, z: 8 (z_hi: 4, z_lo: 2; z = z_hi * 2 + z_lo), core: 2. Of those that a mesh axis runs over, the one named last changes fastest.
Arguments:
- fields: bfloat16 [32, 4096, 128], P('dp', 'line'), may hold values from -6 to 6
- cotangent: bfloat16 [32, 4096, 128], P('dp', 'line'), may hold values from -6 to 6
- norm_gain: float32 [3, 128], replicated, may hold values from 0.1 to 1.9
- kernel: float32 [3, 15, 128], replicated, may hold values from -1.8 to 1.8
- mix_weight: bfloat16 [3, 128, 128], replicated, may hold values from -0.5 to 0.5
- line_order: int32 [3, 4096], P(None, 'line'), may hold values from 0 to 511, as said below
- line_starts: int32 [3, 32], P(None, 'line'), may hold values from 0 to 32
Outputs:
- imitated: bfloat16 [32, 4096, 128], P('dp', 'line')
- field_grad: bfloat16 [32, 4096, 128], P('dp', 'line')
- mix_grad: float32 [3, 128, 128], replicated
- kernel_grad: float32 [3, 15, 128], replicated
- gain_grad: float32 [3, 128], replicated
Inputs may be any that keep to these rules, and one draw needn't show every extreme that they name: For each direction, every aligned block of 512 entries of line_order is a permutation of 0 to 511.
All inputs are finite; a program needn't handle non-finite values.
Results may differ from a plain program's by a relative error of at most 0.014.
Values may be sent and summed in bfloat16 or wider, within the bound.
No kernel may reach another device: no remote copies, remote signals or barrier semaphores. Data moves between devices by JAX's collectives and lax.ppermute only.
A program may use at most 64 MiB of HBM per device.

v0:
```python
import jax
import jax.numpy as jnp
from jax import lax
from jax.sharding import PartitionSpec as P

LINE = 128


EPSILON = 1e-06


def tap_offsets():
    offsets = [0]
    for dilation_level in range(7):
        offsets = offsets + [-(2**dilation_level), 2**dilation_level]
    return offsets


def shifted(values, offset):
    if offset > 0:
        return jnp.concatenate([values[:, offset:], jnp.zeros_like(values[:, :offset])], axis=1)
    if offset < 0:
        return jnp.concatenate([jnp.zeros_like(values[:, offset:]), values[:, :offset]], axis=1)
    return values


def depthwise(inputs, weights):
    running = jnp.zeros(inputs.shape, jnp.float32)
    for tap_index, offset in enumerate(tap_offsets()):
        running = running + weights[tap_index] * shifted(inputs, offset)
    return running


def depthwise_transpose(grads, weights):
    running = jnp.zeros(grads.shape, jnp.float32)
    for tap_index, offset in enumerate(tap_offsets()):
        running = running + weights[tap_index] * shifted(grads, -offset)
    return running


def kernel_terms(grads, inputs):
    return jnp.stack(
        [jnp.sum(grads * shifted(inputs, offset), axis=(0, 1)) for offset in tap_offsets()]
    )


def block_view(array, line_count):
    batch_len, cell_count, channels = array.shape
    return array.reshape(batch_len, line_count, cell_count // line_count, channels)


def unpermute(array, table):
    return jnp.zeros_like(array).at[:, table].set(array)


def into_lines(array, table, shift, line_count):
    rolled = jnp.roll(block_view(array, line_count), shift, axis=1).reshape(array.shape)
    received = lax.all_to_all(rolled, "line", split_axis=1, concat_axis=1, tiled=True)
    return jnp.take(received, table, axis=1)


def out_of_lines(array, table, shift, line_count):
    placed = unpermute(array, table)
    received = lax.all_to_all(placed, "line", split_axis=1, concat_axis=1, tiled=True)
    return jnp.roll(block_view(received, line_count), -shift, axis=1).reshape(array.shape)


def norm_forward(stream, gain_row):
    values = stream.astype(jnp.float32)
    inverse = lax.rsqrt(jnp.mean(values * values, axis=-1, keepdims=True) + EPSILON)
    scaled = values * inverse
    normed = (scaled * gain_row).astype(jnp.bfloat16)
    return (values, inverse, scaled, normed)


def norm_backward(grad_cells, inverse, scaled, gain_row, grad_stream):
    cells_f = grad_cells.astype(jnp.float32)
    gain_part = jnp.sum(cells_f * scaled, axis=(0, 1))
    weighted = cells_f * gain_row
    grad_norm = inverse * (weighted - scaled * jnp.mean(weighted * scaled, axis=-1, keepdims=True))
    return (gain_part, (grad_stream.astype(jnp.float32) + grad_norm).astype(jnp.bfloat16))


def line_forward(regrouped, keep_mask, weights, mixing):
    channels = regrouped.shape[2]
    lined = regrouped.reshape(-1, LINE, channels)
    masked = jnp.where(keep_mask[:, :, None], lined, jnp.zeros_like(lined))
    hidden = depthwise(masked.astype(jnp.float32), weights)
    activated = jax.nn.silu(hidden).astype(jnp.bfloat16)
    mixed = jnp.dot(
        activated.reshape(-1, channels), mixing, preferred_element_type=jnp.float32
    ).astype(jnp.bfloat16)
    return (masked, hidden, activated, mixed.reshape(regrouped.shape))


def line_backward(grad_mixed, masked, hidden, activated, keep_mask, weights, mixing):
    channels = grad_mixed.shape[2]
    flat_grad = grad_mixed.reshape(-1, channels)
    mix_part = jnp.einsum(
        "nc,nd->cd", activated.reshape(-1, channels), flat_grad, preferred_element_type=jnp.float32
    )
    grad_act = jnp.einsum(
        "nd,cd->nc", flat_grad, mixing, preferred_element_type=jnp.float32
    ).reshape(hidden.shape)
    gate_value = jax.nn.sigmoid(hidden)
    grad_hidden = (grad_act * (gate_value * (1.0 + hidden * (1.0 - gate_value)))).astype(
        jnp.bfloat16
    )
    hidden_grad_f = grad_hidden.astype(jnp.float32)
    kernel_part = kernel_terms(hidden_grad_f, masked.astype(jnp.float32))
    grad_masked = depthwise_transpose(hidden_grad_f, weights)
    grad_normed = jnp.where(keep_mask[:, :, None], grad_masked, jnp.zeros_like(grad_masked)).astype(
        jnp.bfloat16
    )
    return (mix_part, kernel_part, grad_normed.reshape(grad_mixed.shape))


def body(fields, cotangent, norm_gain, kernel, mix_weight, line_order, line_starts):
    line_count = lax.axis_size("line")
    line_rank = lax.axis_index("line")
    batch_len = fields.shape[0]
    cell_count = fields.shape[1]
    positions = jnp.arange(LINE, dtype=jnp.int32)
    masks = [
        jnp.tile(positions[None, :] >= line_starts[direction][:, None], (batch_len, 1))
        for direction in range(3)
    ]
    grad_scale = float(lax.axis_size("dp") * batch_len * line_count * cell_count) ** (-0.5)
    collected = []

    def collect(mix_part, kernel_part, gain_part):
        collected.append((mix_part, kernel_part, gain_part))

    saved = []
    stream = fields
    for direction in range(3):
        values, inverse, scaled, normed = norm_forward(stream, norm_gain[direction])
        regrouped = into_lines(normed, line_order[direction], direction * line_rank, line_count)
        masked, hidden, activated, mixed = line_forward(
            regrouped, masks[direction], kernel[direction], mix_weight[direction]
        )
        returned = out_of_lines(mixed, line_order[direction], direction * line_rank, line_count)
        saved.append((inverse, scaled, masked, hidden, activated))
        stream = (values + returned.astype(jnp.float32)).astype(jnp.bfloat16)
    grad_stream = cotangent
    for direction in (2, 1, 0):
        inverse, scaled, masked, hidden, activated = saved[direction]
        grad_mixed = into_lines(
            grad_stream, line_order[direction], direction * line_rank, line_count
        )
        mix_part, kernel_part, grad_normed = line_backward(
            grad_mixed,
            masked,
            hidden,
            activated,
            masks[direction],
            kernel[direction],
            mix_weight[direction],
        )
        grad_cells = out_of_lines(
            grad_normed, line_order[direction], direction * line_rank, line_count
        )
        gain_part, grad_stream = norm_backward(
            grad_cells, inverse, scaled, norm_gain[direction], grad_stream
        )
        collect(mix_part, kernel_part, gain_part)
    ordered = collected[::-1]
    mix_stack = jnp.stack([entry[0] for entry in ordered])
    kernel_stack = jnp.stack([entry[1] for entry in ordered])
    gain_stack = jnp.stack([entry[2] for entry in ordered])
    mix_stack, kernel_stack, gain_stack = lax.psum(
        (mix_stack, kernel_stack, gain_stack), ("line", "dp")
    )
    return (
        stream,
        grad_stream,
        mix_stack * grad_scale,
        kernel_stack * grad_scale,
        gain_stack * grad_scale,
    )


def solution(mesh):
    in_specs = (
        P("dp", "line", None),
        P("dp", "line", None),
        P(),
        P(),
        P(),
        P(None, "line"),
        P(None, "line"),
    )
    out_specs = (P("dp", "line", None), P("dp", "line", None), P(), P(), P())
    return jax.shard_map(body, mesh=mesh, in_specs=in_specs, out_specs=out_specs, check_vma=False)
```

profile of v0, /device:TPU:1, one launch (start us, length us, event | category | flops | bytes accessed | tf_op | source)
XLA Modules:
  0.0 574.2 jit_solution(12604991823495048007)
XLA Ops:
  12.4 10.1 %all-to-all-start = ((bf16[8,2,4096]{2,1,0:T(2,128)(2,1)}), bf16[8,2,4096]{2,1,0:T(2,128)(2,1)S(1)}, u32[]{:S(2)}, u32[]{:S(2)}) async-start(bf16[8,2,4096]{2,1,0:T(2,128)(2,1)} %reshape.868), calls=%async_computation | async-start | bytes 262144 | tf_op jit(solution)/shard_map/all_to_all | solution.py:58
  24.6 6.0 %all-to-all-done = bf16[8,2,4096]{2,1,0:T(2,128)(2,1)S(1)} async-done(((bf16[8,2,4096]{2,1,0:T(2,128)(2,1)}), bf16[8,2,4096]{2,1,0:T(2,128)(2,1)S(1)}, u32[]{:S(2)}, u32[]{:S(2)}) %all-to-all-start) | async-done | bytes 131104 | tf_op jit(solution)/shard_map/all_to_all | solution.py:58
  38.9 4.8 all-to-all-start.1
  44.9 7.1 %all-to-all-done.1 = bf16[8,2,4096]{2,1,0:T(2,128)(2,1)S(1)} async-done(((bf16[8,2,4096]{2,1,0:T(2,128)(2,1)}), bf16[8,2,4096]{2,1,0:T(2,128)(2,1)S(1)}, u32[]{:S(2)}, u32[]{:S(2)}) %all-to-all-start.1) | async-done | bytes 131104 | tf_op jit(solution)/shard_map/all_to_all | solution.py:64
  54.7 4.7 all-to-all-start.2
  60.0 7.5 %all-to-all-done.2 = bf16[8,2,4096]{2,1,0:T(2,128)(2,1)S(1)} async-done(((bf16[8,2,4096]{2,1,0:T(2,128)(2,1)}), bf16[8,2,4096]{2,1,0:T(2,128)(2,1)S(1)}, u32[]{:S(2)}, u32[]{:S(2)}) %all-to-all-start.2) | async-done | bytes 131104 | tf_op jit(solution)/shard_map/all_to_all | solution.py:58
  77.0 4.8 all-to-all-start.3
  84.1 5.9 %all-to-all-done.3 = bf16[8,2,4096]{2,1,0:T(2,128)(2,1)S(1)} async-done(((bf16[8,2,4096]{2,1,0:T(2,128)(2,1)}), bf16[8,2,4096]{2,1,0:T(2,128)(2,1)S(1)}, u32[]{:S(2)}, u32[]{:S(2)}) %all-to-all-start.3) | async-done | bytes 131104 | tf_op jit(solution)/shard_map/all_to_all | solution.py:64
  90.0 4.7 all-to-all-start.6
  98.2 4.7 all-to-all-done.6
  102.9 5.3 all-to-all-start.4
  109.7 6.8 %all-to-all-done.4 = bf16[8,2,4096]{2,1,0:T(2,128)(2,1)} async-done(((bf16[8,2,4096]{2,1,0:T(2,128)(2,1)}), bf16[8,2,4096]{2,1,0:T(2,128)(2,1)}, u32[]{:S(2)}, u32[]{:S(2)}) %all-to-all-start.4) | async-done | bytes 131104 | tf_op jit(solution)/shard_map/all_to_all | solution.py:58
  139.3 5.3 all-to-all-start.5
  152.9 7.1 %all-to-all-start.7 = ((bf16[8,2,4096]{2,1,0:T(2,128)(2,1)}), bf16[8,2,4096]{2,1,0:T(2,128)(2,1)S(1)}, u32[]{:S(2)}, u32[]{:S(2)}) async-start(bf16[8,2,4096]{2,1,0:T(2,128)(2,1)} %reshape.882), calls=%async_computation.7 | async-start | bytes 262144 | tf_op jit(solution)/shard_map/all_to_all | solution.py:64
  162.0 6.0 %all-to-all-done.7 = bf16[8,2,4096]{2,1,0:T(2,128)(2,1)S(1)} async-done(((bf16[8,2,4096]{2,1,0:T(2,128)(2,1)}), bf16[8,2,4096]{2,1,0:T(2,128)(2,1)S(1)}, u32[]{:S(2)}, u32[]{:S(2)}) %all-to-all-start.7) | async-done | bytes 131104 | tf_op jit(solution)/shard_map/all_to_all | solution.py:64
  173.0 11.9 %all_to_all.60 = bf16[8,2,4096]{2,1,0:T(2,128)(2,1)S(1)} all-to-all(bf16[8,2,4096]{2,1,0:T(2,128)(2,1)S(1)} %reshape.884), channel_id=1, replica_groups=mesh['line'=8,'dp'=32] {'line'}, dimensions={0} | all-to-all | bytes 262144 | tf_op jit(solution)/shard_map/all_to_all | solution.py:58
  189.5 2.9 fusion.54
  198.8 4.8 all-to-all-start.9
  204.3 7.5 %all-to-all-done.9 = bf16[8,2,4096]{2,1,0:T(2,128)(2,1)S(1)} async-done(((bf16[8,2,4096]{2,1,0:T(2,128)(2,1)}), bf16[8,2,4096]{2,1,0:T(2,128)(2,1)S(1)}, u32[]{:S(2)}, u32[]{:S(2)}) %all-to-all-start.9) | async-done | bytes 131104 | tf_op jit(solution)/shard_map/all_to_all | solution.py:64
  215.7 4.8 all-to-all-start.10
  223.3 5.4 all-to-all-done.10
  243.7 4.7 all-to-all-start.11
  249.1 236.5 %all-reduce.87.cloned.1.call-done = f32[3,128,128]{2,1,0:T(8,128)} async-done(((f32[3,128,128]{2,1,0:T(8,128)}), f32[3,128,128]{2,1,0:T(8,128)}) %all-reduce.87.cloned.1.call-update) | async-done | bytes 196624 | tf_op jit(solution)/shard_map/psum | solution.py:171
  488.8 76.0 %all-reduce.84 = (f32[3,15,128]{2,1,0:T(8,128)S(1)}, f32[3,128]{1,0:T(4,128)S(1)}) all-reduce(f32[3,15,128]{2,1,0:T(8,128)S(1)} %pad_maximum_fusion.1, f32[3,128]{1,0:T(4,128)S(1)} %pad_maximum_fusion.2), channel_id=1, replica_groups=mesh['line'=8,'dp'=32] {'line','dp'}, use_global_device_ids=true, to_apply=%region_58.62 | all-reduce | flops 6144 | bytes 49152 | tf_op jit(solution)/shard_map/psum | solution.py:171
  (515 shorter events, 112.1 us)
Async XLA Ops:
  8.5 43.7 %copy-start.48 = (f32[128]{0:T(128)}, f32[128]{0:T(128)S(1)}, u32[]{:S(2)}) copy-start(f32[128]{0:T(128)S(1)} %get-tuple-element.213) | copy-start | bytes 1540
  12.4 10.1 %copy-start.43 = (s32[3,512]{1,0:T(4,128)S(1)}, s32[3,512]{1,0:T(4,128)}, u32[]{:S(2)}) copy-start(s32[3,512]{1,0:T(4,128)} %param.18) | copy-start | bytes 18436
  12.4 10.1 %copy-start.42 = (f32[3,15,128]{2,1,0:T(8,128)S(1)}, f32[3,15,128]{2,1,0:T(8,128)}, u32[]{:S(2)}) copy-start(f32[3,15,128]{2,1,0:T(8,128)} %param.16) | copy-start | bytes 69124
  12.4 18.1 %all-to-all-start = ((bf16[8,2,4096]{2,1,0:T(2,128)(2,1)}), bf16[8,2,4096]{2,1,0:T(2,128)(2,1)S(1)}, u32[]{:S(2)}, u32[]{:S(2)}) async-start(bf16[8,2,4096]{2,1,0:T(2,128)(2,1)} %reshape.868), calls=%async_computation | async-start | bytes 262144 | tf_op jit(solution)/shard_map/all_to_all | solution.py:58
  24.6 10.3 %copy-start.117 = (s32[512,1]{0,1:T(1,128)}, s32[512,1]{0,1:T(1,128)S(1)}, u32[]{:S(2)}) copy-start(s32[512,1]{0,1:T(1,128)S(1)} %get-tuple-element.206) | copy-start | bytes 6148
  38.9 13.0 %all-to-all-start.1 = ((bf16[8,2,4096]{2,1,0:T(2,128)(2,1)}), bf16[8,2,4096]{2,1,0:T(2,128)(2,1)S(1)}, u32[]{:S(2)}, u32[]{:S(2)}) async-start(bf16[8,2,4096]{2,1,0:T(2,128)(2,1)} %reshape.870), calls=%async_computation.1 | async-start | bytes 262144 | tf_op jit(solution)/shard_map/all_to_all | solution.py:64
  44.3 25.4 %copy-start.50 = (pred[4,128]{1,0:T(4,128)(4,1)}, pred[4,128]{1,0:T(4,128)(4,1)S(1)}, u32[]{:S(2)}) copy-start(pred[4,128]{1,0:T(4,128)(4,1)S(1)} %get-tuple-element.222) | copy-start | bytes 1540
  44.9 24.2 %copy-start.98 = (pred[512]{0:T(512)(128)(4,1)}, pred[512]{0:T(512)(128)(4,1)S(1)}, u32[]{:S(2)}) copy-start(pred[512]{0:T(512)(128)(4,1)S(1)} %get-tuple-element.220) | copy-start | bytes 1540
  54.7 12.9 %all-to-all-start.2 = ((bf16[8,2,4096]{2,1,0:T(2,128)(2,1)}), bf16[8,2,4096]{2,1,0:T(2,128)(2,1)S(1)}, u32[]{:S(2)}, u32[]{:S(2)}) async-start(bf16[8,2,4096]{2,1,0:T(2,128)(2,1)} %reshape.872), calls=%async_computation.2 | async-start | bytes 262144 | tf_op jit(solution)/shard_map/all_to_all | solution.py:58
  60.0 9.8 %copy-start.84 = (f32[128]{0:T(128)}, f32[128]{0:T(128)S(1)}, u32[]{:S(2)}) copy-start(f32[128]{0:T(128)S(1)} %get-tuple-element.170) | copy-start | bytes 1540
  60.0 9.8 %copy-start.86 = (f32[128]{0:T(128)}, f32[128]{0:T(128)S(1)}, u32[]{:S(2)}) copy-start(f32[128]{0:T(128)S(1)} %get-tuple-element.171) | copy-start | bytes 1540
  60.0 9.8 %copy-start.88 = (f32[128]{0:T(128)}, f32[128]{0:T(128)S(1)}, u32[]{:S(2)}) copy-start(f32[128]{0:T(128)S(1)} %get-tuple-element.172) | copy-start | bytes 1540
  60.0 9.8 %copy-start.90 = (f32[128]{0:T(128)}, f32[128]{0:T(128)S(1)}, u32[]{:S(2)}) copy-start(f32[128]{0:T(128)S(1)} %get-tuple-element.173) | copy-start | bytes 1540
  60.0 9.8 %copy-start.92 = (f32[128]{0:T(128)}, f32[128]{0:T(128)S(1)}, u32[]{:S(2)}) copy-start(f32[128]{0:T(128)S(1)} %get-tuple-element.174) | copy-start | bytes 1540
  60.0 9.8 %copy-start.94 = (f32[128]{0:T(128)}, f32[128]{0:T(128)S(1)}, u32[]{:S(2)}) copy-start(f32[128]{0:T(128)S(1)} %get-tuple-element.175) | copy-start | bytes 1540
  77.0 13.0 %all-to-all-start.3 = ((bf16[8,2,4096]{2,1,0:T(2,128)(2,1)}), bf16[8,2,4096]{2,1,0:T(2,128)(2,1)S(1)}, u32[]{:S(2)}, u32[]{:S(2)}) async-start(bf16[8,2,4096]{2,1,0:T(2,128)(2,1)} %reshape.874), calls=%async_computation.3 | async-start | bytes 262144 | tf_op jit(solution)/shard_map/all_to_all | solution.py:64
  90.0 12.9 %all-to-all-start.6 = ((bf16[8,2,4096]{2,1,0:T(2,128)(2,1)}), bf16[8,2,4096]{2,1,0:T(2,128)(2,1)S(1)}, u32[]{:S(2)}, u32[]{:S(2)}) async-start(bf16[8,2,4096]{2,1,0:T(2,128)(2,1)} %reshape.880), calls=%async_computation.6 | async-start | bytes 262144 | tf_op jit(solution)/shard_map/all_to_all | solution.py:58
  102.9 13.6 %all-to-all-start.4 = ((bf16[8,2,4096]{2,1,0:T(2,128)(2,1)}), bf16[8,2,4096]{2,1,0:T(2,128)(2,1)}, u32[]{:S(2)}, u32[]{:S(2)}) async-start(bf16[8,2,4096]{2,1,0:T(2,128)(2,1)} %reshape.876), calls=%async_computation.4 | async-start | bytes 262144 | tf_op jit(solution)/shard_map/all_to_all | solution.py:58
  139.3 13.6 %all-to-all-start.5 = ((bf16[8,2,4096]{2,1,0:T(2,128)(2,1)}), bf16[8,2,4096]{2,1,0:T(2,128)(2,1)}, u32[]{:S(2)}, u32[]{:S(2)}) async-start(bf16[8,2,4096]{2,1,0:T(2,128)(2,1)} %reshape.878), calls=%async_computation.5 | async-start | bytes 262144 | tf_op jit(solution)/shard_map/all_to_all | solution.py:64
  152.9 15.1 %all-to-all-start.7 = ((bf16[8,2,4096]{2,1,0:T(2,128)(2,1)}), bf16[8,2,4096]{2,1,0:T(2,128)(2,1)S(1)}, u32[]{:S(2)}, u32[]{:S(2)}) async-start(bf16[8,2,4096]{2,1,0:T(2,128)(2,1)} %reshape.882), calls=%async_computation.7 | async-start | bytes 262144 | tf_op jit(solution)/shard_map/all_to_all | solution.py:64
  198.8 13.0 %all-to-all-start.9 = ((bf16[8,2,4096]{2,1,0:T(2,128)(2,1)}), bf16[8,2,4096]{2,1,0:T(2,128)(2,1)S(1)}, u32[]{:S(2)}, u32[]{:S(2)}) async-start(bf16[8,2,4096]{2,1,0:T(2,128)(2,1)} %reshape.886), calls=%async_computation.9 | async-start | bytes 262144 | tf_op jit(solution)/shard_map/all_to_all | solution.py:64
  215.7 13.0 %all-to-all-start.10 = ((bf16[8,2,4096]{2,1,0:T(2,128)(2,1)}), bf16[8,2,4096]{2,1,0:T(2,128)(2,1)S(1)}, u32[]{:S(2)}, u32[]{:S(2)}) async-start(bf16[8,2,4096]{2,1,0:T(2,128)(2,1)} %reshape.888), calls=%async_computation.10 | async-start | bytes 262144 | tf_op jit(solution)/shard_map/all_to_all | solution.py:58
  220.5 265.1 %all-reduce.87.cloned.1.call-start = ((), (), s32[]{:S(2)}) async-start(), calls=%async_computation.12 | async-start | bytes 393216 | tf_op jit(solution)/shard_map/psum | solution.py:171
  243.7 243.5 %all-to-all-start.11 = ((bf16[8,2,4096]{2,1,0:T(2,128)(2,1)}), bf16[8,2,4096]{2,1,0:T(2,128)(2,1)S(1)}, u32[]{:S(2)}, u32[]{:S(2)}) async-start(bf16[8,2,4096]{2,1,0:T(2,128)(2,1)} %reshape.890), calls=%async_computation.11 | async-start | bytes 262144 | tf_op jit(solution)/shard_map/all_to_all | solution.py:64
  (150 other events, 411.8 us)
Sparse Core Ops, SparseCore 0:
  236.7 248.7 all-reduce.86
where the time goes:
time: 584 us; the launch traced here: 574 us
  waiting for transfers between devices  293 us (50%)
  blocking collectives  87.9 us (15%)
  local copies, waits for them, and re-layouts  65.3 us (11%)
  starting transfers between devices  61.2 us (10%)
  other arithmetic  39.9 us (7%)
  between operations  17 us (3%)
  matrix products  9.42 us (2%)
    psum x1, waiting for transfers between devices, body(): lax.psum((mix_stack, kernel_stack, gain_stack), ('line', 'dp'))  236 us
    psum x1, blocking collectives, body(): lax.psum((mix_stack, kernel_stack, gain_stack), ('line', 'dp'))  76 us
    all_to_all x6, starting transfers between devices, out_of_lines(): lax.all_to_all(placed, 'line', split_axis=1, concat_axis=1, tiled=True)  31.5 us
    all_to_all x5, waiting for transfers between devices, into_lines(): lax.all_to_all(rolled, 'line', split_axis=1, concat_axis=1, tiled=True)  30.4 us
    all_to_all x5, starting transfers between devices, into_lines(): lax.all_to_all(rolled, 'line', split_axis=1, concat_axis=1, tiled=True)  29.5 us
    unnamed x359, local copies, waits for them, and re-layouts  29.1 us
    all_to_all x6, waiting for transfers between devices, out_of_lines(): lax.all_to_all(placed, 'line', split_axis=1, concat_axis=1, tiled=True)  26.5 us
    unnamed x12, other arithmetic  17.3 us
  transfers between devices with their start and end apart: 12, of which 11 were waited for; matrix products, arithmetic and copies ran while one was open for 5% of the time, Pallas kernels for 0%

commit v1 on v0

v1 whole, which is shorter than its diff:
```python
import functools

import jax
import jax.numpy as jnp
from jax import lax
from jax.experimental import pallas as pl
from jax.experimental.pallas import tpu as pltpu
from jax.sharding import PartitionSpec as P

LINE = 128
CH = 128
TAPS = 15
CELLS = 512
NL = 8
Q = CELLS // NL
LINES = CELLS // LINE
EPSILON = 1e-06
OFFSETS = [0] + [s * 2**level for level in range(7) for s in (-1, 1)]
F32 = jnp.float32
BF16 = jnp.bfloat16
ROWS = LINE + TAPS + 1


def dot(a, b, ca, cb):
    return lax.dot_general(a, b, (((ca,), (cb,)), ((), ())), preferred_element_type=F32)


def slot_row(order_row, sign):
    if sign == 0:
        return order_row
    me = lax.axis_index("line")
    home = lax.shift_right_logical(order_row, 6)
    within = jnp.bitwise_and(order_row, Q - 1)
    slot = jnp.bitwise_and(me + sign * home + NL, NL - 1)
    return slot * Q + within


def picks(row, line):
    part = row[:, line * LINE : (line + 1) * LINE]
    wanted = jnp.transpose(jnp.broadcast_to(part, (LINE, LINE)))
    lanes = lax.broadcasted_iota(jnp.int32, (LINE, LINE), 1)
    return jnp.concatenate(
        [jnp.where(wanted == lanes + c * LINE, 1.0, 0.0).astype(BF16) for c in range(LINES)],
        axis=1,
    )


def place(row, values):
    wanted = jnp.broadcast_to(row, (LINE, CELLS))
    out = []
    for c in range(LINES):
        rows = lax.broadcasted_iota(jnp.int32, (LINE, CELLS), 0) + c * LINE
        hot = jnp.where(wanted == rows, 1.0, 0.0).astype(BF16)
        out.append(dot(hot, values, 1, 0).astype(BF16))
    return out


def put(ref, first, blocks):
    for c, block in enumerate(blocks):
        for h in range(LINE // Q):
            ref[c * (LINE // Q) + h, first : first + Q, :] = block[h * Q : (h + 1) * Q]


def shifts(pad, values):
    pad[8 : 8 + LINE, :] = values
    for offset in OFFSETS:
        if offset == 0:
            yield values
        elif abs(offset) < 8:
            yield pad[8 + offset : 8 + offset + LINE, :]
        elif offset > 0:
            yield jnp.concatenate([values[offset:], jnp.zeros((offset, CH), F32)], axis=0)
        else:
            yield jnp.concatenate([jnp.zeros((-offset, CH), F32), values[:offset]], axis=0)


def clear(pad):
    pad[0:8, :] = jnp.zeros((8, CH), F32)
    pad[8 + LINE : 16 + LINE, :] = jnp.zeros((8, CH), F32)


def norm(x, gain, start):
    inverse = lax.rsqrt(jnp.mean(x * x, axis=-1, keepdims=True) + EPSILON)
    scaled = x * inverse
    normed = (scaled * gain).astype(BF16).astype(F32)
    keep = lax.broadcasted_iota(jnp.int32, (LINE, CH), 0) >= start
    return inverse, scaled, jnp.where(keep, normed, 0.0), keep


def conv(pad, masked, taps):
    total = None
    for t, moved in enumerate(shifts(pad, masked)):
        term = taps[t : t + 1, :] * moved
        total = term if total is None else total + term
    return total


def sigmoid(h):
    return 1.0 / (1.0 + jnp.exp(-h))


def forward_line(k, line, x, starts, gain_ref, taps_ref, mix_ref, pad):
    inverse, scaled, masked, keep = norm(x, gain_ref[k : k + 1, :], starts[k, line])
    hidden = conv(pad, masked, taps_ref[k])
    gate = sigmoid(hidden)
    active = (hidden * gate).astype(BF16)
    mixed = dot(active, mix_ref[k], 1, 0).astype(BF16).astype(F32)
    after = (x + mixed).astype(BF16)
    return inverse, scaled, masked, keep, hidden, gate, active, after


def backward_line(k, grad, state, gain_ref, taps_ref, mix_ref, pad, sums):
    inverse, scaled, masked, keep, hidden, gate, active = state
    gain = gain_ref[k : k + 1, :]
    taps = taps_ref[k]
    sums["mix"] = sums["mix"] + dot(active, grad, 0, 0)
    grad_act = dot(grad, mix_ref[k], 1, 1)
    grad_hidden = (grad_act * (gate * (1.0 + hidden * (1.0 - gate)))).astype(BF16).astype(F32)
    total = None
    for t, moved in enumerate(shifts(pad, grad_hidden)):
        u = t if t == 0 else (t + 1 if t % 2 else t - 1)
        term = taps[u : u + 1, :] * moved
        total = term if total is None else total + term
        part = jnp.sum((moved * masked).reshape(LINE // 8, 8, CH), axis=0)
        sums["taps"][u] = part if sums["taps"][u] is None else sums["taps"][u] + part
    cells = jnp.where(keep, total, 0.0).astype(BF16).astype(F32)
    part = jnp.sum((cells * scaled).reshape(LINE // 8, 8, CH), axis=0)
    sums["gain"] = part if sums["gain"] is None else sums["gain"] + part
    weighted = cells * gain
    moved = inverse * (weighted - scaled * jnp.mean(weighted * scaled, axis=-1, keepdims=True))
    return (grad.astype(F32) + moved).astype(BF16)


def new_sums():
    return {"mix": jnp.zeros((CH, CH), F32), "taps": [None] * TAPS, "gain": None}


def write_sums(ref, sums):
    ref[0:CH, :] = sums["mix"]
    rows = [jnp.sum(part, axis=0, keepdims=True) for part in sums["taps"]]
    rows.append(jnp.sum(sums["gain"], axis=0, keepdims=True))
    ref[CH:ROWS, :] = jnp.concatenate(rows, axis=0)


def prep_kernel(fields_ref, cot_ref, out_ref):
    me = lax.axis_index("line")
    for b in range(NL):
        out_ref[b, 0:Q, :] = fields_ref[0, b * Q : (b + 1) * Q, :]
        slot = jnp.bitwise_and(b + 2 * me, NL - 1)
        out_ref[pl.ds(slot, 1), Q : 2 * Q, :] = cot_ref[:, b * Q : (b + 1) * Q, :]


def forward_kernel(k, starts, in_ref, gain_ref, taps_ref, mix_ref, order_ref, out_ref, x_ref, h_ref, pad):
    clear(pad)
    received = in_ref[:, 0:Q, :].reshape(CELLS, CH)
    order = order_ref[k : k + 1, :]
    row = slot_row(order, 0 if k == 0 else -1)
    after = []
    for line in range(LINES):
        x = dot(picks(row, line), received, 1, 0)
        done = forward_line(k, line, x, starts, gain_ref, taps_ref, mix_ref, pad)
        x_ref[line] = x.astype(BF16)
        h_ref[line] = done[4]
        after.append(done[7])
    put(out_ref, 0, place(slot_row(order, 1), jnp.concatenate(after, axis=0)))


def turn_kernel(starts, in_ref, cot_ref, gain_ref, taps_ref, mix_ref, order_ref, out_ref, sum_ref, pad):
    k = 2
    clear(pad)
    received = in_ref[...].reshape(CELLS, CH)
    cot = cot_ref[:, Q : 2 * Q, :].reshape(CELLS, CH)
    order = order_ref[k : k + 1, :]
    row = slot_row(order, -1)
    sums = new_sums()
    after, grads = [], []
    for line in range(LINES):
        x = dot(picks(row, line), received, 1, 0)
        done = forward_line(k, line, x, starts, gain_ref, taps_ref, mix_ref, pad)
        after.append(done[7])
        grad = dot(picks(order, line), cot, 1, 0).astype(BF16)
        grads.append(backward_line(k, grad, done[:7], gain_ref, taps_ref, mix_ref, pad, sums))
    put(out_ref, 0, place(order, jnp.concatenate(after, axis=0)))
    put(out_ref, Q, place(row, jnp.concatenate(grads, axis=0)))
    write_sums(sum_ref, sums)


def backward_kernel(k, starts, in_ref, x_ref, h_ref, gain_ref, taps_ref, mix_ref, order_ref, out_ref, sum_ref, *rest):
    pad = rest[-1]
    clear(pad)
    if k == 1:
        me = lax.axis_index("line")
        for b in range(NL):
            slot = jnp.bitwise_and(b + 2 * me, NL - 1)
            rest[0][:, b * Q : (b + 1) * Q, :] = in_ref[pl.ds(slot, 1), 0:Q, :]
        received = in_ref[:, Q : 2 * Q, :].reshape(CELLS, CH)
    else:
        received = in_ref[...].reshape(CELLS, CH)
    order = order_ref[k : k + 1, :]
    row = slot_row(order, 1)
    sums = new_sums()
    grads = []
    for line in range(LINES):
        grad = dot(picks(row, line), received, 1, 0).astype(BF16)
        x = x_ref[line].astype(F32)
        hidden = h_ref[line]
        inverse, scaled, masked, keep = norm(x, gain_ref[k : k + 1, :], starts[k, line])
        gate = sigmoid(hidden)
        active = (hidden * gate).astype(BF16)
        state = (inverse, scaled, masked, keep, hidden, gate, active)
        grads.append(backward_line(k, grad, state, gain_ref, taps_ref, mix_ref, pad, sums))
    put(out_ref, 0, place(slot_row(order, -1 if k else 0), jnp.concatenate(grads, axis=0)))
    write_sums(sum_ref, sums)


def call(kernel, outs, name, n_in):
    smem = pl.BlockSpec(memory_space=pltpu.SMEM)
    vmem = pl.BlockSpec(memory_space=pltpu.VMEM)
    return pl.pallas_call(
        kernel,
        out_shape=outs,
        in_specs=([smem] if n_in > 2 else [vmem]) + [vmem] * (n_in - 1),
        out_specs=[vmem] * len(outs),
        scratch_shapes=[pltpu.VMEM((LINE + 16, CH), F32)] if n_in > 2 else [],
        name=name,
    )


def shape(*dims, dtype=BF16):
    return jax.ShapeDtypeStruct(dims, dtype)


def exchange(blocks):
    return lax.all_to_all(blocks, "line", split_axis=0, concat_axis=0, tiled=True)


def body(fields, cotangent, norm_gain, kernel, mix_weight, line_order, line_starts):
    dp_size = lax.axis_size("dp")
    weights = (norm_gain, kernel, mix_weight, line_order)
    state = (shape(LINES, LINE, CH), shape(LINES, LINE, CH, dtype=F32))
    sums = shape(ROWS, CH, dtype=F32)
    blocks = shape(NL, Q, CH)
    (packed,) = call(prep_kernel, (shape(NL, 2 * Q, CH),), "prep", 2)(fields, cotangent)
    first = exchange(packed)
    moved, x0, h0 = call(functools.partial(forward_kernel, 0), (blocks, *state), "fwd0", 6)(
        line_starts, first, *weights
    )
    moved, x1, h1 = call(functools.partial(forward_kernel, 1), (blocks, *state), "fwd1", 6)(
        line_starts, exchange(moved), *weights
    )
    moved, sums2 = call(turn_kernel, (shape(NL, 2 * Q, CH), sums), "turn", 7)(
        line_starts, exchange(moved), first, *weights
    )
    moved, sums1, imitated = call(
        functools.partial(backward_kernel, 1), (blocks, sums, shape(1, CELLS, CH)), "bwd1", 8
    )(line_starts, exchange(moved), x1, h1, *weights)
    moved, sums0 = call(functools.partial(backward_kernel, 0), (blocks, sums), "bwd0", 8)(
        line_starts, exchange(moved), x0, h0, *weights
    )
    field_grad = exchange(moved).reshape(1, CELLS, CH)
    grad_scale = float(dp_size * NL * CELLS) ** (-0.5)
    total = jnp.stack([sums0, sums1, sums2]).reshape(NL, 3 * ROWS // NL, CH)
    part = jnp.sum(exchange(total), axis=0)
    step = 1
    while step < dp_size:
        pairs = [(i, i ^ step) for i in range(dp_size)]
        part = part + lax.ppermute(part, "dp", pairs)
        step *= 2
    whole = jnp.broadcast_to((part * grad_scale)[None], (NL, 3 * ROWS // NL, CH))
    whole = exchange(whole).reshape(3, ROWS, CH)
    return (
        imitated,
        field_grad,
        whole[:, :CH],
        whole[:, CH : CH + TAPS],
        whole[:, CH + TAPS],
    )


def solution(mesh):
    in_specs = (
        P("dp", "line", None),
        P("dp", "line", None),
        P(),
        P(),
        P(),
        P(None, "line"),
        P(None, "line"),
    )
    out_specs = (P("dp", "line", None), P("dp", "line", None), P(), P(), P())
    return jax.shard_map(body, mesh=mesh, in_specs=in_specs, out_specs=out_specs, check_vma=False)
```

time: 584 us -> 164 us (0.28); the launches traced: 574 us -> 162 us
  waiting for transfers between devices: 293 us -> 23.4 us
  local copies, waits for them, and re-layouts: 65.3 us -> 3.29 us
  other arithmetic: 39.9 us -> 0.95 us
  starting transfers between devices: 61.2 us -> 22.5 us
  Pallas kernels: 0 us -> 20 us
  between operations: 17 us -> 0.69 us
  matrix products: 9.42 us -> 0 us
    psum x1 -> x0, waiting for transfers between devices: 236 us -> none  [body(): lax.psum((mix_stack, kernel_stack, gain_stack), ('line', 'dp'))]
    all_to_all x1 -> x6, blocking collectives: 11.9 us -> 90.8 us  [exchange(): lax.all_to_all(blocks, 'line', split_axis=0, concat_axis=0, tiled=True)]
    psum x1 -> x0, blocking collectives: 76 us -> none  [body(): lax.psum((mix_stack, kernel_stack, gain_stack), ('line', 'dp'))]
    all_to_all x11 -> x2, starting transfers between devices: 61 us -> 14.3 us  [exchange(): lax.all_to_all(blocks, 'line', split_axis=0, concat_axis=0, tiled=True)]
    all_to_all x11 -> x2, waiting for transfers between devices: 56.9 us -> 17.5 us  [exchange(): lax.all_to_all(blocks, 'line', split_axis=0, concat_axis=0, tiled=True)]
    unnamed x359 -> x6, local copies, waits for them, and re-layouts: 29.1 us -> 1.24 us
    pallas_call x0 -> x6, Pallas kernels: none -> 20 us  [the longest x1 4.6 us: body(): call(turn_kernel, (shape(NL, 2 * Q, CH), sums), 'turn', 7)]
    unnamed x12 -> x0, other arithmetic: 17.3 us -> none
  transfers between devices with their start and end apart: 12 -> 7, of which waited for: 11 -> 6; matrix products, arithmetic and copies ran while one was open for 5% -> 0% of each run, Pallas kernels for 0% -> 0%
where the time goes in v1:
time: 164 us; the launch traced here: 162 us
  blocking collectives  90.8 us (55%)
  waiting for transfers between devices  23.4 us (14%)
  starting transfers between devices  22.5 us (14%)
  Pallas kernels  20 us (12%)
  local copies, waits for them, and re-layouts  3.29 us (2%)
    all_to_all x6, blocking collectives, exchange(): lax.all_to_all(blocks, 'line', split_axis=0, concat_axis=0, tiled=True)  90.8 us
    all_to_all x2, waiting for transfers between devices, exchange(): lax.all_to_all(blocks, 'line', split_axis=0, concat_axis=0, tiled=True)  17.5 us
    all_to_all x2, starting transfers between devices, exchange(): lax.all_to_all(blocks, 'line', split_axis=0, concat_axis=0, tiled=True)  14.3 us
    ppermute x5, starting transfers between devices, body(): part = part + lax.ppermute(part, 'dp', pairs)  8.2 us
    ppermute x5, waiting for transfers between devices, body(): part = part + lax.ppermute(part, 'dp', pairs)  5.95 us
    pallas_call x1, Pallas kernels, body(): call(turn_kernel, (shape(NL, 2 * Q, CH), sums), 'turn', 7)  4.6 us
    pallas_call x1, Pallas kernels, body(): call(functools.partial(forward_kernel, 0), (blocks, *state), 'fwd0', 6)  3.47 us
    pallas_call x1, Pallas kernels, body(): call(functools.partial(forward_kernel, 1), (blocks, *state), 'fwd1', 6)  3.43 us
  transfers between devices with their start and end apart: 7, of which 6 were waited for; matrix products, arithmetic and copies ran while one was open for 0% of the time, Pallas kernels for 0%

profile of v1, /device:TPU:1, one launch (start us, length us, event | category | flops | bytes accessed | tf_op | source)
XLA Modules:
  0.0 161.7 jit_solution(8945989352931785721)
XLA Ops:
  0.6 1.7 %prep.1 = bf16[8,128,128]{2,1,0:T(8,128)(2,1)} custom-call(bf16[1,512,128]{2,1,0:T(8,128)(2,1)} %fields_ref.1, bf16[1,512,128]{2,1,0:T(8,128)(2,1)} %cot_ref.1), custom_call_target="tpu_custom_call" | custom-call | tf_op jit(solution)/shard_map/prep/pallas_call | solution.py:243
  2.3 19.4 %all_to_all.40.in_ref.cot_ref = bf16[8,128,128]{2,1,0:T(8,128)(2,1)} all-to-all(bf16[8,128,128]{2,1,0:T(8,128)(2,1)} %prep.1), channel_id=1, replica_groups=mesh['line'=8,'dp'=32] {'line'}, dimensions={0} | all-to-all | bytes 524288 | tf_op jit(solution)/shard_map/all_to_all | solution.py:234
  21.7 3.5 %fwd0.1 = (bf16[8,64,128]{2,1,0:T(8,128)(2,1)}, bf16[4,128,128]{2,1,0:T(8,128)(2,1)}, f32[4,128,128]{2,1,0:T(8,128)}) custom-call(s32[3,4]{1,0:T(4,128)} %starts.9, bf16[8,128,128]{2,1,0:T(8,128)(2,1)} %all_to_all.40.in_ref.cot_ref, f32[3,128]{1,0:T(4,128)} %gain_ref.9, f32[3,15,128]{2,1,0:T(8,128)} %taps_ref.9, bf16[3,128,128]{2,1,0:T(8,128)(2,1)} %mix_ref.9, ...), custom_call_target="tpu_custom_call" | custom-call | tf_op jit(solution)/shard_map/fwd0/pallas_call | solution.py:245
  25.2 15.0 %all_to_all.41.in_ref = bf16[8,64,128]{2,1,0:T(8,128)(2,1)} all-to-all(bf16[8,64,128]{2,1,0:T(8,128)(2,1)} %get-tuple-element.18), channel_id=1, replica_groups=mesh['line'=8,'dp'=32] {'line'}, dimensions={0} | all-to-all | bytes 262144 | tf_op jit(solution)/shard_map/all_to_all | solution.py:234
  40.2 3.4 %fwd1.1 = (bf16[8,64,128]{2,1,0:T(8,128)(2,1)}, bf16[4,128,128]{2,1,0:T(8,128)(2,1)}, f32[4,128,128]{2,1,0:T(8,128)}) custom-call(s32[3,4]{1,0:T(4,128)} %starts.9, bf16[8,64,128]{2,1,0:T(8,128)(2,1)} %all_to_all.41.in_ref, f32[3,128]{1,0:T(4,128)} %gain_ref.9, f32[3,15,128]{2,1,0:T(8,128)} %taps_ref.9, bf16[3,128,128]{2,1,0:T(8,128)(2,1)} %mix_ref.9, ...), custom_call_target="tpu_custom_call" | custom-call | tf_op jit(solution)/shard_map/fwd1/pallas_call | solution.py:248
  43.6 13.2 %all_to_all.42.in_ref = bf16[8,64,128]{2,1,0:T(8,128)(2,1)} all-to-all(bf16[8,64,128]{2,1,0:T(8,128)(2,1)} %get-tuple-element.19), channel_id=1, replica_groups=mesh['line'=8,'dp'=32] {'line'}, dimensions={0} | all-to-all | bytes 262144 | tf_op jit(solution)/shard_map/all_to_all | solution.py:234
  56.8 4.6 %turn.1 = (bf16[8,128,128]{2,1,0:T(8,128)(2,1)}, f32[144,128]{1,0:T(8,128)}) custom-call(s32[3,4]{1,0:T(4,128)} %starts.9, bf16[8,64,128]{2,1,0:T(8,128)(2,1)} %all_to_all.42.in_ref, bf16[8,128,128]{2,1,0:T(8,128)(2,1)} %all_to_all.40.in_ref.cot_ref, f32[3,128]{1,0:T(4,128)} %gain_ref.9, f32[3,15,128]{2,1,0:T(8,128)} %taps_ref.9, ...), custom_call_target="tpu_custom_call" | custom-call | tf_op jit(solution)/shard_map/turn/pallas_call | solution.py:251
  61.4 14.6 %all_to_all.43.in_ref = bf16[8,128,128]{2,1,0:T(8,128)(2,1)} all-to-all(bf16[8,128,128]{2,1,0:T(8,128)(2,1)} %get-tuple-element.20), channel_id=1, replica_groups=mesh['line'=8,'dp'=32] {'line'}, dimensions={0} | all-to-all | bytes 524288 | tf_op jit(solution)/shard_map/all_to_all | solution.py:234
  76.0 3.4 %bwd1.1 = (bf16[8,64,128]{2,1,0:T(8,128)(2,1)}, f32[144,128]{1,0:T(8,128)}, bf16[1,512,128]{2,1,0:T(8,128)(2,1)}) custom-call(s32[3,4]{1,0:T(4,128)} %starts.9, bf16[8,128,128]{2,1,0:T(8,128)(2,1)} %all_to_all.43.in_ref, bf16[4,128,128]{2,1,0:T(8,128)(2,1)} %get-tuple-element.21.x_ref, f32[4,128,128]{2,1,0:T(8,128)} %get-tuple-element.22.h_ref, ...), custom_call_target="tpu_custom_call" | custom-call | tf_op jit(solution)/shard_map/bwd1/pallas_call | solution.py:254
  79.4 15.0 %all_to_all.44.in_ref = bf16[8,64,128]{2,1,0:T(8,128)(2,1)} all-to-all(bf16[8,64,128]{2,1,0:T(8,128)(2,1)} %get-tuple-element.24), channel_id=1, replica_groups=mesh['line'=8,'dp'=32] {'line'}, dimensions={0} | all-to-all | bytes 262144 | tf_op jit(solution)/shard_map/all_to_all | solution.py:234
  94.4 3.4 %bwd0.1 = (bf16[8,64,128]{2,1,0:T(8,128)(2,1)}, f32[144,128]{1,0:T(8,128)}) custom-call(s32[3,4]{1,0:T(4,128)} %starts.9, bf16[8,64,128]{2,1,0:T(8,128)(2,1)} %all_to_all.44.in_ref, bf16[4,128,128]{2,1,0:T(8,128)(2,1)} %get-tuple-element.25.x_ref, f32[4,128,128]{2,1,0:T(8,128)} %get-tuple-element.26.h_ref, f32[3,128]{1,0:T(4,128)} %gain_ref.9, ...), custom_call_target="tpu_custom_call" | custom-call | tf_op jit(solution)/shard_map/bwd0/pallas_call | solution.py:257
  98.8 13.6 %all_to_all.45 = f32[8,54,128]{2,1,0:T(8,128)S(1)} all-to-all(f32[8,54,128]{2,1,0:T(8,128)S(1)} %reshape.21), channel_id=1, replica_groups=mesh['line'=8,'dp'=32] {'line'}, dimensions={0} | all-to-all | bytes 442368 | tf_op jit(solution)/shard_map/all_to_all | solution.py:234
  112.5 1.4 collective-permute-start
  113.8 1.4 collective-permute-done
  115.3 2.9 %collective-permute-start.1 = (f32[54,128]{1,0:T(8,128)S(1)}, f32[54,128]{1,0:T(8,128)S(1)}, u32[]{:S(2)}, u32[]{:S(2)}) collective-permute-start(f32[54,128]{1,0:T(8,128)S(1)} %add.15), channel_id=1, source_target_pairs={{0,2},{1,3},{2,0},{3,1},{4,6},{5,7},{6,4},{7,5},{8,10},{9,11},{10,... | collective-permute-start | bytes 82952 | tf_op jit(solution)/shard_map/ppermute | solution.py:267
  118.2 1.3 collective-permute-done.1
  119.5 1.2 collective-permute-start.2
  120.7 1.7 %collective-permute-done.2 = f32[54,128]{1,0:T(8,128)S(1)} collective-permute-done((f32[54,128]{1,0:T(8,128)S(1)}, f32[54,128]{1,0:T(8,128)S(1)}, u32[]{:S(2)}, u32[]{:S(2)}) %collective-permute-start.2) | collective-permute-done | bytes 27680 | tf_op jit(solution)/shard_map/ppermute | solution.py:267
  122.4 2.7 %collective-permute-start.3 = (f32[54,128]{1,0:T(8,128)S(1)}, f32[54,128]{1,0:T(8,128)S(1)}, u32[]{:S(2)}, u32[]{:S(2)}) collective-permute-start(f32[54,128]{1,0:T(8,128)S(1)} %add.17), channel_id=1, source_target_pairs={{0,8},{1,9},{2,10},{3,11},{4,12},{5,13},{6,14},{7,15},{8,0},{9,1},... | collective-permute-start | bytes 82952 | tf_op jit(solution)/shard_map/ppermute | solution.py:267
  125.1 1.5 collective-permute-done.3
  126.6 10.0 %all-to-all-start.5 = ((bf16[8,64,128]{2,1,0:T(8,128)(2,1)}), bf16[8,64,128]{2,1,0:T(8,128)(2,1)S(1)}, u32[]{:S(2)}, u32[]{:S(2)}) async-start(bf16[8,64,128]{2,1,0:T(8,128)(2,1)} %get-tuple-element.27), calls=%async_computation.5 | async-start | bytes 262144 | tf_op jit(solution)/shard_map/all_to_all | solution.py:234
  136.7 8.1 %all-to-all-done.5 = bf16[8,64,128]{2,1,0:T(8,128)(2,1)S(1)} async-done(((bf16[8,64,128]{2,1,0:T(8,128)(2,1)}), bf16[8,64,128]{2,1,0:T(8,128)(2,1)S(1)}, u32[]{:S(2)}, u32[]{:S(2)}) %all-to-all-start.5) | async-done | bytes 131104 | tf_op jit(solution)/shard_map/all_to_all | solution.py:234
  145.5 4.2 %all-to-all-start.7 = ((f32[8,54,128]{2,1,0:T(8,128)}), f32[8,54,128]{2,1,0:T(8,128)S(1)}, u32[]{:S(2)}, u32[]{:S(2)}) async-start(f32[8,54,128]{2,1,0:T(8,128)} %broadcast_in_dim.2), calls=%async_computation.7 | async-start | bytes 458752 | tf_op jit(solution)/shard_map/all_to_all | solution.py:234
  149.8 9.3 %all-to-all-done.7 = f32[8,54,128]{2,1,0:T(8,128)S(1)} async-done(((f32[8,54,128]{2,1,0:T(8,128)}), f32[8,54,128]{2,1,0:T(8,128)S(1)}, u32[]{:S(2)}, u32[]{:S(2)}) %all-to-all-start.7) | async-done | bytes 221216 | tf_op jit(solution)/shard_map/all_to_all | solution.py:234
  (21 shorter events, 4.2 us)
Async XLA Ops:
  94.4 3.4 %copy-start = (f32[144,128]{1,0:T(8,128)S(1)}, f32[144,128]{1,0:T(8,128)}, u32[]{:S(2)}) copy-start(f32[144,128]{1,0:T(8,128)} %get-tuple-element.30) | copy-start | bytes 221188
  94.4 3.4 %copy-start.1 = (f32[144,128]{1,0:T(8,128)S(1)}, f32[144,128]{1,0:T(8,128)}, u32[]{:S(2)}) copy-start(f32[144,128]{1,0:T(8,128)} %get-tuple-element.29) | copy-start | bytes 221188
  112.5 2.8 %collective-permute-start = (f32[54,128]{1,0:T(8,128)S(1)}, f32[54,128]{1,0:T(8,128)S(1)}, u32[]{:S(2)}, u32[]{:S(2)}) collective-permute-start(f32[54,128]{1,0:T(8,128)S(1)} %reduce_sum.9), channel_id=1, source_target_pairs={{0,1},{1,0},{2,3},{3,2},{4,5},{5,4},{6,7},{7,6},{8,9},{9,8},{10,11... | collective-permute-start | bytes 82952 | tf_op jit(solution)/shard_map/ppermute | solution.py:267
  115.3 4.2 %collective-permute-start.1 = (f32[54,128]{1,0:T(8,128)S(1)}, f32[54,128]{1,0:T(8,128)S(1)}, u32[]{:S(2)}, u32[]{:S(2)}) collective-permute-start(f32[54,128]{1,0:T(8,128)S(1)} %add.15), channel_id=1, source_target_pairs={{0,2},{1,3},{2,0},{3,1},{4,6},{5,7},{6,4},{7,5},{8,10},{9,11},{10,... | collective-permute-start | bytes 82952 | tf_op jit(solution)/shard_map/ppermute | solution.py:267
  119.5 2.9 %collective-permute-start.2 = (f32[54,128]{1,0:T(8,128)S(1)}, f32[54,128]{1,0:T(8,128)S(1)}, u32[]{:S(2)}, u32[]{:S(2)}) collective-permute-start(f32[54,128]{1,0:T(8,128)S(1)} %add.16), channel_id=1, source_target_pairs={{0,4},{1,5},{2,6},{3,7},{4,0},{5,1},{6,2},{7,3},{8,12},{9,13},{10,... | collective-permute-start | bytes 82952 | tf_op jit(solution)/shard_map/ppermute | solution.py:267
  122.4 4.2 %collective-permute-start.3 = (f32[54,128]{1,0:T(8,128)S(1)}, f32[54,128]{1,0:T(8,128)S(1)}, u32[]{:S(2)}, u32[]{:S(2)}) collective-permute-start(f32[54,128]{1,0:T(8,128)S(1)} %add.17), channel_id=1, source_target_pairs={{0,8},{1,9},{2,10},{3,11},{4,12},{5,13},{6,14},{7,15},{8,0},{9,1},... | collective-permute-start | bytes 82952 | tf_op jit(solution)/shard_map/ppermute | solution.py:267
  126.6 10.0 %collective-permute-start.4 = (f32[54,128]{1,0:T(8,128)S(1)}, f32[54,128]{1,0:T(8,128)S(1)}, u32[]{:S(2)}, u32[]{:S(2)}) collective-permute-start(f32[54,128]{1,0:T(8,128)S(1)} %add.18), channel_id=1, source_target_pairs={{0,16},{1,17},{2,18},{3,19},{4,20},{5,21},{6,22},{7,23},{8,24},{9,... | collective-permute-start | bytes 82952 | tf_op jit(solution)/shard_map/ppermute | solution.py:267
  126.6 18.2 %all-to-all-start.5 = ((bf16[8,64,128]{2,1,0:T(8,128)(2,1)}), bf16[8,64,128]{2,1,0:T(8,128)(2,1)S(1)}, u32[]{:S(2)}, u32[]{:S(2)}) async-start(bf16[8,64,128]{2,1,0:T(8,128)(2,1)} %get-tuple-element.27), calls=%async_computation.5 | async-start | bytes 262144 | tf_op jit(solution)/shard_map/all_to_all | solution.py:234
  145.5 13.6 %all-to-all-start.7 = ((f32[8,54,128]{2,1,0:T(8,128)}), f32[8,54,128]{2,1,0:T(8,128)S(1)}, u32[]{:S(2)}, u32[]{:S(2)}) async-start(f32[8,54,128]{2,1,0:T(8,128)} %broadcast_in_dim.2), calls=%async_computation.7 | async-start | bytes 458752 | tf_op jit(solution)/shard_map/all_to_all | solution.py:234

commit v2 on v1

--- a/solution.py
+++ b/solution.py
@@ -19,6 +19,9 @@
 F32 = jnp.float32
 BF16 = jnp.bfloat16
 ROWS = LINE + TAPS + 1
+VMEM_GRANT = 8 * 2**20
+CHIPS = NL // 2
+SHARE = 56
 
 
 def dot(a, b, ca, cb):
@@ -185,17 +188,54 @@
     write_sums(sum_ref, sums)
 
 
-def backward_kernel(k, starts, in_ref, x_ref, h_ref, gain_ref, taps_ref, mix_ref, order_ref, out_ref, sum_ref, *rest):
-    pad = rest[-1]
-    clear(pad)
+def rank_at(zone, core):
+    me = lax.axis_index("line")
+    chip = jnp.bitwise_and(lax.shift_right_logical(me, 1) + zone, CHIPS - 1)
+    return chip * 2 + jnp.bitwise_xor(jnp.bitwise_and(me, 1), core)
+
+
+def share_out(sum_refs, small_ref, keep_ref, send_ref):
+    for r in range(NL):
+        for k, ref in enumerate(sum_refs):
+            small_ref[r, 2 * k : 2 * k + 2, :] = ref[CH + 2 * r : CH + 2 * r + 2, :]
+        small_ref[r, 6:8, :] = jnp.zeros((2, CH), F32)
+    for core, out in ((0, keep_ref), (1, send_ref)):
+        for zone in range(CHIPS):
+            r = rank_at(zone, core)
+            for k, ref in enumerate(sum_refs):
+                out[zone, k * 16 : (k + 1) * 16, :] = ref[pl.ds(pl.multiple_of(r * 16, 16), 16), :]
+            out[zone, 48:SHARE, :] = small_ref[pl.ds(r, 1), :, :].reshape(8, CH)
+
+
+def finish_kernel(own_ref, other_ref, mix_ref, taps_ref, gain_ref, tail_ref):
+    for core, ref in ((0, own_ref), (1, other_ref)):
+        for zone in range(CHIPS):
+            r = rank_at(CHIPS - zone, core)
+            for k in range(3):
+                mix_ref[k, pl.ds(pl.multiple_of(r * 16, 16), 16), :] = ref[zone, k * 16 : (k + 1) * 16, :]
+            tail_ref[pl.ds(r, 1), :, :] = ref[zone, 48:SHARE, :].reshape(1, 8, CH)
+    for k in range(3):
+        for r in range(NL):
+            pair = tail_ref[r, 2 * k : 2 * k + 2, :]
+            if r < NL - 1:
+                taps_ref[k, 2 * r : 2 * r + 2, :] = pair
+            else:
+                taps_ref[k, 2 * r : 2 * r + 1, :] = pair[0:1]
+                gain_ref[k : k + 1, :] = pair[1:2]
+
+
+def backward_kernel(k, starts, in_ref, x_ref, h_ref, gain_ref, taps_ref, mix_ref, order_ref, *rest):
     if k == 1:
+        out_ref, sum_ref, imitated_ref, pad = rest
         me = lax.axis_index("line")
         for b in range(NL):
             slot = jnp.bitwise_and(b + 2 * me, NL - 1)
-            rest[0][:, b * Q : (b + 1) * Q, :] = in_ref[pl.ds(slot, 1), 0:Q, :]
+            imitated_ref[:, b * Q : (b + 1) * Q, :] = in_ref[pl.ds(slot, 1), 0:Q, :]
         received = in_ref[:, Q : 2 * Q, :].reshape(CELLS, CH)
     else:
+        sum1_ref, sum2_ref, out_ref, keep_ref, send_ref, pad, sum_ref, small_ref = rest
         received = in_ref[...].reshape(CELLS, CH)
+    clear(pad)
     order = order_ref[k : k + 1, :]
     row = slot_row(order, 1)
     sums = new_sums()
@@ -211,9 +251,11 @@
         grads.append(backward_line(k, grad, state, gain_ref, taps_ref, mix_ref, pad, sums))
     put(out_ref, 0, place(slot_row(order, -1 if k else 0), jnp.concatenate(grads, axis=0)))
     write_sums(sum_ref, sums)
-
-
-def call(kernel, outs, name, n_in):
+    if k == 0:
+        share_out((sum_ref, sum1_ref, sum2_ref), small_ref, keep_ref, send_ref)
+
+
+def call(kernel, outs, name, n_in, scratch=()):
     smem = pl.BlockSpec(memory_space=pltpu.SMEM)
     vmem = pl.BlockSpec(memory_space=pltpu.VMEM)
     return pl.pallas_call(
@@ -221,13 +263,25 @@
         out_shape=outs,
         in_specs=([smem] if n_in > 2 else [vmem]) + [vmem] * (n_in - 1),
         out_specs=[vmem] * len(outs),
-        scratch_shapes=[pltpu.VMEM((LINE + 16, CH), F32)] if n_in > 2 else [],
+        scratch_shapes=[pltpu.VMEM((LINE + 16, CH), F32)] * (n_in > 2)
+        + [pltpu.VMEM(dims, F32) for dims in scratch],
         name=name,
+        compiler_params=pltpu.CompilerParams(vmem_limit_bytes=VMEM_GRANT),
     )
 
 
 def shape(*dims, dtype=BF16):
     return jax.ShapeDtypeStruct(dims, dtype)
+
+
+def hop(axis, bit, values):
+    size = lax.axis_size(axis)
+    return lax.ppermute(values, axis, [(i, i ^ bit) for i in range(size)])
+
+
+def step(axis, distance, values):
+    size = lax.axis_size(axis)
+    return lax.ppermute(values, axis, [(i, (i + distance) % size) for i in range(size)])
 
 
 def exchange(blocks):
@@ -254,27 +308,32 @@
     moved, sums1, imitated = call(
         functools.partial(backward_kernel, 1), (blocks, sums, shape(1, CELLS, CH)), "bwd1", 8
     )(line_starts, exchange(moved), x1, h1, *weights)
-    moved, sums0 = call(functools.partial(backward_kernel, 0), (blocks, sums), "bwd0", 8)(
-        line_starts, exchange(moved), x0, h0, *weights
-    )
+    share = shape(CHIPS, SHARE, CH, dtype=F32)
+    moved, keep, send = call(
+        functools.partial(backward_kernel, 0),
+        (blocks, share, share),
+        "bwd0",
+        10,
+        scratch=((ROWS, CH), (NL, 8, CH)),
+    )(line_starts, exchange(moved), x0, h0, *weights, sums1, sums2)
     field_grad = exchange(moved).reshape(1, CELLS, CH)
     grad_scale = float(dp_size * NL * CELLS) ** (-0.5)
-    total = jnp.stack([sums0, sums1, sums2]).reshape(NL, 3 * ROWS // NL, CH)
-    part = jnp.sum(exchange(total), axis=0)
-    step = 1
-    while step < dp_size:
-        pairs = [(i, i ^ step) for i in range(dp_size)]
-        part = part + lax.ppermute(part, "dp", pairs)
-        step *= 2
-    whole = jnp.broadcast_to((part * grad_scale)[None], (NL, 3 * ROWS // NL, CH))
-    whole = exchange(whole).reshape(3, ROWS, CH)
-    return (
-        imitated,
-        field_grad,
-        whole[:, :CH],
-        whole[:, CH : CH + TAPS],
-        whole[:, CH + TAPS],
-    )
+    part = keep + hop("line", 1, send)
+    part = part[0] + sum(step("line", 2 * zone, part[zone]) for zone in range(1, CHIPS))
+    bit = 1
+    while bit < dp_size:
+        part = part + hop("dp", bit, part)
+        bit *= 2
+    part = part * grad_scale
+    own = jnp.stack([part] + [step("line", 2 * zone, part) for zone in range(1, CHIPS)])
+    mix_grad, kernel_grad, gain_grad = call(
+        finish_kernel,
+        (shape(3, CH, CH, dtype=F32), shape(3, TAPS, CH, dtype=F32), shape(3, CH, dtype=F32)),
+        "finish",
+        2,
+        scratch=((NL, 8, CH),),
+    )(own, hop("line", 1, own))
+    return imitated, field_grad, mix_grad, kernel_grad, gain_grad
 
 
 def solution(mesh):

time: 164 us -> 143 us (0.87); the launches traced: 162 us -> 143 us
  blocking collectives: 90.8 us -> 71.2 us
  starting transfers between devices: 22.5 us -> 31.6 us
  Pallas kernels: 20 us -> 13.9 us
    all_to_all x6 -> x5, blocking collectives: 90.8 us -> 71.2 us  [exchange(): lax.all_to_all(blocks, 'line', split_axis=0, concat_axis=0, tiled=True)]
    all_to_all x2 -> x1, waiting for transfers between devices: 17.5 us -> 7.86 us  [exchange(): lax.all_to_all(blocks, 'line', split_axis=0, concat_axis=0, tiled=True)]
    ppermute x5 -> x13, starting transfers between devices: 8.2 us -> 17.4 us  [the longest x7 9.34 us: hop(): return lax.ppermute(values, axis, [(i, i ^ bit) for i in range(size)])]
    ppermute x5 -> x13, waiting for transfers between devices: 5.95 us -> 14.8 us  [the longest x7 9.66 us: hop(): return lax.ppermute(values, axis, [(i, i ^ bit) for i in range(size)])]
    pallas_call x1, Pallas kernels: 1.69 us -> 0.02 us  [body(): call(prep_kernel, (shape(NL, 2 * Q, CH),), 'prep', 2)(fields, cotangent)]
    all_to_all x2 -> x1, starting transfers between devices: 14.3 us -> 14.2 us  [exchange(): lax.all_to_all(blocks, 'line', split_axis=0, concat_axis=0, tiled=True)]
    pallas_call x1 -> x2, Pallas kernels: 3.43 us -> 3.53 us  [the longest x1 2.82 us: body(): call(functools.partial(backward_kernel, 0), (blocks, share, share), 'bwd0...]
  transfers between devices with their start and end apart: 7 -> 14, of which waited for: 6 -> 9; matrix products, arithmetic and copies ran while one was open for 0% -> 0% of each run, Pallas kernels for 0% -> 0%
where the time goes in v2:
time: 143 us
  blocking collectives  71.2 us (50%)
  starting transfers between devices  31.6 us (22%)
  waiting for transfers between devices  22.7 us (16%)
  Pallas kernels  13.9 us (10%)
  local copies, waits for them, and re-layouts  2.5 us (2%)
    all_to_all x5, blocking collectives, exchange(): lax.all_to_all(blocks, 'line', split_axis=0, concat_axis=0, tiled=True)  71.2 us
    all_to_all x1, starting transfers between devices, exchange(): lax.all_to_all(blocks, 'line', split_axis=0, concat_axis=0, tiled=True)  14.2 us
    ppermute x7, waiting for transfers between devices, hop(): return lax.ppermute(values, axis, [(i, i ^ bit) for i in range(size)])  9.66 us
    ppermute x7, starting transfers between devices, hop(): return lax.ppermute(values, axis, [(i, i ^ bit) for i in range(size)])  9.34 us
    ppermute x6, starting transfers between devices, step(): lax.ppermute(values, axis, [(i, (i + distance) % size) for i in range(siz...  8.08 us
    all_to_all x1, waiting for transfers between devices, exchange(): lax.all_to_all(blocks, 'line', split_axis=0, concat_axis=0, tiled=True)  7.86 us
    ppermute x6, waiting for transfers between devices, step(): lax.ppermute(values, axis, [(i, (i + distance) % size) for i in range(siz...  5.14 us
    pallas_call x1, Pallas kernels, body(): call(turn_kernel, (shape(NL, 2 * Q, CH), sums), 'turn', 7)  3.39 us
  transfers between devices with their start and end apart: 14, of which 9 were waited for; matrix products, arithmetic and copies ran while one was open for 0% of the time, Pallas kernels for 0%

profile of v2, /device:TPU:1, one launch (start us, length us, event | category | flops | bytes accessed | tf_op | source)
XLA Modules:
  0.0 142.6 jit_solution(14614607593661483963)
XLA Ops:
  2.5 19.2 %all_to_all.30.in_ref.cot_ref = bf16[8,128,128]{2,1,0:T(8,128)(2,1)S(1)} all-to-all(bf16[8,128,128]{2,1,0:T(8,128)(2,1)S(1)} %prep.1), channel_id=1, replica_groups=mesh['line'=8,'dp'=32] {'line'}, dimensions={0} | all-to-all | bytes 524288 | tf_op jit(solution)/shard_map/all_to_all | solution.py:288
  21.8 2.4 %fwd0.1 = (bf16[8,64,128]{2,1,0:T(8,128)(2,1)S(1)}, bf16[4,128,128]{2,1,0:T(8,128)(2,1)S(1)}, f32[4,128,128]{2,1,0:T(8,128)S(1)}) custom-call(s32[3,4]{1,0:T(4,128)S(1)} %copy-done.5, bf16[8,128,128]{2,1,0:T(8,128)(2,1)S(1)} %all_to_all.30.in_ref.cot_ref, f32[3,128]{1,0:T(4,128)S(1)} %copy-done.6, f32[3,15,128]{2,1,0:T(8,128)S(1)} %copy-done.1, ...), custom_call_target="tpu_custom_call" | custom-call | tf_op jit(solution)/shard_map/fwd0/pallas_call | solution.py:299
  24.1 13.5 %all_to_all.31.in_ref = bf16[8,64,128]{2,1,0:T(8,128)(2,1)S(1)} all-to-all(bf16[8,64,128]{2,1,0:T(8,128)(2,1)S(1)} %get-tuple-element.22), channel_id=1, replica_groups=mesh['line'=8,'dp'=32] {'line'}, dimensions={0} | all-to-all | bytes 262144 | tf_op jit(solution)/shard_map/all_to_all | solution.py:288
  37.6 2.4 %fwd1.1 = (bf16[8,64,128]{2,1,0:T(8,128)(2,1)S(1)}, bf16[4,128,128]{2,1,0:T(8,128)(2,1)S(1)}, f32[4,128,128]{2,1,0:T(8,128)S(1)}) custom-call(s32[3,4]{1,0:T(4,128)S(1)} %copy-done.5, bf16[8,64,128]{2,1,0:T(8,128)(2,1)S(1)} %all_to_all.31.in_ref, f32[3,128]{1,0:T(4,128)S(1)} %copy-done.6, f32[3,15,128]{2,1,0:T(8,128)S(1)} %copy-done.1, ...), custom_call_target="tpu_custom_call" | custom-call | tf_op jit(solution)/shard_map/fwd1/pallas_call | solution.py:302
  40.0 11.5 %all_to_all.32.in_ref = bf16[8,64,128]{2,1,0:T(8,128)(2,1)S(1)} all-to-all(bf16[8,64,128]{2,1,0:T(8,128)(2,1)S(1)} %get-tuple-element.23), channel_id=1, replica_groups=mesh['line'=8,'dp'=32] {'line'}, dimensions={0} | all-to-all | bytes 262144 | tf_op jit(solution)/shard_map/all_to_all | solution.py:288
  51.5 3.4 %turn.1 = (bf16[8,128,128]{2,1,0:T(8,128)(2,1)S(1)}, f32[144,128]{1,0:T(8,128)S(1)}) custom-call(s32[3,4]{1,0:T(4,128)S(1)} %copy-done.5, bf16[8,64,128]{2,1,0:T(8,128)(2,1)S(1)} %all_to_all.32.in_ref, bf16[8,128,128]{2,1,0:T(8,128)(2,1)S(1)} %all_to_all.30.in_ref.cot_ref, f32[3,128]{1,0:T(4,128)S(1)} %copy-done.6, f32[3,15,128]{2,1,0:T(8,128)S(1)} %copy-done.1, ...), custom_call_target="tpu_custom_call" | custom-call | tf_op jit(solution)/shard_map/turn/pallas_call | solution.py:305
  54.9 13.5 %all_to_all.33.in_ref = bf16[8,128,128]{2,1,0:T(8,128)(2,1)S(1)} all-to-all(bf16[8,128,128]{2,1,0:T(8,128)(2,1)S(1)} %get-tuple-element.24), channel_id=1, replica_groups=mesh['line'=8,'dp'=32] {'line'}, dimensions={0} | all-to-all | bytes 524288 | tf_op jit(solution)/shard_map/all_to_all | solution.py:288
  68.4 2.2 %bwd1.1 = (bf16[8,64,128]{2,1,0:T(8,128)(2,1)S(1)}, f32[144,128]{1,0:T(8,128)S(1)}, bf16[1,512,128]{2,1,0:T(8,128)(2,1)}) custom-call(s32[3,4]{1,0:T(4,128)S(1)} %copy-done.5, bf16[8,128,128]{2,1,0:T(8,128)(2,1)S(1)} %all_to_all.33.in_ref, bf16[4,128,128]{2,1,0:T(8,128)(2,1)S(1)} %get-tuple-element.25.x_ref, f32[4,128,128]{2,1,0:T(8,128)S(1)} %get-tuple-element.26.h_ref, ...), custom_call_target="tpu_custom_call" | custom-call | tf_op jit(solution)/shard_map/bwd1/pallas_call | solution.py:308
  70.6 13.4 %all_to_all.34.in_ref = bf16[8,64,128]{2,1,0:T(8,128)(2,1)S(1)} all-to-all(bf16[8,64,128]{2,1,0:T(8,128)(2,1)S(1)} %get-tuple-element.28), channel_id=1, replica_groups=mesh['line'=8,'dp'=32] {'line'}, dimensions={0} | all-to-all | bytes 262144 | tf_op jit(solution)/shard_map/all_to_all | solution.py:288
  84.0 2.8 %bwd0.1 = (bf16[8,64,128]{2,1,0:T(8,128)(2,1)}, f32[4,56,128]{2,1,0:T(8,128)S(1)}, f32[4,56,128]{2,1,0:T(8,128)S(1)}) custom-call(s32[3,4]{1,0:T(4,128)S(1)} %copy-done.5, bf16[8,64,128]{2,1,0:T(8,128)(2,1)S(1)} %all_to_all.34.in_ref, bf16[4,128,128]{2,1,0:T(8,128)(2,1)S(1)} %get-tuple-element.29.x_ref, f32[4,128,128]{2,1,0:T(8,128)S(1)} %get-tuple-element.30.h_ref, ...), custom_call_target="tpu_custom_call" | custom-call | tf_op jit(solution)/shard_map/bwd0/pallas_call | solution.py:312
  90.1 3.3 %collective-permute-start.3 = (f32[56,128]{1,0:T(8,128)S(1)}, f32[56,128]{1,0:T(8,128)S(1)}, u32[]{:S(2)}, u32[]{:S(2)}) collective-permute-start(f32[56,128]{1,0:T(8,128)S(1)} %get-tuple-element.40), channel_id=1, source_target_pairs={{0,192},{32,224},{64,0},{96,32},{128,64},{160,96},{192,128},{224,1... | collective-permute-start | bytes 86024 | tf_op jit(solution)/shard_map/ppermute | solution.py:284
  93.3 2.3 %collective-permute-done.2 = f32[56,128]{1,0:T(8,128)S(1)} collective-permute-done((f32[56,128]{1,0:T(8,128)S(1)}, f32[56,128]{1,0:T(8,128)S(1)}, u32[]{:S(2)}, u32[]{:S(2)}) %collective-permute-start.2) | collective-permute-done | bytes 28704 | tf_op jit(solution)/shard_map/ppermute | solution.py:284
  95.6 2.8 %collective-permute-done.1 = f32[56,128]{1,0:T(8,128)S(1)} collective-permute-done((f32[56,128]{1,0:T(8,128)S(1)}, f32[56,128]{1,0:T(8,128)S(1)}, u32[]{:S(2)}, u32[]{:S(2)}) %collective-permute-start.1) | collective-permute-done | bytes 28704 | tf_op jit(solution)/shard_map/ppermute | solution.py:284
  98.5 1.4 collective-permute-start.4
  99.9 1.4 collective-permute-done.4
  101.3 2.9 %collective-permute-start.5 = (f32[56,128]{1,0:T(8,128)S(1)}, f32[56,128]{1,0:T(8,128)S(1)}, u32[]{:S(2)}, u32[]{:S(2)}) collective-permute-start(f32[56,128]{1,0:T(8,128)S(1)} %add.31), channel_id=1, source_target_pairs={{0,2},{1,3},{2,0},{3,1},{4,6},{5,7},{6,4},{7,5},{8,10},{9,11},{10,... | collective-permute-start | bytes 86024 | tf_op jit(solution)/shard_map/ppermute | solution.py:279
  106.7 1.8 %collective-permute-done.6 = f32[56,128]{1,0:T(8,128)S(1)} collective-permute-done((f32[56,128]{1,0:T(8,128)S(1)}, f32[56,128]{1,0:T(8,128)S(1)}, u32[]{:S(2)}, u32[]{:S(2)}) %collective-permute-start.6) | collective-permute-done | bytes 28704 | tf_op jit(solution)/shard_map/ppermute | solution.py:279
  108.5 2.8 %collective-permute-start.7 = (f32[56,128]{1,0:T(8,128)S(1)}, f32[56,128]{1,0:T(8,128)S(1)}, u32[]{:S(2)}, u32[]{:S(2)}) collective-permute-start(f32[56,128]{1,0:T(8,128)S(1)} %add.33), channel_id=1, source_target_pairs={{0,8},{1,9},{2,10},{3,11},{4,12},{5,13},{6,14},{7,15},{8,0},{9,1},... | collective-permute-start | bytes 86024 | tf_op jit(solution)/shard_map/ppermute | solution.py:279
  111.3 1.5 %collective-permute-done.7 = f32[56,128]{1,0:T(8,128)S(1)} collective-permute-done((f32[56,128]{1,0:T(8,128)S(1)}, f32[56,128]{1,0:T(8,128)S(1)}, u32[]{:S(2)}, u32[]{:S(2)}) %collective-permute-start.7) | collective-permute-done | bytes 28704 | tf_op jit(solution)/shard_map/ppermute | solution.py:279
  112.8 2.7 %collective-permute-done.8 = f32[56,128]{1,0:T(8,128)S(1)} collective-permute-done((f32[56,128]{1,0:T(8,128)S(1)}, f32[56,128]{1,0:T(8,128)S(1)}, u32[]{:S(2)}, u32[]{:S(2)}) %collective-permute-start.8) | collective-permute-done | bytes 28704 | tf_op jit(solution)/shard_map/ppermute | solution.py:279
  115.5 2.1 %collective-permute-start.10 = (f32[56,128]{1,0:T(8,128)S(1)}, f32[56,128]{1,0:T(8,128)S(1)}, u32[]{:S(2)}, u32[]{:S(2)}) collective-permute-start(f32[56,128]{1,0:T(8,128)S(1)} %add_multiply_fusion), channel_id=1, source_target_pairs={{0,128},{32,160},{64,192},{96,224},{128,0},{160,32},{192,64},{224,... | collective-permute-start | bytes 86024 | tf_op jit(solution)/shard_map/ppermute | solution.py:284
  117.6 1.5 %collective-permute-start.9 = (f32[56,128]{1,0:T(8,128)S(1)}, f32[56,128]{1,0:T(8,128)S(1)}, u32[]{:S(2)}, u32[]{:S(2)}) collective-permute-start(f32[56,128]{1,0:T(8,128)S(1)} %add_multiply_fusion), channel_id=1, source_target_pairs={{0,64},{32,96},{64,128},{96,160},{128,192},{160,224},{192,0},{224,... | collective-permute-start | bytes 86024 | tf_op jit(solution)/shard_map/ppermute | solution.py:284
  119.1 14.2 %all-to-all-start.5 = ((bf16[8,64,128]{2,1,0:T(8,128)(2,1)}), bf16[8,64,128]{2,1,0:T(8,128)(2,1)S(1)}, u32[]{:S(2)}, u32[]{:S(2)}) async-start(bf16[8,64,128]{2,1,0:T(8,128)(2,1)} %get-tuple-element.33), calls=%async_computation.5 | async-start | bytes 262144 | tf_op jit(solution)/shard_map/all_to_all | solution.py:288
  133.4 7.9 %all-to-all-done.5 = bf16[8,64,128]{2,1,0:T(8,128)(2,1)S(1)} async-done(((bf16[8,64,128]{2,1,0:T(8,128)(2,1)}), bf16[8,64,128]{2,1,0:T(8,128)(2,1)S(1)}, u32[]{:S(2)}, u32[]{:S(2)}) %all-to-all-start.5) | async-done | bytes 131104 | tf_op jit(solution)/shard_map/all_to_all | solution.py:288
  (40 shorter events, 9.1 us)
Async XLA Ops:
  0.6 0.9 copy-start.3
  1.5 0.9 copy-start.4
  2.5 19.3 %copy-start = (bf16[3,128,128]{2,1,0:T(8,128)(2,1)S(1)}, bf16[3,128,128]{2,1,0:T(8,128)(2,1)}, u32[]{:S(2)}) copy-start(bf16[3,128,128]{2,1,0:T(8,128)(2,1)} %mix_ref.9) | copy-start | bytes 294916
  2.5 19.3 %copy-start.1 = (f32[3,15,128]{2,1,0:T(8,128)S(1)}, f32[3,15,128]{2,1,0:T(8,128)}, u32[]{:S(2)}) copy-start(f32[3,15,128]{2,1,0:T(8,128)} %taps_ref.9) | copy-start | bytes 69124
  2.5 19.3 %copy-start.2 = (s32[3,512]{1,0:T(4,128)S(1)}, s32[3,512]{1,0:T(4,128)}, u32[]{:S(2)}) copy-start(s32[3,512]{1,0:T(4,128)} %order_ref.9) | copy-start | bytes 18436
  2.5 19.2 %copy-start.5 = (s32[3,4]{1,0:T(4,128)S(1)}, s32[3,4]{1,0:T(4,128)}, u32[]{:S(2)}) copy-start(s32[3,4]{1,0:T(4,128)} %starts.9) | copy-start | bytes 148
  2.5 19.2 %copy-start.6 = (f32[3,128]{1,0:T(4,128)S(1)}, f32[3,128]{1,0:T(4,128)}, u32[]{:S(2)}) copy-start(f32[3,128]{1,0:T(4,128)} %gain_ref.9) | copy-start | bytes 4612
  86.9 1.9 %collective-permute-start = (f32[4,56,128]{2,1,0:T(8,128)S(1)}, f32[4,56,128]{2,1,0:T(8,128)S(1)}, u32[]{:S(2)}, u32[]{:S(2)}) collective-permute-start(f32[4,56,128]{2,1,0:T(8,128)S(1)} %get-tuple-element.35), channel_id=1, source_target_pairs={{0,32},{32,0},{64,96},{96,64},{128,160},{160,128},{192,224},{224,1... | collective-permute-start | bytes 344072 | tf_op jit(solution)/shard_map/ppermute | solution.py:279
  88.8 6.8 %collective-permute-start.2 = (f32[56,128]{1,0:T(8,128)S(1)}, f32[56,128]{1,0:T(8,128)S(1)}, u32[]{:S(2)}, u32[]{:S(2)}) collective-permute-start(f32[56,128]{1,0:T(8,128)S(1)} %get-tuple-element.39), channel_id=1, source_target_pairs={{0,128},{32,160},{64,192},{96,224},{128,0},{160,32},{192,64},{224,... | collective-permute-start | bytes 86024 | tf_op jit(solution)/shard_map/ppermute | solution.py:284
  90.1 5.6 %collective-permute-start.3 = (f32[56,128]{1,0:T(8,128)S(1)}, f32[56,128]{1,0:T(8,128)S(1)}, u32[]{:S(2)}, u32[]{:S(2)}) collective-permute-start(f32[56,128]{1,0:T(8,128)S(1)} %get-tuple-element.40), channel_id=1, source_target_pairs={{0,192},{32,224},{64,0},{96,32},{128,64},{160,96},{192,128},{224,1... | collective-permute-start | bytes 86024 | tf_op jit(solution)/shard_map/ppermute | solution.py:284
  93.3 5.1 %collective-permute-start.1 = (f32[56,128]{1,0:T(8,128)S(1)}, f32[56,128]{1,0:T(8,128)S(1)}, u32[]{:S(2)}, u32[]{:S(2)}) collective-permute-start(f32[56,128]{1,0:T(8,128)S(1)} %get-tuple-element.41), channel_id=1, source_target_pairs={{0,64},{32,96},{64,128},{96,160},{128,192},{160,224},{192,0},{224,... | collective-permute-start | bytes 86024 | tf_op jit(solution)/shard_map/ppermute | solution.py:284
  98.5 2.8 %collective-permute-start.4 = (f32[56,128]{1,0:T(8,128)S(1)}, f32[56,128]{1,0:T(8,128)S(1)}, u32[]{:S(2)}, u32[]{:S(2)}) collective-permute-start(f32[56,128]{1,0:T(8,128)S(1)} %fusion), channel_id=1, source_target_pairs={{0,1},{1,0},{2,3},{3,2},{4,5},{5,4},{6,7},{7,6},{8,9},{9,8},{10,11... | collective-permute-start | bytes 86024 | tf_op jit(solution)/shard_map/ppermute | solution.py:279
  101.3 4.2 %collective-permute-start.5 = (f32[56,128]{1,0:T(8,128)S(1)}, f32[56,128]{1,0:T(8,128)S(1)}, u32[]{:S(2)}, u32[]{:S(2)}) collective-permute-start(f32[56,128]{1,0:T(8,128)S(1)} %add.31), channel_id=1, source_target_pairs={{0,2},{1,3},{2,0},{3,1},{4,6},{5,7},{6,4},{7,5},{8,10},{9,11},{10,... | collective-permute-start | bytes 86024 | tf_op jit(solution)/shard_map/ppermute | solution.py:279
  105.5 3.0 %collective-permute-start.6 = (f32[56,128]{1,0:T(8,128)S(1)}, f32[56,128]{1,0:T(8,128)S(1)}, u32[]{:S(2)}, u32[]{:S(2)}) collective-permute-start(f32[56,128]{1,0:T(8,128)S(1)} %add.32), channel_id=1, source_target_pairs={{0,4},{1,5},{2,6},{3,7},{4,0},{5,1},{6,2},{7,3},{8,12},{9,13},{10,... | collective-permute-start | bytes 86024 | tf_op jit(solution)/shard_map/ppermute | solution.py:279
  108.5 4.2 %collective-permute-start.7 = (f32[56,128]{1,0:T(8,128)S(1)}, f32[56,128]{1,0:T(8,128)S(1)}, u32[]{:S(2)}, u32[]{:S(2)}) collective-permute-start(f32[56,128]{1,0:T(8,128)S(1)} %add.33), channel_id=1, source_target_pairs={{0,8},{1,9},{2,10},{3,11},{4,12},{5,13},{6,14},{7,15},{8,0},{9,1},... | collective-permute-start | bytes 86024 | tf_op jit(solution)/shard_map/ppermute | solution.py:279
  112.8 2.7 %collective-permute-start.8 = (f32[56,128]{1,0:T(8,128)S(1)}, f32[56,128]{1,0:T(8,128)S(1)}, u32[]{:S(2)}, u32[]{:S(2)}) collective-permute-start(f32[56,128]{1,0:T(8,128)S(1)} %add.34), channel_id=1, source_target_pairs={{0,16},{1,17},{2,18},{3,19},{4,20},{5,21},{6,22},{7,23},{8,24},{9,... | collective-permute-start | bytes 86024 | tf_op jit(solution)/shard_map/ppermute | solution.py:279
  115.5 17.7 %collective-permute-start.11 = (f32[56,128]{1,0:T(8,128)S(1)}, f32[56,128]{1,0:T(8,128)S(1)}, u32[]{:S(2)}, u32[]{:S(2)}) collective-permute-start(f32[56,128]{1,0:T(8,128)S(1)} %add_multiply_fusion), channel_id=1, source_target_pairs={{0,192},{32,224},{64,0},{96,32},{128,64},{160,96},{192,128},{224,1... | collective-permute-start | bytes 86024 | tf_op jit(solution)/shard_map/ppermute | solution.py:284
  115.5 17.7 %collective-permute-start.10 = (f32[56,128]{1,0:T(8,128)S(1)}, f32[56,128]{1,0:T(8,128)S(1)}, u32[]{:S(2)}, u32[]{:S(2)}) collective-permute-start(f32[56,128]{1,0:T(8,128)S(1)} %add_multiply_fusion), channel_id=1, source_target_pairs={{0,128},{32,160},{64,192},{96,224},{128,0},{160,32},{192,64},{224,... | collective-permute-start | bytes 86024 | tf_op jit(solution)/shard_map/ppermute | solution.py:284
  117.6 15.7 %collective-permute-start.9 = (f32[56,128]{1,0:T(8,128)S(1)}, f32[56,128]{1,0:T(8,128)S(1)}, u32[]{:S(2)}, u32[]{:S(2)}) collective-permute-start(f32[56,128]{1,0:T(8,128)S(1)} %add_multiply_fusion), channel_id=1, source_target_pairs={{0,64},{32,96},{64,128},{96,160},{128,192},{160,224},{192,0},{224,... | collective-permute-start | bytes 86024 | tf_op jit(solution)/shard_map/ppermute | solution.py:284
  119.1 22.2 %all-to-all-start.5 = ((bf16[8,64,128]{2,1,0:T(8,128)(2,1)}), bf16[8,64,128]{2,1,0:T(8,128)(2,1)S(1)}, u32[]{:S(2)}, u32[]{:S(2)}) async-start(bf16[8,64,128]{2,1,0:T(8,128)(2,1)} %get-tuple-element.33), calls=%async_computation.5 | async-start | bytes 262144 | tf_op jit(solution)/shard_map/all_to_all | solution.py:288
  133.3 8.0 %collective-permute-start.12 = (f32[4,56,128]{2,1,0:T(8,128)S(1)}, f32[4,56,128]{2,1,0:T(8,128)S(1)}, u32[]{:S(2)}, u32[]{:S(2)}) collective-permute-start(f32[4,56,128]{2,1,0:T(8,128)S(1)} %pad_maximum_fusion.own_ref), channel_id=1, source_target_pairs={{0,32},{32,0},{64,96},{96,64},{128,160},{160,128},{192,224},{224,1... | collective-permute-start | bytes 344072 | tf_op jit(solution)/shard_map/ppermute | solution.py:279

commit v3 on v1

v3 whole, which is shorter than its diff:
```python
import functools

import jax
import jax.numpy as jnp
from jax import lax
from jax.experimental import pallas as pl
from jax.experimental.pallas import tpu as pltpu
from jax.sharding import PartitionSpec as P

LINE = 128
CH = 128
TAPS = 15
CELLS = 512
NL = 8
CHIPS = NL // 2
Q = CELLS // NL
HALF = CELLS // 2
LINES = CELLS // LINE
EPSILON = 1e-06
OFFSETS = [0] + [s * 2**level for level in range(7) for s in (-1, 1)]
F32 = jnp.float32
BF16 = jnp.bfloat16
I32 = jnp.int32
ROWS = LINE + TAPS + 1
EXTRA = 48
SHARE = 56
VMEM_GRANT = 12 * 2**20


def dot(a, b, ca, cb):
    return lax.dot_general(a, b, (((ca,), (cb,)), ((), ())), preferred_element_type=F32)


def place_of():
    me = lax.axis_index("line")
    return lax.shift_right_logical(me, 1), jnp.bitwise_and(me, 1)


def wrap(index):
    return jnp.bitwise_and(index, CHIPS - 1)


def block_row(order, gathered):
    home = lax.shift_right_logical(order, 6)
    within = jnp.bitwise_and(order, Q - 1)
    odd = jnp.bitwise_and(home, 1)
    chip = lax.shift_right_logical(home, 1)
    if gathered:
        zone, core = place_of()
        odd = jnp.bitwise_xor(odd, core)
        chip = wrap(zone - chip + CHIPS)
    return odd * HALF + chip * Q + within


def picks(row, line):
    part = row[:, line * LINE : (line + 1) * LINE]
    wanted = jnp.transpose(jnp.broadcast_to(part, (LINE, LINE)))
    lanes = lax.broadcasted_iota(I32, (LINE, LINE), 1)
    return jnp.concatenate(
        [jnp.where(wanted == lanes + c * LINE, 1.0, 0.0).astype(BF16) for c in range(LINES)],
        axis=1,
    )


def place(row, values, rows):
    hot = jnp.where(jnp.broadcast_to(row, (LINE, CELLS)) == rows, 1.0, 0.0).astype(BF16)
    return dot(hot, values, 1, 0).astype(BF16)


def put_next(row, values, m, sign, same_ref, swap_ref):
    _, core = place_of()
    for c in range(LINES):
        rows = lax.broadcasted_iota(I32, (LINE, CELLS), 0) + c * LINE
        placed = place(row, values, rows)
        for half in range(2):
            h = (c * 2 + half) % CHIPS
            block = placed[half * Q : (half + 1) * Q]
            if c < LINES // 2:
                same_ref[wrap(m + sign * h + CHIPS), h] = block
            else:
                at = m + h + core if sign > 0 else m - h - 1 + core + CHIPS
                swap_ref[wrap(at), h] = block


def put_home(row, values, m, own_ref, swap_ref):
    zone, core = place_of()
    step = lax.broadcasted_iota(I32, (LINE, CELLS), 0)
    mine = (core * CHIPS + zone) * Q
    other = ((1 - core) * CHIPS + zone) * Q - Q
    placed = place(row, values, step + jnp.where(step < Q, mine, other))
    own_ref[m] = placed[:Q]
    swap_ref[m] = placed[Q:]


def shifts(pad, values):
    pad[8 : 8 + LINE, :] = values
    for offset in OFFSETS:
        if offset == 0:
            yield values
        elif abs(offset) < 8:
            yield pad[8 + offset : 8 + offset + LINE, :]
        elif offset > 0:
            yield jnp.concatenate([values[offset:], jnp.zeros((offset, CH), F32)], axis=0)
        else:
            yield jnp.concatenate([jnp.zeros((-offset, CH), F32), values[:offset]], axis=0)


def clear(pad):
    pad[0:8, :] = jnp.zeros((8, CH), F32)
    pad[8 + LINE : 16 + LINE, :] = jnp.zeros((8, CH), F32)


def norm(x, gain, start):
    inverse = lax.rsqrt(jnp.mean(x * x, axis=-1, keepdims=True) + EPSILON)
    scaled = x * inverse
    normed = (scaled * gain).astype(BF16).astype(F32)
    keep = lax.broadcasted_iota(I32, (LINE, CH), 0).astype(F32) >= start
    return inverse, scaled, jnp.where(keep, normed, 0.0), keep


def conv(pad, masked, taps):
    total = None
    for t, moved in enumerate(shifts(pad, masked)):
        term = taps[t : t + 1, :] * moved
        total = term if total is None else total + term
    return total


def sigmoid(h):
    return 1.0 / (1.0 + jnp.exp(-h))


def forward_line(k, x, start, gain_ref, taps_ref, mix_ref, pad):
    inverse, scaled, masked, keep = norm(x, gain_ref[k : k + 1, :], start)
    hidden = conv(pad, masked, taps_ref[k])
    gate = sigmoid(hidden)
    active = (hidden * gate).astype(BF16)
    mixed = dot(active, mix_ref[k], 1, 0).astype(BF16).astype(F32)
    after = (x + mixed).astype(BF16)
    return (inverse, scaled, masked, keep, hidden, gate, active), after


def backward_line(k, grad, state, gain_ref, taps_ref, mix_ref, pad, sums):
    inverse, scaled, masked, keep, hidden, gate, active = state
    gain = gain_ref[k : k + 1, :]
    taps = taps_ref[k]
    sums["active"].append(active)
    sums["grad"].append(grad)
    grad_act = dot(grad, mix_ref[k], 1, 1)
    grad_hidden = (grad_act * (gate * (1.0 + hidden * (1.0 - gate)))).astype(BF16).astype(F32)
    total = None
    for t, moved in enumerate(shifts(pad, grad_hidden)):
        u = t if t == 0 else (t + 1 if t % 2 else t - 1)
        term = taps[u : u + 1, :] * moved
        total = term if total is None else total + term
        part = jnp.sum((moved * masked).reshape(LINE // 8, 8, CH), axis=0)
        sums["rows"][u] = part if sums["rows"][u] is None else sums["rows"][u] + part
    cells = jnp.where(keep, total, 0.0).astype(BF16).astype(F32)
    part = jnp.sum((cells * scaled).reshape(LINE // 8, 8, CH), axis=0)
    sums["rows"][TAPS] = part if sums["rows"][TAPS] is None else sums["rows"][TAPS] + part
    weighted = cells * gain
    moved = inverse * (weighted - scaled * jnp.mean(weighted * scaled, axis=-1, keepdims=True))
    return (grad.astype(F32) + moved).astype(BF16)


def new_sums():
    return {"active": [], "grad": [], "rows": [None] * (TAPS + 1)}


def add_sums(sum_ref, rows_ref, sums):
    active = jnp.concatenate(sums["active"], axis=0)
    sum_ref[0:CH, :] += dot(active, jnp.concatenate(sums["grad"], axis=0), 0, 0)
    for t, part in enumerate(sums["rows"]):
        rows_ref[t] += part


def start_sums(sum_ref, rows_ref):
    sum_ref[...] = jnp.zeros_like(sum_ref)
    rows_ref[...] = jnp.zeros_like(rows_ref)


def end_sums(sum_ref, rows_ref):
    sum_ref[CH:ROWS, :] = jnp.sum(rows_ref[...], axis=1)


def prep_kernel(starts, fields_ref, cot_ref, order_ref, keep_ref, keep_cot_ref, send_ref, extra_ref):
    _, core = place_of()
    for m in range(CHIPS):
        here = pl.ds(pl.multiple_of((2 * m + core) * Q, Q), Q)
        there = pl.ds(pl.multiple_of((2 * m + 1 - core) * Q, Q), Q)
        keep_ref[m] = fields_ref[0, here, :]
        keep_cot_ref[m] = cot_ref[0, here, :]
        send_ref[m] = fields_ref[0, there, :]
        send_ref[CHIPS + m] = cot_ref[0, there, :]
    rows = []
    for k in range(3):
        order = order_ref[k : k + 1, :]
        for part in (lax.shift_right_logical(order, 1), jnp.bitwise_and(order, 1)):
            rows += [part[:, c * LINE : (c + 1) * LINE].astype(F32) for c in range(LINES)]
    for k in range(3):
        rows += [jnp.full((1, CH), starts[k, line], I32).astype(F32) for line in range(LINES)]
    rows.append(jnp.zeros((EXTRA - len(rows), CH), F32))
    extra_ref[...] = jnp.concatenate(rows, axis=0).astype(BF16)


def read_tables(pieces, order_ref, starts_ref):
    zone, _ = place_of()
    for back, ref in enumerate(pieces):
        m = wrap(zone - back + CHIPS)
        extra = ref[CELLS : CELLS + EXTRA, :].astype(F32)
        for k in range(3):
            for c in range(LINES):
                high = extra[8 * k + c : 8 * k + c + 1]
                low = extra[8 * k + 4 + c : 8 * k + 5 + c]
                order_ref[k, m, :, c * LINE : (c + 1) * LINE] = (2.0 * high + low).astype(I32)
            starts_ref[k, m] = extra[24 + 4 * k : 28 + 4 * k]


def gathered_rows(pieces, m, k):
    zone, core = place_of()
    rows = []
    for odd in range(2):
        for back, ref in enumerate(pieces):
            home = 2 * (zone - back) + jnp.bitwise_xor(core, odd)
            block = wrap(m - (k // 2) * home + NL)
            rows.append(ref[pl.ds(pl.multiple_of(odd * HALF + block * Q, Q), Q), :])
    return jnp.concatenate(rows, axis=0)


def moved_rows(same_ref, swap_ref, m):
    return jnp.concatenate([same_ref[m].reshape(HALF, CH), swap_ref[m].reshape(HALF, CH)], axis=0)


def forward_kernel(k, *refs):
    if k == 0:
        pieces, refs = refs[:CHIPS], refs[CHIPS:]
        gain_ref, taps_ref, mix_ref, order_ref, starts_ref, same_ref, swap_ref, x_ref, h_ref, pad = refs
        read_tables(pieces, order_ref, starts_ref)
    else:
        (in_ref, in_swap_ref, gain_ref, taps_ref, mix_ref, order_ref, starts_ref) = refs[:7]
        same_ref, swap_ref, x_ref, h_ref, pad = refs[7:]
    clear(pad)

    def holder(m, carry):
        received = gathered_rows(pieces, m, k) if k == 0 else moved_rows(in_ref, in_swap_ref, m)
        order = order_ref[k, m]
        row = block_row(order, k == 0)
        after = []
        for line in range(LINES):
            x = dot(picks(row, line), received, 1, 0)
            state, new = forward_line(
                k, x, starts_ref[k, m, line : line + 1, :], gain_ref, taps_ref, mix_ref, pad
            )
            x_ref[m, line] = x.astype(BF16)
            h_ref[m, line] = state[4]
            after.append(new)
        put_next(block_row(order, False), jnp.concatenate(after, axis=0), m, 1, same_ref, swap_ref)
        return carry

    lax.fori_loop(0, CHIPS, holder, 0)


def turn_kernel(*refs):
    k = 2
    in_ref, in_swap_ref = refs[:2]
    pieces = refs[2 : 2 + CHIPS]
    gain_ref, taps_ref, mix_ref, order_ref, starts_ref = refs[2 + CHIPS : 7 + CHIPS]
    same_ref, swap_ref, own_ref, home_ref, sum_ref, pad, rows_ref = refs[7 + CHIPS :]
    clear(pad)
    start_sums(sum_ref, rows_ref)

    def holder(m, carry):
        received = moved_rows(in_ref, in_swap_ref, m)
        cot = gathered_rows(pieces, m, k)
        order = order_ref[k, m]
        row = block_row(order, False)
        cot_row = block_row(order, True)
        sums = new_sums()
        after, grads = [], []
        for line in range(LINES):
            x = dot(picks(row, line), received, 1, 0)
            state, new = forward_line(
                k, x, starts_ref[k, m, line : line + 1, :], gain_ref, taps_ref, mix_ref, pad
            )
            after.append(new)
            grad = dot(picks(cot_row, line), cot, 1, 0).astype(BF16)
            grads.append(backward_line(k, grad, state, gain_ref, taps_ref, mix_ref, pad, sums))
        put_home(row, jnp.concatenate(after, axis=0), m, own_ref, home_ref)
        put_next(row, jnp.concatenate(grads, axis=0), m, -1, same_ref, swap_ref)
        add_sums(sum_ref, rows_ref, sums)
        return carry

    lax.fori_loop(0, CHIPS, holder, 0)
    end_sums(sum_ref, rows_ref)


def share_out(sum_refs, small_ref, keep_ref, send_ref):
    zone, core = place_of()
    for r in range(NL):
        for k, ref in enumerate(sum_refs):
            small_ref[r, 2 * k : 2 * k + 2, :] = ref[CH + 2 * r : CH + 2 * r + 2, :]
        small_ref[r, 6:8, :] = jnp.zeros((2, CH), F32)
    for r, out in ((2 * zone + core, keep_ref), (2 * zone + 1 - core, send_ref)):
        for k, ref in enumerate(sum_refs):
            out[k * 16 : (k + 1) * 16, :] = ref[pl.ds(pl.multiple_of(r * 16, 16), 16), :]
        out[48:SHARE, :] = small_ref[r]


def backward_kernel(k, *refs):
    in_ref, in_swap_ref, x_ref, h_ref, gain_ref, taps_ref, mix_ref, order_ref, starts_ref = refs[:9]
    if k == 1:
        own_ref, home_ref, same_ref, swap_ref, sum_ref, imitated_ref, pad, rows_ref = refs[9:]
        zone, core = place_of()
        for m in range(CHIPS):
            for ref, first in ((own_ref, 2 * m - core), (home_ref, 2 * m + 1 - 3 * core)):
                b = jnp.bitwise_and(first - 4 * zone + 4 * NL, NL - 1)
                imitated_ref[0, pl.ds(pl.multiple_of(b * Q, Q), Q), :] = ref[m]
    else:
        sum1_ref, sum2_ref, own_ref, home_ref, keep_ref, send_ref, pad, rows_ref, sum_ref, small_ref = refs[9:]
    clear(pad)
    start_sums(sum_ref, rows_ref)

    def holder(m, carry):
        received = moved_rows(in_ref, in_swap_ref, m)
        row = block_row(order_ref[k, m], False)
        sums = new_sums()
        grads = []
        for line in range(LINES):
            grad = dot(picks(row, line), received, 1, 0).astype(BF16)
            hidden = h_ref[m, line]
            inverse, scaled, masked, keep = norm(
                x_ref[m, line].astype(F32), gain_ref[k : k + 1, :], starts_ref[k, m, line : line + 1, :]
            )
            gate = sigmoid(hidden)
            state = (inverse, scaled, masked, keep, hidden, gate, (hidden * gate).astype(BF16))
            grads.append(backward_line(k, grad, state, gain_ref, taps_ref, mix_ref, pad, sums))
        if k == 1:
            put_next(row, jnp.concatenate(grads, axis=0), m, -1, same_ref, swap_ref)
        else:
            put_home(row, jnp.concatenate(grads, axis=0), m, own_ref, home_ref)
        add_sums(sum_ref, rows_ref, sums)
        return carry

    lax.fori_loop(0, CHIPS, holder, 0)
    end_sums(sum_ref, rows_ref)
    if k == 0:
        share_out((sum_ref, sum1_ref, sum2_ref), small_ref, keep_ref, send_ref)


def finish_kernel(own_ref, other_ref, grad_ref, home_ref, mix_ref, taps_ref, gain_ref, out_ref, tail_ref):
    zone, core = place_of()
    for m in range(CHIPS):
        for ref, b in ((grad_ref, 2 * m + core), (home_ref, 2 * m + 1 - core)):
            out_ref[0, pl.ds(pl.multiple_of(b * Q, Q), Q), :] = ref[m]
    for ref, side in ((own_ref, core), (other_ref, 1 - core)):
        for back in range(CHIPS):
            r = 2 * wrap(zone - back + CHIPS) + side
            for k in range(3):
                mix_ref[k, pl.ds(pl.multiple_of(r * 16, 16), 16), :] = ref[back, k * 16 : (k + 1) * 16, :]
            tail_ref[r] = ref[back, 48:SHARE, :]
    for k in range(3):
        for r in range(NL):
            pair = tail_ref[r, 2 * k : 2 * k + 2, :]
            if r < NL - 1:
                taps_ref[k, 2 * r : 2 * r + 2, :] = pair
            else:
                taps_ref[k, 2 * r : 2 * r + 1, :] = pair[0:1]
                gain_ref[k : k + 1, :] = pair[1:2]


def call(kernel, outs, name, n_in, scratch=(), scalars=0):
    smem = pl.BlockSpec(memory_space=pltpu.SMEM)
    vmem = pl.BlockSpec(memory_space=pltpu.VMEM)
    return pl.pallas_call(
        kernel,
        out_shape=outs,
        in_specs=[smem] * scalars + [vmem] * (n_in - scalars),
        out_specs=[vmem] * len(outs),
        scratch_shapes=[pltpu.VMEM(dims, F32) for dims in scratch],
        name=name,
        compiler_params=pltpu.CompilerParams(vmem_limit_bytes=VMEM_GRANT),
    )


def shape(*dims, dtype=BF16):
    return jax.ShapeDtypeStruct(dims, dtype)


def swap(values):
    return lax.ppermute(values, "line", [(i, i ^ 1) for i in range(NL)])


def from_chips(values):
    got = {
        back: lax.ppermute(values, "line", [(i, (i + 2 * back) % NL) for i in range(NL)])
        for back in (2, 1, 3)
    }
    return [values, got[1], got[2], got[3]]


def sum_over_dp(part):
    size = lax.axis_size("dp")
    stride = 1
    while stride < size:
        ring = 4 if size % (stride * 4) == 0 else 2
        got = [part]
        for turn in range(1, ring):
            pairs = []
            for i in range(size):
                at = i // stride % ring
                pairs.append((i, i + ((at + turn) % ring - at) * stride))
            got.append(lax.ppermute(part, "dp", pairs))
        part = sum(got[1:], got[0])
        stride *= ring
    return part


def body(fields, cotangent, norm_gain, kernel, mix_weight, line_order, line_starts):
    dp_size = lax.axis_size("dp")
    weights = (norm_gain, kernel, mix_weight)
    quarter = shape(CHIPS, Q, CH)
    moving = shape(CHIPS, CHIPS, Q, CH)
    tables = (shape(3, CHIPS, 1, CELLS, dtype=I32), shape(3, CHIPS, LINES, CH, dtype=F32))
    state = (shape(CHIPS, LINES, LINE, CH), shape(CHIPS, LINES, LINE, CH, dtype=F32))
    sums = shape(ROWS, CH, dtype=F32)
    pad = (LINE + 16, CH)
    parts = (TAPS + 1, 8, CH)

    keep, keep_cot, send, extra = call(
        prep_kernel, (quarter, quarter, shape(NL, Q, CH), shape(EXTRA, CH)), "prep", 4, scalars=1
    )(line_starts, fields, cotangent, line_order)
    got = swap(send)
    piece = jnp.concatenate([keep.reshape(HALF, CH), got[:CHIPS].reshape(HALF, CH), extra])
    piece_cot = jnp.concatenate([keep_cot.reshape(HALF, CH), got[CHIPS:].reshape(HALF, CH)])
    pieces = from_chips(piece)
    pieces_cot = from_chips(piece_cot)
    order, starts, same, moved, x0, h0 = call(
        functools.partial(forward_kernel, 0), (*tables, moving, moving, *state), "fwd0", 7, scratch=(pad,)
    )(*pieces, *weights)
    given = (*weights, order, starts)
    same, moved, x1, h1 = call(
        functools.partial(forward_kernel, 1), (moving, moving, *state), "fwd1", 7, scratch=(pad,)
    )(same, swap(moved), *given)
    same, moved, own, home, sums2 = call(
        turn_kernel, (moving, moving, quarter, quarter, sums), "turn", 11, scratch=(pad, parts)
    )(same, swap(moved), *pieces_cot, *given)
    same, moved, sums1, imitated = call(
        functools.partial(backward_kernel, 1),
        (moving, moving, sums, shape(1, CELLS, CH)),
        "bwd1",
        11,
        scratch=(pad, parts),
    )(same, swap(moved), x1, h1, *given, own, swap(home))
    share = shape(SHARE, CH, dtype=F32)
    own, home, keep, send = call(
        functools.partial(backward_kernel, 0),
        (quarter, quarter, share, share),
        "bwd0",
        11,
        scratch=(pad, parts, (ROWS, CH), (NL, 8, CH)),
    )(same, swap(moved), x0, h0, *given, sums1, sums2)
    grad_scale = float(dp_size * NL * CELLS) ** (-0.5)
    part = sum_over_dp(keep + swap(send)) * grad_scale
    shares = jnp.stack(from_chips(part))
    mix_grad, kernel_grad, gain_grad, field_grad = call(
        finish_kernel,
        (
            shape(3, CH, CH, dtype=F32),
            shape(3, TAPS, CH, dtype=F32),
            shape(3, CH, dtype=F32),
            shape(1, CELLS, CH),
        ),
        "finish",
        4,
        scratch=((NL, 8, CH),),
    )(shares, swap(shares), own, swap(home))
    return imitated, field_grad, mix_grad, kernel_grad, gain_grad


def solution(mesh):
    in_specs = (
        P("dp", "line", None),
        P("dp", "line", None),
        P(),
        P(),
        P(),
        P(None, "line"),
        P(None, "line"),
    )
    out_specs = (P("dp", "line", None), P("dp", "line", None), P(), P(), P())
    return jax.shard_map(body, mesh=mesh, in_specs=in_specs, out_specs=out_specs, check_vma=False)
```

time: 164 us -> 127 us (0.77); the launches traced: 162 us -> 127 us
  blocking collectives: 90.8 us -> 0 us
  starting transfers between devices: 22.5 us -> 50 us
  Pallas kernels: 20 us -> 39.4 us
  waiting for transfers between devices: 23.4 us -> 33.5 us
    all_to_all x6 -> x0, blocking collectives: 90.8 us -> none  [exchange(): lax.all_to_all(blocks, 'line', split_axis=0, concat_axis=0, tiled=True)]
    ppermute x5 -> x25, starting transfers between devices: 8.2 us -> 50 us  [the longest x9 23.1 us: from_chips(): lax.ppermute(values, 'line', [(i, (i + 2 * back) % NL) for i in range(NL)])]
    ppermute x5 -> x25, waiting for transfers between devices: 5.95 us -> 33.5 us  [the longest x9 19 us: from_chips(): lax.ppermute(values, 'line', [(i, (i + 2 * back) % NL) for i in range(NL)])]
    pallas_call x6 -> x7, Pallas kernels: 20 us -> 39.4 us  [the longest x1 10.9 us: body(): call(turn_kernel, (moving, moving, quarter, quarter, sums), 'turn', 11, s...]
    all_to_all x2 -> x0, waiting for transfers between devices: 17.5 us -> none  [exchange(): lax.all_to_all(blocks, 'line', split_axis=0, concat_axis=0, tiled=True)]
    all_to_all x2 -> x0, starting transfers between devices: 14.3 us -> none  [exchange(): lax.all_to_all(blocks, 'line', split_axis=0, concat_axis=0, tiled=True)]
    unnamed x6 -> x14, local copies, waits for them, and re-layouts: 1.24 us -> 3.2 us
  transfers between devices with their start and end apart: 7 -> 25, of which waited for: 6 -> 17; matrix products, arithmetic and copies ran while one was open for 0% -> 0% of each run, Pallas kernels for 0% -> 0%
where the time goes in v3:
time: 127 us
  starting transfers between devices  50 us (39%)
  Pallas kernels  39.4 us (31%)
  waiting for transfers between devices  33.5 us (26%)
  local copies, waits for them, and re-layouts  3.21 us (3%)
    ppermute x9, starting transfers between devices, from_chips(): lax.ppermute(values, 'line', [(i, (i + 2 * back) % NL) for i in range(NL)])  23.1 us
    ppermute x9, waiting for transfers between devices, from_chips(): lax.ppermute(values, 'line', [(i, (i + 2 * back) % NL) for i in range(NL)])  19 us
    ppermute x9, starting transfers between devices, swap(): return lax.ppermute(values, 'line', [(i, i ^ 1) for i in range(NL)])  15.7 us
    ppermute x7, starting transfers between devices, sum_over_dp(): got.append(lax.ppermute(part, 'dp', pairs))  11.2 us
    pallas_call x1, Pallas kernels, body(): call(turn_kernel, (moving, moving, quarter, quarter, sums), 'turn', 11, s...  10.9 us
    ppermute x7, waiting for transfers between devices, sum_over_dp(): got.append(lax.ppermute(part, 'dp', pairs))  8.16 us
    pallas_call x1, Pallas kernels, body(): call(functools.partial(forward_kernel, 0), (*tables, moving, moving, *sta...  7.25 us
    pallas_call x1, Pallas kernels, body(): call(functools.partial(forward_kernel, 1), (moving, moving, *state), 'fwd...  7.19 us
  transfers between devices with their start and end apart: 25, of which 17 were waited for; matrix products, arithmetic and copies ran while one was open for 0% of the time, Pallas kernels for 0%

profile of v3, /device:TPU:1, one launch (start us, length us, event | category | flops | bytes accessed | tf_op | source)
XLA Modules:
  0.0 126.8 jit_solution(8841903949933058170)
XLA Ops:
  4.4 3.3 %collective-permute-start = (bf16[8,64,128]{2,1,0:T(8,128)(2,1)S(1)}, bf16[8,64,128]{2,1,0:T(8,128)(2,1)S(1)}, u32[]{:S(2)}, u32[]{:S(2)}) collective-permute-start(bf16[8,64,128]{2,1,0:T(8,128)(2,1)S(1)} %get-tuple-element.37), channel_id=1, source_target_pairs={{0,32},{32,0},{64,96},{96,64},{128,160},{160,128},{192,224},{224,1... | collective-permute-start | bytes 393224 | tf_op jit(solution)/shard_map/ppermute | solution.py:390
  8.8 4.4 %collective-permute-start.3 = (bf16[560,128]{1,0:T(8,128)(2,1)S(1)}, bf16[560,128]{1,0:T(8,128)(2,1)S(1)}, u32[]{:S(2)}, u32[]{:S(2)}) collective-permute-start(bf16[560,128]{1,0:T(8,128)(2,1)S(1)} %pad_maximum_fusion.refs_0_), channel_id=1, source_target_pairs={{0,192},{32,224},{64,0},{96,32},{128,64},{160,96},{192,128},{224,1... | collective-permute-start | bytes 430088 | tf_op jit(solution)/shard_map/ppermute | solution.py:395
  14.2 2.3 %collective-permute-start.1 = (bf16[560,128]{1,0:T(8,128)(2,1)S(1)}, bf16[560,128]{1,0:T(8,128)(2,1)S(1)}, u32[]{:S(2)}, u32[]{:S(2)}) collective-permute-start(bf16[560,128]{1,0:T(8,128)(2,1)S(1)} %pad_maximum_fusion.refs_0_), channel_id=1, source_target_pairs={{0,64},{32,96},{64,128},{96,160},{128,192},{160,224},{192,0},{224,... | collective-permute-start | bytes 430088 | tf_op jit(solution)/shard_map/ppermute | solution.py:395
  16.4 3.4 %collective-permute-done.3.refs_3_ = bf16[560,128]{1,0:T(8,128)(2,1)S(1)} collective-permute-done((bf16[560,128]{1,0:T(8,128)(2,1)S(1)}, bf16[560,128]{1,0:T(8,128)(2,1)S(1)}, u32[]{:S(2)}, u32[]{:S(2)}) %collective-permute-start.3) | collective-permute-done | bytes 143392 | tf_op jit(solution)/shard_map/ppermute | solution.py:395
  19.8 5.4 %collective-permute-done.2.refs_2_ = bf16[560,128]{1,0:T(8,128)(2,1)S(1)} collective-permute-done((bf16[560,128]{1,0:T(8,128)(2,1)S(1)}, bf16[560,128]{1,0:T(8,128)(2,1)S(1)}, u32[]{:S(2)}, u32[]{:S(2)}) %collective-permute-start.2) | collective-permute-done | bytes 143392 | tf_op jit(solution)/shard_map/ppermute | solution.py:395
  25.2 7.2 %fwd0.1 = (s32[3,4,1,512]{3,2,1,0:T(1,128)S(1)}, f32[3,4,4,128]{3,2,1,0:T(4,128)S(1)}, bf16[4,4,64,128]{3,2,1,0:T(8,128)(2,1)S(1)}, bf16[4,4,64,128]{3,2,1,0:T(8...) custom-call(bf16[560,128]{1,0:T(8,128)(2,1)S(1)} %pad_maximum_fusion.refs_0_, ...), custom_call_target="tpu_custom_call" | custom-call | tf_op jit(solution)/shard_map/fwd0/pallas_call | solution.py:437
  32.5 2.5 %collective-permute-start.4 = (bf16[4,4,64,128]{3,2,1,0:T(8,128)(2,1)S(1)}, bf16[4,4,64,128]{3,2,1,0:T(8,128)(2,1)S(1)}, u32[]{:S(2)}, u32[]{:S(2)}) collective-permute-start(bf16[4,4,64,128]{3,2,1,0:T(8,128)(2,1)S(1)} %get-tuple-element.40), channel_id=1, source_target_pairs={{0,32},{32,0},{64,96},{96,64},{128,160},{160,128},{192,224},{224,1... | collective-permute-start | bytes 786440 | tf_op jit(solution)/shard_map/ppermute | solution.py:390
  36.1 7.2 %fwd1.1 = (bf16[4,4,64,128]{3,2,1,0:T(8,128)(2,1)S(1)}, bf16[4,4,64,128]{3,2,1,0:T(8,128)(2,1)S(1)}, bf16[4,4,128,128]{3,2,1,0:T(8,128)(2,1)S(1)}, f32[4,4,128,128]{3,2,1,0:T(8,128)S(1)}) custom-call(bf16[4,4,64,128]{3,2,1,0:T(8,128)(2,1)S(1)} %get-tuple-element.39.refs_0_, bf16[4,4,64,128]{3,2,1,0:T(8,128)(2,1)S(1)} %collective-permute-done.4.refs_1_, ...), custom_call_target="tpu_custom_call" | custom-call | tf_op jit(solution)/shard_map/fwd1/pallas_call | solution.py:441
  43.8 3.4 %collective-permute-start.8 = (bf16[512,128]{1,0:T(8,128)(2,1)S(1)}, bf16[512,128]{1,0:T(8,128)(2,1)S(1)}, u32[]{:S(2)}, u32[]{:S(2)}) collective-permute-start(bf16[512,128]{1,0:T(8,128)(2,1)S(1)} %pad_maximum_fusion.1.refs_2_), channel_id=1, source_target_pairs={{0,192},{32,224},{64,0},{96,32},{128,64},{160,96},{192,128},{224,1... | collective-permute-start | bytes 393224 | tf_op jit(solution)/shard_map/ppermute | solution.py:395
  49.0 2.0 %collective-permute-start.6 = (bf16[512,128]{1,0:T(8,128)(2,1)S(1)}, bf16[512,128]{1,0:T(8,128)(2,1)S(1)}, u32[]{:S(2)}, u32[]{:S(2)}) collective-permute-start(bf16[512,128]{1,0:T(8,128)(2,1)S(1)} %pad_maximum_fusion.1.refs_2_), channel_id=1, source_target_pairs={{0,64},{32,96},{64,128},{96,160},{128,192},{160,224},{192,0},{224,... | collective-permute-start | bytes 393224 | tf_op jit(solution)/shard_map/ppermute | solution.py:395
  51.0 7.1 %collective-permute-done.7.refs_4_ = bf16[512,128]{1,0:T(8,128)(2,1)S(1)} collective-permute-done((bf16[512,128]{1,0:T(8,128)(2,1)S(1)}, bf16[512,128]{1,0:T(8,128)(2,1)S(1)}, u32[]{:S(2)}, u32[]{:S(2)}) %collective-permute-start.7) | collective-permute-done | bytes 131104 | tf_op jit(solution)/shard_map/ppermute | solution.py:395
  58.6 10.9 %turn.1 = (bf16[4,4,64,128]{3,2,1,0:T(8,128)(2,1)S(1)}, bf16[4,4,64,128]{3,2,1,0:T(8,128)(2,1)S(1)}, bf16[4,64,128]{2,1,0:T(8,128)(2,1)S(1)}, bf16[4,64,128]{2,1,0:T(8,128)(2,1)S(1)}, f32[144,128]{1,0:T(8,128)S(1)}) custom-call(bf16[4,4,64,128]{3,2,1,0:T(8,128)(2,1)S(1)} %get-tuple-element.43.refs_0_, ...), custom_call_target="tpu_custom_call" | custom-call | tf_op jit(solution)/shard_map/turn/pallas_call | solution.py:444
  69.6 2.0 %collective-permute-start.9 = (bf16[4,4,64,128]{3,2,1,0:T(8,128)(2,1)S(1)}, bf16[4,4,64,128]{3,2,1,0:T(8,128)(2,1)S(1)}, u32[]{:S(2)}, u32[]{:S(2)}) collective-permute-start(bf16[4,4,64,128]{3,2,1,0:T(8,128)(2,1)S(1)} %get-tuple-element.47), channel_id=1, source_target_pairs={{0,32},{32,0},{64,96},{96,64},{128,160},{160,128},{192,224},{224,1... | collective-permute-start | bytes 786440 | tf_op jit(solution)/shard_map/ppermute | solution.py:390
  72.9 6.6 %bwd1.1 = (bf16[4,4,64,128]{3,2,1,0:T(8,128)(2,1)S(1)}, bf16[4,4,64,128]{3,2,1,0:T(8,128)(2,1)S(1)}, f32[144,128]{1,0:T(8,128)S(1)}, bf16[1,512,128]{2,1,0:T(8,128)(2,1)}) custom-call(bf16[4,4,64,128]{3,2,1,0:T(8,128)(2,1)S(1)} %get-tuple-element.46.refs_0_, bf16[4,4,64,128]{3,2,1,0:T(8,128)(2,1)S(1)} %collective-permute-done.9.refs_1_, ...), custom_call_target="tpu_custom_call" | custom-call | tf_op jit(solution)/shard_map/bwd1/pallas_call | solution.py:447
  81.1 6.1 %bwd0.1 = (bf16[4,64,128]{2,1,0:T(8,128)(2,1)S(1)}, bf16[4,64,128]{2,1,0:T(8,128)(2,1)S(1)}, f32[56,128]{1,0:T(8,128)S(1)}, f32[56,128]{1,0:T(8,128)S(1)}) custom-call(bf16[4,4,64,128]{3,2,1,0:T(8,128)(2,1)S(1)} %get-tuple-element.53.refs_0_, bf16[4,4,64,128]{3,2,1,0:T(8,128)(2,1)S(1)} %collective-permute-done.11.refs_1_, ...), custom_call_target="tpu_custom_call" | custom-call | tf_op jit(solution)/shard_map/bwd0/pallas_call | solution.py:455
  88.5 2.8 %collective-permute-start.15 = (f32[56,128]{1,0:T(8,128)S(1)}, f32[56,128]{1,0:T(8,128)S(1)}, u32[]{:S(2)}, u32[]{:S(2)}) collective-permute-start(f32[56,128]{1,0:T(8,128)S(1)} %add.24), channel_id=1, source_target_pairs={{0,3},{1,0},{2,1},{3,2},{4,7},{5,4},{6,5},{7,6},{8,11},{9,8},{10,9... | collective-permute-start | bytes 86024 | tf_op jit(solution)/shard_map/ppermute | solution.py:412
  92.3 3.2 %collective-permute-done.14 = f32[56,128]{1,0:T(8,128)S(1)} collective-permute-done((f32[56,128]{1,0:T(8,128)S(1)}, f32[56,128]{1,0:T(8,128)S(1)}, u32[]{:S(2)}, u32[]{:S(2)}) %collective-permute-start.14) | collective-permute-done | bytes 28704 | tf_op jit(solution)/shard_map/ppermute | solution.py:412
  95.8 2.6 %collective-permute-start.18 = (f32[56,128]{1,0:T(8,128)S(1)}, f32[56,128]{1,0:T(8,128)S(1)}, u32[]{:S(2)}, u32[]{:S(2)}) collective-permute-start(f32[56,128]{1,0:T(8,128)S(1)} %add_add_fusion.1), channel_id=1, source_target_pairs={{0,12},{1,13},{2,14},{3,15},{4,0},{5,1},{6,2},{7,3},{8,4},{9,5},{1... | collective-permute-start | bytes 86024 | tf_op jit(solution)/shard_map/ppermute | solution.py:412
  99.4 3.1 %collective-permute-done.17 = f32[56,128]{1,0:T(8,128)S(1)} collective-permute-done((f32[56,128]{1,0:T(8,128)S(1)}, f32[56,128]{1,0:T(8,128)S(1)}, u32[]{:S(2)}, u32[]{:S(2)}) %collective-permute-start.17) | collective-permute-done | bytes 28704 | tf_op jit(solution)/shard_map/ppermute | solution.py:412
  102.9 3.7 %collective-permute-start.19 = (f32[56,128]{1,0:T(8,128)S(1)}, f32[56,128]{1,0:T(8,128)S(1)}, u32[]{:S(2)}, u32[]{:S(2)}) collective-permute-start(f32[56,128]{1,0:T(8,128)S(1)} %add_add_fusion), channel_id=1, source_target_pairs={{0,16},{1,17},{2,18},{3,19},{4,20},{5,21},{6,22},{7,23},{8,24},{9,... | collective-permute-start | bytes 86024 | tf_op jit(solution)/shard_map/ppermute | solution.py:412
  107.8 3.0 %collective-permute-start.22 = (f32[56,128]{1,0:T(8,128)S(1)}, f32[56,128]{1,0:T(8,128)S(1)}, u32[]{:S(2)}, u32[]{:S(2)}) collective-permute-start(f32[56,128]{1,0:T(8,128)S(1)} %add_multiply_fusion), channel_id=1, source_target_pairs={{0,192},{32,224},{64,0},{96,32},{128,64},{160,96},{192,128},{224,1... | collective-permute-start | bytes 86024 | tf_op jit(solution)/shard_map/ppermute | solution.py:395
  110.8 3.0 %collective-permute-start.21 = (f32[56,128]{1,0:T(8,128)S(1)}, f32[56,128]{1,0:T(8,128)S(1)}, u32[]{:S(2)}, u32[]{:S(2)}) collective-permute-start(f32[56,128]{1,0:T(8,128)S(1)} %add_multiply_fusion), channel_id=1, source_target_pairs={{0,128},{32,160},{64,192},{96,224},{128,0},{160,32},{192,64},{224,... | collective-permute-start | bytes 86024 | tf_op jit(solution)/shard_map/ppermute | solution.py:395
  113.8 2.3 %collective-permute-start.20 = (f32[56,128]{1,0:T(8,128)S(1)}, f32[56,128]{1,0:T(8,128)S(1)}, u32[]{:S(2)}, u32[]{:S(2)}) collective-permute-start(f32[56,128]{1,0:T(8,128)S(1)} %add_multiply_fusion), channel_id=1, source_target_pairs={{0,64},{32,96},{64,128},{96,160},{128,192},{160,224},{192,0},{224,... | collective-permute-start | bytes 86024 | tf_op jit(solution)/shard_map/ppermute | solution.py:395
  118.6 6.1 %collective-permute-start.23 = (f32[4,56,128]{2,1,0:T(8,128)S(1)}, f32[4,56,128]{2,1,0:T(8,128)S(1)}, u32[]{:S(2)}, u32[]{:S(2)}) collective-permute-start(f32[4,56,128]{2,1,0:T(8,128)S(1)} %pad_maximum_fusion.2.own_ref), channel_id=1, source_target_pairs={{0,32},{32,0},{64,96},{96,64},{128,160},{160,128},{192,224},{224,1... | collective-permute-start | bytes 344072 | tf_op jit(solution)/shard_map/ppermute | solution.py:390
  (55 shorter events, 22.7 us)
Async XLA Ops:
  4.4 4.3 %collective-permute-start = (bf16[8,64,128]{2,1,0:T(8,128)(2,1)S(1)}, bf16[8,64,128]{2,1,0:T(8,128)(2,1)S(1)}, u32[]{:S(2)}, u32[]{:S(2)}) collective-permute-start(bf16[8,64,128]{2,1,0:T(8,128)(2,1)S(1)} %get-tuple-element.37), channel_id=1, source_target_pairs={{0,32},{32,0},{64,96},{96,64},{128,160},{160,128},{192,224},{224,1... | collective-permute-start | bytes 393224 | tf_op jit(solution)/shard_map/ppermute | solution.py:390
  8.8 11.0 %collective-permute-start.3 = (bf16[560,128]{1,0:T(8,128)(2,1)S(1)}, bf16[560,128]{1,0:T(8,128)(2,1)S(1)}, u32[]{:S(2)}, u32[]{:S(2)}) collective-permute-start(bf16[560,128]{1,0:T(8,128)(2,1)S(1)} %pad_maximum_fusion.refs_0_), channel_id=1, source_target_pairs={{0,192},{32,224},{64,0},{96,32},{128,64},{160,96},{192,128},{224,1... | collective-permute-start | bytes 430088 | tf_op jit(solution)/shard_map/ppermute | solution.py:395
  13.2 12.1 %collective-permute-start.2 = (bf16[560,128]{1,0:T(8,128)(2,1)S(1)}, bf16[560,128]{1,0:T(8,128)(2,1)S(1)}, u32[]{:S(2)}, u32[]{:S(2)}) collective-permute-start(bf16[560,128]{1,0:T(8,128)(2,1)S(1)} %pad_maximum_fusion.refs_0_), channel_id=1, source_target_pairs={{0,128},{32,160},{64,192},{96,224},{128,0},{160,32},{192,64},{224,... | collective-permute-start | bytes 430088 | tf_op jit(solution)/shard_map/ppermute | solution.py:395
  14.2 11.1 %collective-permute-start.1 = (bf16[560,128]{1,0:T(8,128)(2,1)S(1)}, bf16[560,128]{1,0:T(8,128)(2,1)S(1)}, u32[]{:S(2)}, u32[]{:S(2)}) collective-permute-start(bf16[560,128]{1,0:T(8,128)(2,1)S(1)} %pad_maximum_fusion.refs_0_), channel_id=1, source_target_pairs={{0,64},{32,96},{64,128},{96,160},{128,192},{160,224},{192,0},{224,... | collective-permute-start | bytes 430088 | tf_op jit(solution)/shard_map/ppermute | solution.py:395
  32.5 3.6 %collective-permute-start.4 = (bf16[4,4,64,128]{3,2,1,0:T(8,128)(2,1)S(1)}, bf16[4,4,64,128]{3,2,1,0:T(8,128)(2,1)S(1)}, u32[]{:S(2)}, u32[]{:S(2)}) collective-permute-start(bf16[4,4,64,128]{3,2,1,0:T(8,128)(2,1)S(1)} %get-tuple-element.40), channel_id=1, source_target_pairs={{0,32},{32,0},{64,96},{96,64},{128,160},{160,128},{192,224},{224,1... | collective-permute-start | bytes 786440 | tf_op jit(solution)/shard_map/ppermute | solution.py:390
  43.3 15.3 %collective-permute-start.5 = (bf16[4,4,64,128]{3,2,1,0:T(8,128)(2,1)S(1)}, bf16[4,4,64,128]{3,2,1,0:T(8,128)(2,1)S(1)}, u32[]{:S(2)}, u32[]{:S(2)}) collective-permute-start(bf16[4,4,64,128]{3,2,1,0:T(8,128)(2,1)S(1)} %get-tuple-element.44), channel_id=1, source_target_pairs={{0,32},{32,0},{64,96},{96,64},{128,160},{160,128},{192,224},{224,1... | collective-permute-start | bytes 786440 | tf_op jit(solution)/shard_map/ppermute | solution.py:390
  43.8 7.2 %collective-permute-start.8 = (bf16[512,128]{1,0:T(8,128)(2,1)S(1)}, bf16[512,128]{1,0:T(8,128)(2,1)S(1)}, u32[]{:S(2)}, u32[]{:S(2)}) collective-permute-start(bf16[512,128]{1,0:T(8,128)(2,1)S(1)} %pad_maximum_fusion.1.refs_2_), channel_id=1, source_target_pairs={{0,192},{32,224},{64,0},{96,32},{128,64},{160,96},{192,128},{224,1... | collective-permute-start | bytes 393224 | tf_op jit(solution)/shard_map/ppermute | solution.py:395
  47.2 10.9 %collective-permute-start.7 = (bf16[512,128]{1,0:T(8,128)(2,1)S(1)}, bf16[512,128]{1,0:T(8,128)(2,1)S(1)}, u32[]{:S(2)}, u32[]{:S(2)}) collective-permute-start(bf16[512,128]{1,0:T(8,128)(2,1)S(1)} %pad_maximum_fusion.1.refs_2_), channel_id=1, source_target_pairs={{0,128},{32,160},{64,192},{96,224},{128,0},{160,32},{192,64},{224,... | collective-permute-start | bytes 393224 | tf_op jit(solution)/shard_map/ppermute | solution.py:395
  49.0 9.6 %collective-permute-start.6 = (bf16[512,128]{1,0:T(8,128)(2,1)S(1)}, bf16[512,128]{1,0:T(8,128)(2,1)S(1)}, u32[]{:S(2)}, u32[]{:S(2)}) collective-permute-start(bf16[512,128]{1,0:T(8,128)(2,1)S(1)} %pad_maximum_fusion.1.refs_2_), channel_id=1, source_target_pairs={{0,64},{32,96},{64,128},{96,160},{128,192},{160,224},{192,0},{224,... | collective-permute-start | bytes 393224 | tf_op jit(solution)/shard_map/ppermute | solution.py:395
  69.6 3.3 %collective-permute-start.9 = (bf16[4,4,64,128]{3,2,1,0:T(8,128)(2,1)S(1)}, bf16[4,4,64,128]{3,2,1,0:T(8,128)(2,1)S(1)}, u32[]{:S(2)}, u32[]{:S(2)}) collective-permute-start(bf16[4,4,64,128]{3,2,1,0:T(8,128)(2,1)S(1)} %get-tuple-element.47), channel_id=1, source_target_pairs={{0,32},{32,0},{64,96},{96,64},{128,160},{160,128},{192,224},{224,1... | collective-permute-start | bytes 786440 | tf_op jit(solution)/shard_map/ppermute | solution.py:390
  71.6 1.3 collective-permute-start.10
  79.4 1.6 %collective-permute-start.11 = (bf16[4,4,64,128]{3,2,1,0:T(8,128)(2,1)S(1)}, bf16[4,4,64,128]{3,2,1,0:T(8,128)(2,1)S(1)}, u32[]{:S(2)}, u32[]{:S(2)}) collective-permute-start(bf16[4,4,64,128]{3,2,1,0:T(8,128)(2,1)S(1)} %get-tuple-element.54), channel_id=1, source_target_pairs={{0,32},{32,0},{64,96},{96,64},{128,160},{160,128},{192,224},{224,1... | collective-permute-start | bytes 786440 | tf_op jit(solution)/shard_map/ppermute | solution.py:390
  87.1 1.3 %collective-permute-start.12 = (f32[56,128]{1,0:T(8,128)S(1)}, f32[56,128]{1,0:T(8,128)S(1)}, u32[]{:S(2)}, u32[]{:S(2)}) collective-permute-start(f32[56,128]{1,0:T(8,128)S(1)} %get-tuple-element.60), channel_id=1, source_target_pairs={{0,32},{32,0},{64,96},{96,64},{128,160},{160,128},{192,224},{224,1... | collective-permute-start | bytes 86024 | tf_op jit(solution)/shard_map/ppermute | solution.py:390
  88.5 3.8 %collective-permute-start.15 = (f32[56,128]{1,0:T(8,128)S(1)}, f32[56,128]{1,0:T(8,128)S(1)}, u32[]{:S(2)}, u32[]{:S(2)}) collective-permute-start(f32[56,128]{1,0:T(8,128)S(1)} %add.24), channel_id=1, source_target_pairs={{0,3},{1,0},{2,1},{3,2},{4,7},{5,4},{6,5},{7,6},{8,11},{9,8},{10,9... | collective-permute-start | bytes 86024 | tf_op jit(solution)/shard_map/ppermute | solution.py:412
  91.2 4.2 %collective-permute-start.14 = (f32[56,128]{1,0:T(8,128)S(1)}, f32[56,128]{1,0:T(8,128)S(1)}, u32[]{:S(2)}, u32[]{:S(2)}) collective-permute-start(f32[56,128]{1,0:T(8,128)S(1)} %add.24), channel_id=1, source_target_pairs={{0,2},{1,3},{2,0},{3,1},{4,6},{5,7},{6,4},{7,5},{8,10},{9,11},{10,... | collective-permute-start | bytes 86024 | tf_op jit(solution)/shard_map/ppermute | solution.py:412
  91.6 4.2 %collective-permute-start.13 = (f32[56,128]{1,0:T(8,128)S(1)}, f32[56,128]{1,0:T(8,128)S(1)}, u32[]{:S(2)}, u32[]{:S(2)}) collective-permute-start(f32[56,128]{1,0:T(8,128)S(1)} %add.24), channel_id=1, source_target_pairs={{0,1},{1,2},{2,3},{3,0},{4,5},{5,6},{6,7},{7,4},{8,9},{9,10},{10,1... | collective-permute-start | bytes 86024 | tf_op jit(solution)/shard_map/ppermute | solution.py:412
  95.8 3.7 %collective-permute-start.18 = (f32[56,128]{1,0:T(8,128)S(1)}, f32[56,128]{1,0:T(8,128)S(1)}, u32[]{:S(2)}, u32[]{:S(2)}) collective-permute-start(f32[56,128]{1,0:T(8,128)S(1)} %add_add_fusion.1), channel_id=1, source_target_pairs={{0,12},{1,13},{2,14},{3,15},{4,0},{5,1},{6,2},{7,3},{8,4},{9,5},{1... | collective-permute-start | bytes 86024 | tf_op jit(solution)/shard_map/ppermute | solution.py:412
  98.3 4.2 %collective-permute-start.17 = (f32[56,128]{1,0:T(8,128)S(1)}, f32[56,128]{1,0:T(8,128)S(1)}, u32[]{:S(2)}, u32[]{:S(2)}) collective-permute-start(f32[56,128]{1,0:T(8,128)S(1)} %add_add_fusion.1), channel_id=1, source_target_pairs={{0,8},{1,9},{2,10},{3,11},{4,12},{5,13},{6,14},{7,15},{8,0},{9,1},... | collective-permute-start | bytes 86024 | tf_op jit(solution)/shard_map/ppermute | solution.py:412
  98.8 4.0 %collective-permute-start.16 = (f32[56,128]{1,0:T(8,128)S(1)}, f32[56,128]{1,0:T(8,128)S(1)}, u32[]{:S(2)}, u32[]{:S(2)}) collective-permute-start(f32[56,128]{1,0:T(8,128)S(1)} %add_add_fusion.1), channel_id=1, source_target_pairs={{0,4},{1,5},{2,6},{3,7},{4,8},{5,9},{6,10},{7,11},{8,12},{9,13},{1... | collective-permute-start | bytes 86024 | tf_op jit(solution)/shard_map/ppermute | solution.py:412
  102.9 5.0 %collective-permute-start.19 = (f32[56,128]{1,0:T(8,128)S(1)}, f32[56,128]{1,0:T(8,128)S(1)}, u32[]{:S(2)}, u32[]{:S(2)}) collective-permute-start(f32[56,128]{1,0:T(8,128)S(1)} %add_add_fusion), channel_id=1, source_target_pairs={{0,16},{1,17},{2,18},{3,19},{4,20},{5,21},{6,22},{7,23},{8,24},{9,... | collective-permute-start | bytes 86024 | tf_op jit(solution)/shard_map/ppermute | solution.py:412
  107.8 8.2 %collective-permute-start.22 = (f32[56,128]{1,0:T(8,128)S(1)}, f32[56,128]{1,0:T(8,128)S(1)}, u32[]{:S(2)}, u32[]{:S(2)}) collective-permute-start(f32[56,128]{1,0:T(8,128)S(1)} %add_multiply_fusion), channel_id=1, source_target_pairs={{0,192},{32,224},{64,0},{96,32},{128,64},{160,96},{192,128},{224,1... | collective-permute-start | bytes 86024 | tf_op jit(solution)/shard_map/ppermute | solution.py:395
  110.8 6.6 %collective-permute-start.21 = (f32[56,128]{1,0:T(8,128)S(1)}, f32[56,128]{1,0:T(8,128)S(1)}, u32[]{:S(2)}, u32[]{:S(2)}) collective-permute-start(f32[56,128]{1,0:T(8,128)S(1)} %add_multiply_fusion), channel_id=1, source_target_pairs={{0,128},{32,160},{64,192},{96,224},{128,0},{160,32},{192,64},{224,... | collective-permute-start | bytes 86024 | tf_op jit(solution)/shard_map/ppermute | solution.py:395
  113.8 4.9 %collective-permute-start.20 = (f32[56,128]{1,0:T(8,128)S(1)}, f32[56,128]{1,0:T(8,128)S(1)}, u32[]{:S(2)}, u32[]{:S(2)}) collective-permute-start(f32[56,128]{1,0:T(8,128)S(1)} %add_multiply_fusion), channel_id=1, source_target_pairs={{0,64},{32,96},{64,128},{96,160},{128,192},{160,224},{192,0},{224,... | collective-permute-start | bytes 86024 | tf_op jit(solution)/shard_map/ppermute | solution.py:395
  118.6 7.4 %collective-permute-start.23 = (f32[4,56,128]{2,1,0:T(8,128)S(1)}, f32[4,56,128]{2,1,0:T(8,128)S(1)}, u32[]{:S(2)}, u32[]{:S(2)}) collective-permute-start(f32[4,56,128]{2,1,0:T(8,128)S(1)} %pad_maximum_fusion.2.own_ref), channel_id=1, source_target_pairs={{0,32},{32,0},{64,96},{96,64},{128,160},{160,128},{192,224},{224,1... | collective-permute-start | bytes 344072 | tf_op jit(solution)/shard_map/ppermute | solution.py:390
  (8 other events, 53.9 us)

commit v4 on v3

--- a/solution.py
+++ b/solution.py
@@ -7,12 +7,14 @@
 from jax.experimental.pallas import tpu as pltpu
 from jax.sharding import PartitionSpec as P
 
+
 LINE = 128
 CH = 128
 TAPS = 15
 CELLS = 512
 NL = 8
 CHIPS = NL // 2
+RING = 4
 Q = CELLS // NL
 HALF = CELLS // 2
 LINES = CELLS // LINE
@@ -96,18 +98,28 @@
     pad[8 : 8 + LINE, :] = values
     for offset in OFFSETS:
         if offset == 0:
-            yield values
+            yield 0, values
         elif abs(offset) < 8:
-            yield pad[8 + offset : 8 + offset + LINE, :]
+            yield 0, pad[8 + offset : 8 + offset + LINE, :]
         elif offset > 0:
-            yield jnp.concatenate([values[offset:], jnp.zeros((offset, CH), F32)], axis=0)
+            yield 0, values[offset:]
         else:
-            yield jnp.concatenate([jnp.zeros((-offset, CH), F32), values[:offset]], axis=0)
-
-
-def clear(pad):
-    pad[0:8, :] = jnp.zeros((8, CH), F32)
-    pad[8 + LINE : 16 + LINE, :] = jnp.zeros((8, CH), F32)
+            yield -offset, values[:offset]
+
+
+def accumulate(total, first, rows):
+    size = rows.shape[0]
+    pieces = [total[:first]] if first else []
+    pieces.append(total[first : first + size] + rows)
+    if first + size < LINE:
+        pieces.append(total[first + size :])
+    return jnp.concatenate(pieces, axis=0) if len(pieces) > 1 else pieces[0]
+
+
+def clear(pads):
+    for line in range(LINES):
+        pads[line, 0:8, :] = jnp.zeros((8, CH), F32)
+        pads[line, 8 + LINE : 16 + LINE, :] = jnp.zeros((8, CH), F32)
 
 
 def norm(x, gain, start):
@@ -120,9 +132,9 @@
 
 def conv(pad, masked, taps):
     total = None
-    for t, moved in enumerate(shifts(pad, masked)):
+    for t, (first, moved) in enumerate(shifts(pad, masked)):
         term = taps[t : t + 1, :] * moved
-        total = term if total is None else total + term
+        total = term if total is None else accumulate(total, first, term)
     return total
 
 
@@ -149,11 +161,12 @@
     grad_act = dot(grad, mix_ref[k], 1, 1)
     grad_hidden = (grad_act * (gate * (1.0 + hidden * (1.0 - gate)))).astype(BF16).astype(F32)
     total = None
-    for t, moved in enumerate(shifts(pad, grad_hidden)):
+    for t, (first, moved) in enumerate(shifts(pad, grad_hidden)):
         u = t if t == 0 else (t + 1 if t % 2 else t - 1)
+        size = moved.shape[0]
         term = taps[u : u + 1, :] * moved
-        total = term if total is None else total + term
-        part = jnp.sum((moved * masked).reshape(LINE // 8, 8, CH), axis=0)
+        total = term if total is None else accumulate(total, first, term)
+        part = jnp.sum((moved * masked[first : first + size]).reshape(size // 8, 8, CH), axis=0)
         sums["rows"][u] = part if sums["rows"][u] is None else sums["rows"][u] + part
     cells = jnp.where(keep, total, 0.0).astype(BF16).astype(F32)
     part = jnp.sum((cells * scaled).reshape(LINE // 8, 8, CH), axis=0)
@@ -183,24 +196,34 @@
     sum_ref[CH:ROWS, :] = jnp.sum(rows_ref[...], axis=1)
 
 
-def prep_kernel(starts, fields_ref, cot_ref, order_ref, keep_ref, keep_cot_ref, send_ref, extra_ref):
+def prep_kernel(fields_ref, cot_ref, table_ref, begin_ref, keep_ref, keep_cot_ref, send_ref, extra_ref, order_ref, starts_ref, sem):
     _, core = place_of()
+    copies = [
+        pltpu.make_async_copy(table_ref, order_ref, sem.at[0]),
+        pltpu.make_async_copy(begin_ref, starts_ref, sem.at[1]),
+    ]
     for m in range(CHIPS):
         here = pl.ds(pl.multiple_of((2 * m + core) * Q, Q), Q)
         there = pl.ds(pl.multiple_of((2 * m + 1 - core) * Q, Q), Q)
-        keep_ref[m] = fields_ref[0, here, :]
-        keep_cot_ref[m] = cot_ref[0, here, :]
-        send_ref[m] = fields_ref[0, there, :]
-        send_ref[CHIPS + m] = cot_ref[0, there, :]
+        for source, own, first in ((fields_ref, keep_ref, 0), (cot_ref, keep_cot_ref, CHIPS)):
+            for rows, target in ((here, own.at[m]), (there, send_ref.at[first + m])):
+                copies.append(pltpu.make_async_copy(source.at[0, rows, :], target, sem.at[len(copies)]))
+    for copy in copies:
+        copy.start()
+    for copy in copies[:2]:
+        copy.wait()
     rows = []
     for k in range(3):
         order = order_ref[k : k + 1, :]
         for part in (lax.shift_right_logical(order, 1), jnp.bitwise_and(order, 1)):
             rows += [part[:, c * LINE : (c + 1) * LINE].astype(F32) for c in range(LINES)]
+    starts = starts_ref[...].astype(F32)
     for k in range(3):
-        rows += [jnp.full((1, CH), starts[k, line], I32).astype(F32) for line in range(LINES)]
+        rows += [jnp.broadcast_to(starts[k : k + 1, line : line + 1], (1, CH)) for line in range(LINES)]
     rows.append(jnp.zeros((EXTRA - len(rows), CH), F32))
     extra_ref[...] = jnp.concatenate(rows, axis=0).astype(BF16)
+    for copy in copies[2:]:
+        copy.wait()
 
 
 def read_tables(pieces, order_ref, starts_ref):
@@ -249,7 +272,7 @@
         for line in range(LINES):
             x = dot(picks(row, line), received, 1, 0)
             state, new = forward_line(
-                k, x, starts_ref[k, m, line : line + 1, :], gain_ref, taps_ref, mix_ref, pad
+                k, x, starts_ref[k, m, line : line + 1, :], gain_ref, taps_ref, mix_ref, pad.at[line]
             )
             x_ref[m, line] = x.astype(BF16)
             h_ref[m, line] = state[4]
@@ -280,11 +303,11 @@
         for line in range(LINES):
             x = dot(picks(row, line), received, 1, 0)
             state, new = forward_line(
-                k, x, starts_ref[k, m, line : line + 1, :], gain_ref, taps_ref, mix_ref, pad
+                k, x, starts_ref[k, m, line : line + 1, :], gain_ref, taps_ref, mix_ref, pad.at[line]
             )
             after.append(new)
             grad = dot(picks(cot_row, line), cot, 1, 0).astype(BF16)
-            grads.append(backward_line(k, grad, state, gain_ref, taps_ref, mix_ref, pad, sums))
+            grads.append(backward_line(k, grad, state, gain_ref, taps_ref, mix_ref, pad.at[line], sums))
         put_home(row, jnp.concatenate(after, axis=0), m, own_ref, home_ref)
         put_next(row, jnp.concatenate(grads, axis=0), m, -1, same_ref, swap_ref)
         add_sums(sum_ref, rows_ref, sums)
@@ -294,29 +317,37 @@
     end_sums(sum_ref, rows_ref)
 
 
+def ring_of():
+    return jnp.bitwise_and(lax.axis_index("dp"), RING - 1)
+
+
 def share_out(sum_refs, small_ref, keep_ref, send_ref):
-    zone, core = place_of()
+    _, core = place_of()
+    here = ring_of()
     for r in range(NL):
         for k, ref in enumerate(sum_refs):
             small_ref[r, 2 * k : 2 * k + 2, :] = ref[CH + 2 * r : CH + 2 * r + 2, :]
         small_ref[r, 6:8, :] = jnp.zeros((2, CH), F32)
-    for r, out in ((2 * zone + core, keep_ref), (2 * zone + 1 - core, send_ref)):
-        for k, ref in enumerate(sum_refs):
-            out[k * 16 : (k + 1) * 16, :] = ref[pl.ds(pl.multiple_of(r * 16, 16), 16), :]
-        out[48:SHARE, :] = small_ref[r]
+    for side, out in ((core, keep_ref), (1 - core, send_ref)):
+        for ahead in range(RING):
+            r = 2 * jnp.bitwise_and(here + ahead, RING - 1) + side
+            for k, ref in enumerate(sum_refs):
+                out[ahead, k * 16 : (k + 1) * 16, :] = ref[pl.ds(pl.multiple_of(r * 16, 16), 16), :]
+            out[ahead, 48:SHARE, :] = small_ref[r]
 
 
 def backward_kernel(k, *refs):
     in_ref, in_swap_ref, x_ref, h_ref, gain_ref, taps_ref, mix_ref, order_ref, starts_ref = refs[:9]
     if k == 1:
-        own_ref, home_ref, same_ref, swap_ref, sum_ref, imitated_ref, pad, rows_ref = refs[9:]
+        same_ref, swap_ref, sum_ref, pad, rows_ref = refs[9:]
+    else:
+        sum1_ref, sum2_ref, first_ref, second_ref = refs[9:13]
+        imitated_ref, own_ref, home_ref, keep_ref, send_ref, pad, rows_ref, sum_ref, small_ref = refs[13:]
         zone, core = place_of()
         for m in range(CHIPS):
-            for ref, first in ((own_ref, 2 * m - core), (home_ref, 2 * m + 1 - 3 * core)):
+            for ref, first in ((first_ref, 2 * m - core), (second_ref, 2 * m + 1 - 3 * core)):
                 b = jnp.bitwise_and(first - 4 * zone + 4 * NL, NL - 1)
                 imitated_ref[0, pl.ds(pl.multiple_of(b * Q, Q), Q), :] = ref[m]
-    else:
-        sum1_ref, sum2_ref, own_ref, home_ref, keep_ref, send_ref, pad, rows_ref, sum_ref, small_ref = refs[9:]
     clear(pad)
     start_sums(sum_ref, rows_ref)
 
@@ -333,7 +364,7 @@
             )
             gate = sigmoid(hidden)
             state = (inverse, scaled, masked, keep, hidden, gate, (hidden * gate).astype(BF16))
-            grads.append(backward_line(k, grad, state, gain_ref, taps_ref, mix_ref, pad, sums))
+            grads.append(backward_line(k, grad, state, gain_ref, taps_ref, mix_ref, pad.at[line], sums))
         if k == 1:
             put_next(row, jnp.concatenate(grads, axis=0), m, -1, same_ref, swap_ref)
         else:
@@ -348,13 +379,14 @@
 
 
 def finish_kernel(own_ref, other_ref, grad_ref, home_ref, mix_ref, taps_ref, gain_ref, out_ref, tail_ref):
-    zone, core = place_of()
+    _, core = place_of()
+    here = ring_of()
     for m in range(CHIPS):
         for ref, b in ((grad_ref, 2 * m + core), (home_ref, 2 * m + 1 - core)):
             out_ref[0, pl.ds(pl.multiple_of(b * Q, Q), Q), :] = ref[m]
     for ref, side in ((own_ref, core), (other_ref, 1 - core)):
-        for back in range(CHIPS):
-            r = 2 * wrap(zone - back + CHIPS) + side
+        for back in range(RING):
+            r = 2 * jnp.bitwise_and(here - back + RING, RING - 1) + side
             for k in range(3):
                 mix_ref[k, pl.ds(pl.multiple_of(r * 16, 16), 16), :] = ref[back, k * 16 : (k + 1) * 16, :]
             tail_ref[r] = ref[back, 48:SHARE, :]
@@ -368,17 +400,15 @@
                 gain_ref[k : k + 1, :] = pair[1:2]
 
 
-def call(kernel, outs, name, n_in, scratch=(), scalars=0):
-    smem = pl.BlockSpec(memory_space=pltpu.SMEM)
+def call(kernel, outs, n_in, scratch=(), space=pltpu.VMEM, grant=VMEM_GRANT):
     vmem = pl.BlockSpec(memory_space=pltpu.VMEM)
     return pl.pallas_call(
         kernel,
         out_shape=outs,
-        in_specs=[smem] * scalars + [vmem] * (n_in - scalars),
+        in_specs=[pl.BlockSpec(memory_space=space)] * n_in,
         out_specs=[vmem] * len(outs),
-        scratch_shapes=[pltpu.VMEM(dims, F32) for dims in scratch],
-        name=name,
-        compiler_params=pltpu.CompilerParams(vmem_limit_bytes=VMEM_GRANT),
+        scratch_shapes=[pltpu.VMEM(dims, F32) if isinstance(dims, tuple) else dims for dims in scratch],
+        compiler_params=pltpu.CompilerParams(vmem_limit_bytes=grant),
     )
 
 
@@ -398,24 +428,26 @@
     return [values, got[1], got[2], got[3]]
 
 
-def sum_over_dp(part):
+def to_ring(values, turn, ring, stride):
+    pairs = []
+    for i in range(lax.axis_size("dp")):
+        at = i // stride % ring
+        pairs.append((i, i + ((at + turn) % ring - at) * stride))
+    return lax.ppermute(values, "dp", pairs)
+
+
+def sum_over_dp(parts):
     size = lax.axis_size("dp")
-    stride = 1
+    part = sum((to_ring(parts[turn], turn, RING, 1) for turn in (1, 3, 2)), parts[0])
+    stride = RING
     while stride < size:
-        ring = 4 if size % (stride * 4) == 0 else 2
-        got = [part]
-        for turn in range(1, ring):
-            pairs = []
-            for i in range(size):
-                at = i // stride % ring
-                pairs.append((i, i + ((at + turn) % ring - at) * stride))
-            got.append(lax.ppermute(part, "dp", pairs))
-        part = sum(got[1:], got[0])
+        ring = RING if size % (stride * RING) == 0 else 2
+        part = sum((to_ring(part, turn, ring, stride) for turn in range(1, ring)), part)
         stride *= ring
     return part
 
 
-def body(fields, cotangent, norm_gain, kernel, mix_weight, line_order, line_starts):
+def block(fields, cotangent, norm_gain, kernel, mix_weight, line_order, line_starts):
     dp_size = lax.axis_size("dp")
     weights = (norm_gain, kernel, mix_weight)
     quarter = shape(CHIPS, Q, CH)
@@ -423,45 +455,49 @@
     tables = (shape(3, CHIPS, 1, CELLS, dtype=I32), shape(3, CHIPS, LINES, CH, dtype=F32))
     state = (shape(CHIPS, LINES, LINE, CH), shape(CHIPS, LINES, LINE, CH, dtype=F32))
     sums = shape(ROWS, CH, dtype=F32)
-    pad = (LINE + 16, CH)
+    pad = (LINES, LINE + 16, CH)
     parts = (TAPS + 1, 8, CH)
 
     keep, keep_cot, send, extra = call(
-        prep_kernel, (quarter, quarter, shape(NL, Q, CH), shape(EXTRA, CH)), "prep", 4, scalars=1
-    )(line_starts, fields, cotangent, line_order)
+        prep_kernel,
+        (quarter, quarter, shape(NL, Q, CH), shape(EXTRA, CH)),
+        4,
+        scratch=(pltpu.VMEM((3, CELLS), I32), pltpu.VMEM((3, LINES), I32), pltpu.SemaphoreType.DMA((18,))),
+        space=pltpu.HBM,
+        grant=None,
+    )(fields, cotangent, line_order, line_starts)
     got = swap(send)
     piece = jnp.concatenate([keep.reshape(HALF, CH), got[:CHIPS].reshape(HALF, CH), extra])
     piece_cot = jnp.concatenate([keep_cot.reshape(HALF, CH), got[CHIPS:].reshape(HALF, CH)])
     pieces = from_chips(piece)
     pieces_cot = from_chips(piece_cot)
     order, starts, same, moved, x0, h0 = call(
-        functools.partial(forward_kernel, 0), (*tables, moving, moving, *state), "fwd0", 7, scratch=(pad,)
+        functools.partial(forward_kernel, 0), (*tables, moving, moving, *state), 7, scratch=(pad,)
     )(*pieces, *weights)
     given = (*weights, order, starts)
     same, moved, x1, h1 = call(
-        functools.partial(forward_kernel, 1), (moving, moving, *state), "fwd1", 7, scratch=(pad,)
+        functools.partial(forward_kernel, 1), (moving, moving, *state), 7, scratch=(pad,)
     )(same, swap(moved), *given)
-    same, moved, own, home, sums2 = call(
-        turn_kernel, (moving, moving, quarter, quarter, sums), "turn", 11, scratch=(pad, parts)
+    same, moved, first, second, sums2 = call(
+        turn_kernel, (moving, moving, quarter, quarter, sums), 11, scratch=(pad, parts)
     )(same, swap(moved), *pieces_cot, *given)
-    same, moved, sums1, imitated = call(
-        functools.partial(backward_kernel, 1),
-        (moving, moving, sums, shape(1, CELLS, CH)),
-        "bwd1",
-        11,
-        scratch=(pad, parts),
-    )(same, swap(moved), x1, h1, *given, own, swap(home))
-    share = shape(SHARE, CH, dtype=F32)
-    own, home, keep, send = call(
+    second = swap(second)
+    moved = swap(moved)
+    same, moved, sums1 = call(
+        functools.partial(backward_kernel, 1), (moving, moving, sums), 9, scratch=(pad, parts)
+    )(same, moved, x1, h1, *given)
+    share = shape(RING, SHARE, CH, dtype=F32)
+    imitated, own, home, keep, send = call(
         functools.partial(backward_kernel, 0),
-        (quarter, quarter, share, share),
-        "bwd0",
-        11,
+        (shape(1, CELLS, CH), quarter, quarter, share, share),
+        13,
         scratch=(pad, parts, (ROWS, CH), (NL, 8, CH)),
-    )(same, swap(moved), x0, h0, *given, sums1, sums2)
+    )(same, swap(moved), x0, h0, *given, sums1, sums2, first, second)
     grad_scale = float(dp_size * NL * CELLS) ** (-0.5)
-    part = sum_over_dp(keep + swap(send)) * grad_scale
-    shares = jnp.stack(from_chips(part))
+    got = swap(send)
+    home = swap(home)
+    part = sum_over_dp(keep + got) * grad_scale
+    shares = jnp.stack([part] + [to_ring(part, turn, RING, 1) for turn in range(1, RING)])
     mix_grad, kernel_grad, gain_grad, field_grad = call(
         finish_kernel,
         (
@@ -470,10 +506,9 @@
             shape(3, CH, dtype=F32),
             shape(1, CELLS, CH),
         ),
-        "finish",
         4,
         scratch=((NL, 8, CH),),
-    )(shares, swap(shares), own, swap(home))
+    )(shares, swap(shares), own, home)
     return imitated, field_grad, mix_grad, kernel_grad, gain_grad
 
 
@@ -488,4 +523,4 @@
         P(None, "line"),
     )
     out_specs = (P("dp", "line", None), P("dp", "line", None), P(), P(), P())
-    return jax.shard_map(body, mesh=mesh, in_specs=in_specs, out_specs=out_specs, check_vma=False)
+    return jax.shard_map(block, mesh=mesh, in_specs=in_specs, out_specs=out_specs, check_vma=False)

time: 127 us -> 121 us (0.953)
  starting transfers between devices: 50 us -> 45.6 us
  local copies, waits for them, and re-layouts: 3.21 us -> 0.72 us
    ppermute x9 -> x6, starting transfers between devices: 23.1 us -> 14.9 us  [from_chips(): lax.ppermute(values, 'line', [(i, (i + 2 * back) % NL) for i in range(NL)])]
    ppermute x7 -> x10, starting transfers between devices: 11.2 us -> 15.1 us  [to_ring(): return lax.ppermute(values, 'dp', pairs)]
    ppermute x9 -> x6, waiting for transfers between devices: 19 us -> 16.4 us  [from_chips(): lax.ppermute(values, 'line', [(i, (i + 2 * back) % NL) for i in range(NL)])]
    unnamed x14 -> x12, local copies, waits for them, and re-layouts: 3.2 us -> 0.7 us
    ppermute x7 -> x10, waiting for transfers between devices: 8.16 us -> 10.2 us  [to_ring(): return lax.ppermute(values, 'dp', pairs)]
where the time goes in v4:
time: 121 us
  starting transfers between devices  45.6 us (38%)
  Pallas kernels  40.1 us (33%)
  waiting for transfers between devices  33.4 us (28%)
    ppermute x6, waiting for transfers between devices, from_chips(): lax.ppermute(values, 'line', [(i, (i + 2 * back) % NL) for i in range(NL)])  16.4 us
    ppermute x9, starting transfers between devices, swap(): return lax.ppermute(values, 'line', [(i, i ^ 1) for i in range(NL)])  15.6 us
    ppermute x10, starting transfers between devices, to_ring(): return lax.ppermute(values, 'dp', pairs)  15.1 us
    ppermute x6, starting transfers between devices, from_chips(): lax.ppermute(values, 'line', [(i, (i + 2 * back) % NL) for i in range(NL)])  14.9 us
    pallas_call x1, Pallas kernels, block(): call(turn_kernel, (moving, moving, quarter, quarter, sums), 11, scratch=(...  10.7 us
    ppermute x10, waiting for transfers between devices, to_ring(): return lax.ppermute(values, 'dp', pairs)  10.2 us
    pallas_call x1, Pallas kernels, block(): call(functools.partial(forward_kernel, 0), (*tables, moving, moving, *sta...  7.06 us
    pallas_call x1, Pallas kernels, block(): call(functools.partial(forward_kernel, 1), (moving, moving, *state), 7, s...  7.03 us
  transfers between devices with their start and end apart: 25, of which 17 were waited for; matrix products, arithmetic and copies ran while one was open for 0% of the time, Pallas kernels for 0%

profile of v4, /device:TPU:1, one launch (start us, length us, event | category | flops | bytes accessed | tf_op | source)
XLA Modules:
  0.0 120.6 jit_solution(13285415895761973667)
XLA Ops:
  0.6 1.8 %shard_map.110 = (bf16[4,64,128]{2,1,0:T(8,128)(2,1)}, bf16[4,64,128]{2,1,0:T(8,128)(2,1)}, bf16[8,64,128]{2,1,0:T(8,128)(2,1)}, bf16[48,128]{1,0:T(8,128)(2,1)}) custom-call(bf16[1,512,128]{2,1,0:T(8,128)(2,1)} %fields_ref.1, bf16[1,512,128]{2,1,0:T(8,128)(2,1)} %cot_ref.1, s32[3,512]{1,0:T(4,128)} %table_ref.1, s32[3,4]{1,0:T(4,128)} %begin_ref.1), custom_call_target="tpu_custom_call" | custom-call | tf_op jit(solution)/shard_map/pallas_call | solution.py:461
  2.4 3.3 %collective-permute-start = (bf16[8,64,128]{2,1,0:T(8,128)(2,1)}, bf16[8,64,128]{2,1,0:T(8,128)(2,1)S(1)}, u32[]{:S(2)}, u32[]{:S(2)}) collective-permute-start(bf16[8,64,128]{2,1,0:T(8,128)(2,1)} %get-tuple-element.37), channel_id=1, source_target_pairs={{0,32},{32,0},{64,96},{96,64},{128,160},{160,128},{192,224},{224,1... | collective-permute-start | bytes 393224 | tf_op jit(solution)/shard_map/ppermute | solution.py:420
  7.6 4.4 %collective-permute-start.3 = (bf16[560,128]{1,0:T(8,128)(2,1)S(1)}, bf16[560,128]{1,0:T(8,128)(2,1)S(1)}, u32[]{:S(2)}, u32[]{:S(2)}) collective-permute-start(bf16[560,128]{1,0:T(8,128)(2,1)S(1)} %pad_maximum_fusion.refs_0_), channel_id=1, source_target_pairs={{0,192},{32,224},{64,0},{96,32},{128,64},{160,96},{192,128},{224,1... | collective-permute-start | bytes 430088 | tf_op jit(solution)/shard_map/ppermute | solution.py:425
  13.0 2.3 %collective-permute-start.1 = (bf16[560,128]{1,0:T(8,128)(2,1)S(1)}, bf16[560,128]{1,0:T(8,128)(2,1)S(1)}, u32[]{:S(2)}, u32[]{:S(2)}) collective-permute-start(bf16[560,128]{1,0:T(8,128)(2,1)S(1)} %pad_maximum_fusion.refs_0_), channel_id=1, source_target_pairs={{0,64},{32,96},{64,128},{96,160},{128,192},{160,224},{192,0},{224,... | collective-permute-start | bytes 430088 | tf_op jit(solution)/shard_map/ppermute | solution.py:425
  15.3 3.4 %collective-permute-done.3.refs_3_ = bf16[560,128]{1,0:T(8,128)(2,1)S(1)} collective-permute-done((bf16[560,128]{1,0:T(8,128)(2,1)S(1)}, bf16[560,128]{1,0:T(8,128)(2,1)S(1)}, u32[]{:S(2)}, u32[]{:S(2)}) %collective-permute-start.3) | collective-permute-done | bytes 143392 | tf_op jit(solution)/shard_map/ppermute | solution.py:425
  18.7 5.4 %collective-permute-done.2.refs_2_ = bf16[560,128]{1,0:T(8,128)(2,1)S(1)} collective-permute-done((bf16[560,128]{1,0:T(8,128)(2,1)S(1)}, bf16[560,128]{1,0:T(8,128)(2,1)S(1)}, u32[]{:S(2)}, u32[]{:S(2)}) %collective-permute-start.2) | collective-permute-done | bytes 143392 | tf_op jit(solution)/shard_map/ppermute | solution.py:425
  24.1 7.1 %shard_map.111 = (s32[3,4,1,512]{3,2,1,0:T(1,128)S(1)}, f32[3,4,4,128]{3,2,1,0:T(4,128)S(1)}, bf16[4,4,64,128]{3,2,1,0:T(8,128)(2,1)S(1)}, bf16[4,4,64,128]{3,2,...) custom-call(bf16[560,128]{1,0:T(8,128)(2,1)S(1)} %pad_maximum_fusion.refs_0_, ...), custom_call_target="tpu_custom_call" | custom-call | tf_op jit(solution)/shard_map/pallas_call | solution.py:474
  31.2 2.5 %collective-permute-start.4 = (bf16[4,4,64,128]{3,2,1,0:T(8,128)(2,1)S(1)}, bf16[4,4,64,128]{3,2,1,0:T(8,128)(2,1)S(1)}, u32[]{:S(2)}, u32[]{:S(2)}) collective-permute-start(bf16[4,4,64,128]{3,2,1,0:T(8,128)(2,1)S(1)} %get-tuple-element.40), channel_id=1, source_target_pairs={{0,32},{32,0},{64,96},{96,64},{128,160},{160,128},{192,224},{224,1... | collective-permute-start | bytes 786440 | tf_op jit(solution)/shard_map/ppermute | solution.py:420
  34.8 7.0 %shard_map.112 = (bf16[4,4,64,128]{3,2,1,0:T(8,128)(2,1)S(1)}, bf16[4,4,64,128]{3,2,1,0:T(8,128)(2,1)S(1)}, bf16[4,4,128,128]{3,2,1,0:T(8,128)(2,1)S(1)}, f32[4,4,128,128]{3,2,1,0:T(8,128)S(1)}) custom-call(bf16[4,4,64,128]{3,2,1,0:T(8,128)(2,1)S(1)} %get-tuple-element.39.refs_0_, bf16[4,4,64,128]{3,2,1,0:T(8,128)(2,1)S(1)} %collective-permute-done.4.refs_1_, ...), custom_call_target="tpu_custom_call" | custom-call | tf_op jit(solution)/shard_map/pallas_call | solution.py:478
  42.3 3.4 %collective-permute-start.8 = (bf16[512,128]{1,0:T(8,128)(2,1)S(1)}, bf16[512,128]{1,0:T(8,128)(2,1)S(1)}, u32[]{:S(2)}, u32[]{:S(2)}) collective-permute-start(bf16[512,128]{1,0:T(8,128)(2,1)S(1)} %pad_maximum_fusion.1.refs_2_), channel_id=1, source_target_pairs={{0,192},{32,224},{64,0},{96,32},{128,64},{160,96},{192,128},{224,1... | collective-permute-start | bytes 393224 | tf_op jit(solution)/shard_map/ppermute | solution.py:425
  45.7 1.8 %collective-permute-start.7 = (bf16[512,128]{1,0:T(8,128)(2,1)S(1)}, bf16[512,128]{1,0:T(8,128)(2,1)S(1)}, u32[]{:S(2)}, u32[]{:S(2)}) collective-permute-start(bf16[512,128]{1,0:T(8,128)(2,1)S(1)} %pad_maximum_fusion.1.refs_2_), channel_id=1, source_target_pairs={{0,128},{32,160},{64,192},{96,224},{128,0},{160,32},{192,64},{224,... | collective-permute-start | bytes 393224 | tf_op jit(solution)/shard_map/ppermute | solution.py:425
  47.5 2.0 %collective-permute-start.6 = (bf16[512,128]{1,0:T(8,128)(2,1)S(1)}, bf16[512,128]{1,0:T(8,128)(2,1)S(1)}, u32[]{:S(2)}, u32[]{:S(2)}) collective-permute-start(bf16[512,128]{1,0:T(8,128)(2,1)S(1)} %pad_maximum_fusion.1.refs_2_), channel_id=1, source_target_pairs={{0,64},{32,96},{64,128},{96,160},{128,192},{160,224},{192,0},{224,... | collective-permute-start | bytes 393224 | tf_op jit(solution)/shard_map/ppermute | solution.py:425
  49.6 7.1 %collective-permute-done.7.refs_4_ = bf16[512,128]{1,0:T(8,128)(2,1)S(1)} collective-permute-done((bf16[512,128]{1,0:T(8,128)(2,1)S(1)}, bf16[512,128]{1,0:T(8,128)(2,1)S(1)}, u32[]{:S(2)}, u32[]{:S(2)}) %collective-permute-start.7) | collective-permute-done | bytes 131104 | tf_op jit(solution)/shard_map/ppermute | solution.py:425
  57.2 10.7 %shard_map.113 = (bf16[4,4,64,128]{3,2,1,0:T(8,128)(2,1)S(1)}, bf16[4,4,64,128]{3,2,1,0:T(8,128)(2,1)S(1)}, bf16[4,64,128]{2,1,0:T(8,128)(2,1)S(1)}, bf16[4,64,128]{2,1,0:T(8,128)(2,1)S(1)}, f32[144,128]{1,0:T(8,128)S(1)}) custom-call(bf16[4,4,64,128]{3,2,1,0:T(8,128)(2,1)S(1)} %get-tuple-element.43.refs_0_, ...), custom_call_target="tpu_custom_call" | custom-call | tf_op jit(solution)/shard_map/pallas_call | solution.py:481
  67.9 2.2 %collective-permute-start.9 = (bf16[4,4,64,128]{3,2,1,0:T(8,128)(2,1)S(1)}, bf16[4,4,64,128]{3,2,1,0:T(8,128)(2,1)S(1)}, u32[]{:S(2)}, u32[]{:S(2)}) collective-permute-start(bf16[4,4,64,128]{3,2,1,0:T(8,128)(2,1)S(1)} %get-tuple-element.47), channel_id=1, source_target_pairs={{0,32},{32,0},{64,96},{96,64},{128,160},{160,128},{192,224},{224,1... | collective-permute-start | bytes 786440 | tf_op jit(solution)/shard_map/ppermute | solution.py:420
  71.3 6.2 %shard_map.114 = (bf16[4,4,64,128]{3,2,1,0:T(8,128)(2,1)S(1)}, bf16[4,4,64,128]{3,2,1,0:T(8,128)(2,1)S(1)}, f32[144,128]{1,0:T(8,128)S(1)}) custom-call(bf16[4,4,64,128]{3,2,1,0:T(8,128)(2,1)S(1)} %get-tuple-element.46.refs_0_, bf16[4,4,64,128]{3,2,1,0:T(8,128)(2,1)S(1)} %collective-permute-done.9.refs_1_, ...), custom_call_target="tpu_custom_call" | custom-call | tf_op jit(solution)/shard_map/pallas_call | solution.py:486
  79.2 6.5 %shard_map.115 = (bf16[1,512,128]{2,1,0:T(8,128)(2,1)}, bf16[4,64,128]{2,1,0:T(8,128)(2,1)S(1)}, bf16[4,64,128]{2,1,0:T(8,128)(2,1)S(1)}, f32[4,56,128]{2,1,0:T(8,128)S(1)}, f32[4,56,128]{2,1,0:T(8,128)S(1)}) custom-call(bf16[4,4,64,128]{3,2,1,0:T(8,128)(2,1)S(1)} %get-tuple-element.50.refs_0_, bf16[4,4,64,128]{3,2,1,0:T(8,128)(2,1)S(1)} %collective-permute-done.10.refs_1_, ...), custom_call_target="tpu_custom_call" | custom-call | tf_op jit(solution)/shard_map/pallas_call | solution.py:490
  88.6 2.6 %collective-permute-start.15 = (f32[56,128]{1,0:T(8,128)S(1)}, f32[56,128]{1,0:T(8,128)S(1)}, u32[]{:S(2)}, u32[]{:S(2)}) collective-permute-start(f32[56,128]{1,0:T(8,128)S(1)} %get-tuple-element.70), channel_id=1, source_target_pairs={{0,2},{1,3},{2,0},{3,1},{4,6},{5,7},{6,4},{7,5},{8,10},{9,11},{10,... | collective-permute-start | bytes 86024 | tf_op jit(solution)/shard_map/ppermute | solution.py:436
  94.2 2.5 %collective-permute-start.18 = (f32[56,128]{1,0:T(8,128)S(1)}, f32[56,128]{1,0:T(8,128)S(1)}, u32[]{:S(2)}, u32[]{:S(2)}) collective-permute-start(f32[56,128]{1,0:T(8,128)S(1)} %fusion.2), channel_id=1, source_target_pairs={{0,12},{1,13},{2,14},{3,15},{4,0},{5,1},{6,2},{7,3},{8,4},{9,5},{1... | collective-permute-start | bytes 86024 | tf_op jit(solution)/shard_map/ppermute | solution.py:436
  97.9 3.1 %collective-permute-done.17 = f32[56,128]{1,0:T(8,128)S(1)} collective-permute-done((f32[56,128]{1,0:T(8,128)S(1)}, f32[56,128]{1,0:T(8,128)S(1)}, u32[]{:S(2)}, u32[]{:S(2)}) %collective-permute-start.17) | collective-permute-done | bytes 28704 | tf_op jit(solution)/shard_map/ppermute | solution.py:436
  101.3 3.7 %collective-permute-start.19 = (f32[56,128]{1,0:T(8,128)S(1)}, f32[56,128]{1,0:T(8,128)S(1)}, u32[]{:S(2)}, u32[]{:S(2)}) collective-permute-start(f32[56,128]{1,0:T(8,128)S(1)} %add_add_fusion), channel_id=1, source_target_pairs={{0,16},{1,17},{2,18},{3,19},{4,20},{5,21},{6,22},{7,23},{8,24},{9,... | collective-permute-start | bytes 86024 | tf_op jit(solution)/shard_map/ppermute | solution.py:436
  106.2 2.0 %collective-permute-start.22 = (f32[56,128]{1,0:T(8,128)S(1)}, f32[56,128]{1,0:T(8,128)S(1)}, u32[]{:S(2)}, u32[]{:S(2)}) collective-permute-start(f32[56,128]{1,0:T(8,128)S(1)} %add_multiply_fusion), channel_id=1, source_target_pairs={{0,3},{1,0},{2,1},{3,2},{4,7},{5,4},{6,5},{7,6},{8,11},{9,8},{10,9... | collective-permute-start | bytes 86024 | tf_op jit(solution)/shard_map/ppermute | solution.py:436
  109.2 3.3 %collective-permute-done.21 = f32[56,128]{1,0:T(8,128)S(1)} collective-permute-done((f32[56,128]{1,0:T(8,128)S(1)}, f32[56,128]{1,0:T(8,128)S(1)}, u32[]{:S(2)}, u32[]{:S(2)}) %collective-permute-start.21) | collective-permute-done | bytes 28704 | tf_op jit(solution)/shard_map/ppermute | solution.py:436
  112.5 6.1 %collective-permute-start.23 = (f32[4,56,128]{2,1,0:T(8,128)S(1)}, f32[4,56,128]{2,1,0:T(8,128)S(1)}, u32[]{:S(2)}, u32[]{:S(2)}) collective-permute-start(f32[4,56,128]{2,1,0:T(8,128)S(1)} %pad_maximum_fusion.2.own_ref), channel_id=1, source_target_pairs={{0,32},{32,0},{64,96},{96,64},{128,160},{160,128},{192,224},{224,1... | collective-permute-start | bytes 344072 | tf_op jit(solution)/shard_map/ppermute | solution.py:420
  (54 shorter events, 19.5 us)
Async XLA Ops:
  2.4 4.5 %collective-permute-start = (bf16[8,64,128]{2,1,0:T(8,128)(2,1)}, bf16[8,64,128]{2,1,0:T(8,128)(2,1)S(1)}, u32[]{:S(2)}, u32[]{:S(2)}) collective-permute-start(bf16[8,64,128]{2,1,0:T(8,128)(2,1)} %get-tuple-element.37), channel_id=1, source_target_pairs={{0,32},{32,0},{64,96},{96,64},{128,160},{160,128},{192,224},{224,1... | collective-permute-start | bytes 393224 | tf_op jit(solution)/shard_map/ppermute | solution.py:420
  7.6 11.0 %collective-permute-start.3 = (bf16[560,128]{1,0:T(8,128)(2,1)S(1)}, bf16[560,128]{1,0:T(8,128)(2,1)S(1)}, u32[]{:S(2)}, u32[]{:S(2)}) collective-permute-start(bf16[560,128]{1,0:T(8,128)(2,1)S(1)} %pad_maximum_fusion.refs_0_), channel_id=1, source_target_pairs={{0,192},{32,224},{64,0},{96,32},{128,64},{160,96},{192,128},{224,1... | collective-permute-start | bytes 430088 | tf_op jit(solution)/shard_map/ppermute | solution.py:425
  12.0 12.1 %collective-permute-start.2 = (bf16[560,128]{1,0:T(8,128)(2,1)S(1)}, bf16[560,128]{1,0:T(8,128)(2,1)S(1)}, u32[]{:S(2)}, u32[]{:S(2)}) collective-permute-start(bf16[560,128]{1,0:T(8,128)(2,1)S(1)} %pad_maximum_fusion.refs_0_), channel_id=1, source_target_pairs={{0,128},{32,160},{64,192},{96,224},{128,0},{160,32},{192,64},{224,... | collective-permute-start | bytes 430088 | tf_op jit(solution)/shard_map/ppermute | solution.py:425
  13.0 11.1 %collective-permute-start.1 = (bf16[560,128]{1,0:T(8,128)(2,1)S(1)}, bf16[560,128]{1,0:T(8,128)(2,1)S(1)}, u32[]{:S(2)}, u32[]{:S(2)}) collective-permute-start(bf16[560,128]{1,0:T(8,128)(2,1)S(1)} %pad_maximum_fusion.refs_0_), channel_id=1, source_target_pairs={{0,64},{32,96},{64,128},{96,160},{128,192},{160,224},{192,0},{224,... | collective-permute-start | bytes 430088 | tf_op jit(solution)/shard_map/ppermute | solution.py:425
  31.2 3.6 %collective-permute-start.4 = (bf16[4,4,64,128]{3,2,1,0:T(8,128)(2,1)S(1)}, bf16[4,4,64,128]{3,2,1,0:T(8,128)(2,1)S(1)}, u32[]{:S(2)}, u32[]{:S(2)}) collective-permute-start(bf16[4,4,64,128]{3,2,1,0:T(8,128)(2,1)S(1)} %get-tuple-element.40), channel_id=1, source_target_pairs={{0,32},{32,0},{64,96},{96,64},{128,160},{160,128},{192,224},{224,1... | collective-permute-start | bytes 786440 | tf_op jit(solution)/shard_map/ppermute | solution.py:420
  41.8 15.3 %collective-permute-start.5 = (bf16[4,4,64,128]{3,2,1,0:T(8,128)(2,1)S(1)}, bf16[4,4,64,128]{3,2,1,0:T(8,128)(2,1)S(1)}, u32[]{:S(2)}, u32[]{:S(2)}) collective-permute-start(bf16[4,4,64,128]{3,2,1,0:T(8,128)(2,1)S(1)} %get-tuple-element.44), channel_id=1, source_target_pairs={{0,32},{32,0},{64,96},{96,64},{128,160},{160,128},{192,224},{224,1... | collective-permute-start | bytes 786440 | tf_op jit(solution)/shard_map/ppermute | solution.py:420
  42.3 7.2 %collective-permute-start.8 = (bf16[512,128]{1,0:T(8,128)(2,1)S(1)}, bf16[512,128]{1,0:T(8,128)(2,1)S(1)}, u32[]{:S(2)}, u32[]{:S(2)}) collective-permute-start(bf16[512,128]{1,0:T(8,128)(2,1)S(1)} %pad_maximum_fusion.1.refs_2_), channel_id=1, source_target_pairs={{0,192},{32,224},{64,0},{96,32},{128,64},{160,96},{192,128},{224,1... | collective-permute-start | bytes 393224 | tf_op jit(solution)/shard_map/ppermute | solution.py:425
  45.7 10.9 %collective-permute-start.7 = (bf16[512,128]{1,0:T(8,128)(2,1)S(1)}, bf16[512,128]{1,0:T(8,128)(2,1)S(1)}, u32[]{:S(2)}, u32[]{:S(2)}) collective-permute-start(bf16[512,128]{1,0:T(8,128)(2,1)S(1)} %pad_maximum_fusion.1.refs_2_), channel_id=1, source_target_pairs={{0,128},{32,160},{64,192},{96,224},{128,0},{160,32},{192,64},{224,... | collective-permute-start | bytes 393224 | tf_op jit(solution)/shard_map/ppermute | solution.py:425
  47.5 9.6 %collective-permute-start.6 = (bf16[512,128]{1,0:T(8,128)(2,1)S(1)}, bf16[512,128]{1,0:T(8,128)(2,1)S(1)}, u32[]{:S(2)}, u32[]{:S(2)}) collective-permute-start(bf16[512,128]{1,0:T(8,128)(2,1)S(1)} %pad_maximum_fusion.1.refs_2_), channel_id=1, source_target_pairs={{0,64},{32,96},{64,128},{96,160},{128,192},{160,224},{192,0},{224,... | collective-permute-start | bytes 393224 | tf_op jit(solution)/shard_map/ppermute | solution.py:425
  67.9 3.4 %collective-permute-start.9 = (bf16[4,4,64,128]{3,2,1,0:T(8,128)(2,1)S(1)}, bf16[4,4,64,128]{3,2,1,0:T(8,128)(2,1)S(1)}, u32[]{:S(2)}, u32[]{:S(2)}) collective-permute-start(bf16[4,4,64,128]{3,2,1,0:T(8,128)(2,1)S(1)} %get-tuple-element.47), channel_id=1, source_target_pairs={{0,32},{32,0},{64,96},{96,64},{128,160},{160,128},{192,224},{224,1... | collective-permute-start | bytes 786440 | tf_op jit(solution)/shard_map/ppermute | solution.py:420
  77.5 1.7 %collective-permute-start.10 = (bf16[4,4,64,128]{3,2,1,0:T(8,128)(2,1)S(1)}, bf16[4,4,64,128]{3,2,1,0:T(8,128)(2,1)S(1)}, u32[]{:S(2)}, u32[]{:S(2)}) collective-permute-start(bf16[4,4,64,128]{3,2,1,0:T(8,128)(2,1)S(1)} %get-tuple-element.51), channel_id=1, source_target_pairs={{0,32},{32,0},{64,96},{96,64},{128,160},{160,128},{192,224},{224,1... | collective-permute-start | bytes 786440 | tf_op jit(solution)/shard_map/ppermute | solution.py:420
  78.0 1.3 %collective-permute-start.11 = (bf16[4,64,128]{2,1,0:T(8,128)(2,1)S(1)}, bf16[4,64,128]{2,1,0:T(8,128)(2,1)S(1)}, u32[]{:S(2)}, u32[]{:S(2)}) collective-permute-start(bf16[4,64,128]{2,1,0:T(8,128)(2,1)S(1)} %get-tuple-element.57), channel_id=1, source_target_pairs={{0,32},{32,0},{64,96},{96,64},{128,160},{160,128},{192,224},{224,1... | collective-permute-start | bytes 196616 | tf_op jit(solution)/shard_map/ppermute | solution.py:420
  85.8 1.3 %collective-permute-start.12 = (f32[4,56,128]{2,1,0:T(8,128)S(1)}, f32[4,56,128]{2,1,0:T(8,128)S(1)}, u32[]{:S(2)}, u32[]{:S(2)}) collective-permute-start(f32[4,56,128]{2,1,0:T(8,128)S(1)} %get-tuple-element.60), channel_id=1, source_target_pairs={{0,32},{32,0},{64,96},{96,64},{128,160},{160,128},{192,224},{224,1... | collective-permute-start | bytes 344072 | tf_op jit(solution)/shard_map/ppermute | solution.py:420
  87.2 5.1 %collective-permute-start.13 = (f32[56,128]{1,0:T(8,128)S(1)}, f32[56,128]{1,0:T(8,128)S(1)}, u32[]{:S(2)}, u32[]{:S(2)}) collective-permute-start(f32[56,128]{1,0:T(8,128)S(1)} %get-tuple-element.69), channel_id=1, source_target_pairs={{0,1},{1,2},{2,3},{3,0},{4,5},{5,6},{6,7},{7,4},{8,9},{9,10},{10,1... | collective-permute-start | bytes 86024 | tf_op jit(solution)/shard_map/ppermute | solution.py:436
  88.6 4.2 %collective-permute-start.15 = (f32[56,128]{1,0:T(8,128)S(1)}, f32[56,128]{1,0:T(8,128)S(1)}, u32[]{:S(2)}, u32[]{:S(2)}) collective-permute-start(f32[56,128]{1,0:T(8,128)S(1)} %get-tuple-element.70), channel_id=1, source_target_pairs={{0,2},{1,3},{2,0},{3,1},{4,6},{5,7},{6,4},{7,5},{8,10},{9,11},{10,... | collective-permute-start | bytes 86024 | tf_op jit(solution)/shard_map/ppermute | solution.py:436
  91.2 3.0 %collective-permute-start.14 = (f32[56,128]{1,0:T(8,128)S(1)}, f32[56,128]{1,0:T(8,128)S(1)}, u32[]{:S(2)}, u32[]{:S(2)}) collective-permute-start(f32[56,128]{1,0:T(8,128)S(1)} %get-tuple-element.71), channel_id=1, source_target_pairs={{0,3},{1,0},{2,1},{3,2},{4,7},{5,4},{6,5},{7,6},{8,11},{9,8},{10,9... | collective-permute-start | bytes 86024 | tf_op jit(solution)/shard_map/ppermute | solution.py:436
  94.2 3.7 %collective-permute-start.18 = (f32[56,128]{1,0:T(8,128)S(1)}, f32[56,128]{1,0:T(8,128)S(1)}, u32[]{:S(2)}, u32[]{:S(2)}) collective-permute-start(f32[56,128]{1,0:T(8,128)S(1)} %fusion.2), channel_id=1, source_target_pairs={{0,12},{1,13},{2,14},{3,15},{4,0},{5,1},{6,2},{7,3},{8,4},{9,5},{1... | collective-permute-start | bytes 86024 | tf_op jit(solution)/shard_map/ppermute | solution.py:436
  96.7 4.2 %collective-permute-start.17 = (f32[56,128]{1,0:T(8,128)S(1)}, f32[56,128]{1,0:T(8,128)S(1)}, u32[]{:S(2)}, u32[]{:S(2)}) collective-permute-start(f32[56,128]{1,0:T(8,128)S(1)} %fusion.2), channel_id=1, source_target_pairs={{0,8},{1,9},{2,10},{3,11},{4,12},{5,13},{6,14},{7,15},{8,0},{9,1},... | collective-permute-start | bytes 86024 | tf_op jit(solution)/shard_map/ppermute | solution.py:436
  97.3 4.0 %collective-permute-start.16 = (f32[56,128]{1,0:T(8,128)S(1)}, f32[56,128]{1,0:T(8,128)S(1)}, u32[]{:S(2)}, u32[]{:S(2)}) collective-permute-start(f32[56,128]{1,0:T(8,128)S(1)} %fusion.2), channel_id=1, source_target_pairs={{0,4},{1,5},{2,6},{3,7},{4,8},{5,9},{6,10},{7,11},{8,12},{9,13},{1... | collective-permute-start | bytes 86024 | tf_op jit(solution)/shard_map/ppermute | solution.py:436
  101.3 5.0 %collective-permute-start.19 = (f32[56,128]{1,0:T(8,128)S(1)}, f32[56,128]{1,0:T(8,128)S(1)}, u32[]{:S(2)}, u32[]{:S(2)}) collective-permute-start(f32[56,128]{1,0:T(8,128)S(1)} %add_add_fusion), channel_id=1, source_target_pairs={{0,16},{1,17},{2,18},{3,19},{4,20},{5,21},{6,22},{7,23},{8,24},{9,... | collective-permute-start | bytes 86024 | tf_op jit(solution)/shard_map/ppermute | solution.py:436
  106.2 3.0 %collective-permute-start.22 = (f32[56,128]{1,0:T(8,128)S(1)}, f32[56,128]{1,0:T(8,128)S(1)}, u32[]{:S(2)}, u32[]{:S(2)}) collective-permute-start(f32[56,128]{1,0:T(8,128)S(1)} %add_multiply_fusion), channel_id=1, source_target_pairs={{0,3},{1,0},{2,1},{3,2},{4,7},{5,4},{6,5},{7,6},{8,11},{9,8},{10,9... | collective-permute-start | bytes 86024 | tf_op jit(solution)/shard_map/ppermute | solution.py:436
  108.2 4.2 %collective-permute-start.21 = (f32[56,128]{1,0:T(8,128)S(1)}, f32[56,128]{1,0:T(8,128)S(1)}, u32[]{:S(2)}, u32[]{:S(2)}) collective-permute-start(f32[56,128]{1,0:T(8,128)S(1)} %add_multiply_fusion), channel_id=1, source_target_pairs={{0,2},{1,3},{2,0},{3,1},{4,6},{5,7},{6,4},{7,5},{8,10},{9,11},{10,... | collective-permute-start | bytes 86024 | tf_op jit(solution)/shard_map/ppermute | solution.py:436
  108.3 4.2 %collective-permute-start.20 = (f32[56,128]{1,0:T(8,128)S(1)}, f32[56,128]{1,0:T(8,128)S(1)}, u32[]{:S(2)}, u32[]{:S(2)}) collective-permute-start(f32[56,128]{1,0:T(8,128)S(1)} %add_multiply_fusion), channel_id=1, source_target_pairs={{0,1},{1,2},{2,3},{3,0},{4,5},{5,6},{6,7},{7,4},{8,9},{9,10},{10,1... | collective-permute-start | bytes 86024 | tf_op jit(solution)/shard_map/ppermute | solution.py:436
  112.5 7.3 %collective-permute-start.23 = (f32[4,56,128]{2,1,0:T(8,128)S(1)}, f32[4,56,128]{2,1,0:T(8,128)S(1)}, u32[]{:S(2)}, u32[]{:S(2)}) collective-permute-start(f32[4,56,128]{2,1,0:T(8,128)S(1)} %pad_maximum_fusion.2.own_ref), channel_id=1, source_target_pairs={{0,32},{32,0},{64,96},{96,64},{128,160},{160,128},{192,224},{224,1... | collective-permute-start | bytes 344072 | tf_op jit(solution)/shard_map/ppermute | solution.py:420
  (7 other events, 63.4 us)

commit v5 on v4

--- a/solution.py
+++ b/solution.py
@@ -15,6 +15,7 @@
 NL = 8
 CHIPS = NL // 2
 RING = 4
+GROUP = 2
 Q = CELLS // NL
 HALF = CELLS // 2
 LINES = CELLS // LINE
@@ -117,9 +118,9 @@
 
 
 def clear(pads):
-    for line in range(LINES):
-        pads[line, 0:8, :] = jnp.zeros((8, CH), F32)
-        pads[line, 8 + LINE : 16 + LINE, :] = jnp.zeros((8, CH), F32)
+    edge = jnp.zeros((GROUP, LINES, 8, CH), F32)
+    pads[:, :, 0:8, :] = edge
+    pads[:, :, 8 + LINE : 16 + LINE, :] = edge
 
 
 def norm(x, gain, start):
@@ -142,48 +143,61 @@
     return 1.0 / (1.0 + jnp.exp(-h))
 
 
-def forward_line(k, x, start, gain_ref, taps_ref, mix_ref, pad):
-    inverse, scaled, masked, keep = norm(x, gain_ref[k : k + 1, :], start)
-    hidden = conv(pad, masked, taps_ref[k])
-    gate = sigmoid(hidden)
-    active = (hidden * gate).astype(BF16)
-    mixed = dot(active, mix_ref[k], 1, 0).astype(BF16).astype(F32)
-    after = (x + mixed).astype(BF16)
-    return (inverse, scaled, masked, keep, hidden, gate, active), after
-
-
-def backward_line(k, grad, state, gain_ref, taps_ref, mix_ref, pad, sums):
-    inverse, scaled, masked, keep, hidden, gate, active = state
+def gather_stage(row, received, out):
+    for line in range(LINES):
+        out[line] = dot(picks(row, line), received, 1, 0).astype(BF16)
+
+
+def hidden_stage(k, x_at, start_at, h_at, active, gain_ref, taps_ref, pads, line):
+    x = x_at[line].astype(F32)
+    masked = norm(x, gain_ref[k : k + 1, :], start_at[line : line + 1, :])[2]
+    hidden = conv(pads.at[line], masked, taps_ref[k])
+    h_at[line] = hidden
+    active[line] = (hidden * sigmoid(hidden)).astype(BF16)
+
+
+def mix_stage(k, x_at, active, mix_ref):
+    mixed = dot(active[...].reshape(CELLS, CH), mix_ref[k], 1, 0).astype(BF16).astype(F32)
+    return (x_at[...].reshape(CELLS, CH).astype(F32) + mixed).astype(BF16)
+
+
+def activity_stage(h_at, active):
+    for line in range(LINES):
+        hidden = h_at[line]
+        active[line] = (hidden * sigmoid(hidden)).astype(BF16)
+
+
+def slope_stage(k, grad_at, h_at, slope_at, mix_ref):
+    grad_act = dot(grad_at[...].reshape(CELLS, CH), mix_ref[k], 1, 1).reshape(LINES, LINE, CH)
+    for line in range(LINES):
+        hidden = h_at[line]
+        gate = sigmoid(hidden)
+        slope_at[line] = (grad_act[line] * (gate * (1.0 + hidden * (1.0 - gate)))).astype(BF16)
+
+
+def backward_line(k, grad_at, x_at, start_at, slope_at, gain_ref, taps_ref, pads, line, sums):
     gain = gain_ref[k : k + 1, :]
     taps = taps_ref[k]
-    sums["active"].append(active)
-    sums["grad"].append(grad)
-    grad_act = dot(grad, mix_ref[k], 1, 1)
-    grad_hidden = (grad_act * (gate * (1.0 + hidden * (1.0 - gate)))).astype(BF16).astype(F32)
+    inverse, scaled, masked, keep = norm(x_at[line].astype(F32), gain, start_at[line : line + 1, :])
     total = None
-    for t, (first, moved) in enumerate(shifts(pad, grad_hidden)):
+    for t, (first, moved) in enumerate(shifts(pads.at[line], slope_at[line].astype(F32))):
         u = t if t == 0 else (t + 1 if t % 2 else t - 1)
         size = moved.shape[0]
         term = taps[u : u + 1, :] * moved
         total = term if total is None else accumulate(total, first, term)
         part = jnp.sum((moved * masked[first : first + size]).reshape(size // 8, 8, CH), axis=0)
-        sums["rows"][u] = part if sums["rows"][u] is None else sums["rows"][u] + part
+        sums[u] = part if sums[u] is None else sums[u] + part
     cells = jnp.where(keep, total, 0.0).astype(BF16).astype(F32)
     part = jnp.sum((cells * scaled).reshape(LINE // 8, 8, CH), axis=0)
-    sums["rows"][TAPS] = part if sums["rows"][TAPS] is None else sums["rows"][TAPS] + part
+    sums[TAPS] = part if sums[TAPS] is None else sums[TAPS] + part
     weighted = cells * gain
     moved = inverse * (weighted - scaled * jnp.mean(weighted * scaled, axis=-1, keepdims=True))
-    return (grad.astype(F32) + moved).astype(BF16)
-
-
-def new_sums():
-    return {"active": [], "grad": [], "rows": [None] * (TAPS + 1)}
-
-
-def add_sums(sum_ref, rows_ref, sums):
-    active = jnp.concatenate(sums["active"], axis=0)
-    sum_ref[0:CH, :] += dot(active, jnp.concatenate(sums["grad"], axis=0), 0, 0)
-    for t, part in enumerate(sums["rows"]):
+    return (grad_at[line].astype(F32) + moved).astype(BF16)
+
+
+def add_sums(sum_ref, rows_ref, active, grad_at, sums):
+    sum_ref[0:CH, :] += dot(active[...].reshape(CELLS, CH), grad_at[...].reshape(CELLS, CH), 0, 0)
+    for t, part in enumerate(sums):
         rows_ref[t] += part
 
 
@@ -257,30 +271,31 @@
 def forward_kernel(k, *refs):
     if k == 0:
         pieces, refs = refs[:CHIPS], refs[CHIPS:]
-        gain_ref, taps_ref, mix_ref, order_ref, starts_ref, same_ref, swap_ref, x_ref, h_ref, pad = refs
+        gain_ref, taps_ref, mix_ref, order_ref, starts_ref, same_ref, swap_ref, x_ref, h_ref, pad, active = refs
         read_tables(pieces, order_ref, starts_ref)
     else:
         (in_ref, in_swap_ref, gain_ref, taps_ref, mix_ref, order_ref, starts_ref) = refs[:7]
-        same_ref, swap_ref, x_ref, h_ref, pad = refs[7:]
+        same_ref, swap_ref, x_ref, h_ref, pad, active = refs[7:]
     clear(pad)
 
-    def holder(m, carry):
-        received = gathered_rows(pieces, m, k) if k == 0 else moved_rows(in_ref, in_swap_ref, m)
-        order = order_ref[k, m]
-        row = block_row(order, k == 0)
-        after = []
-        for line in range(LINES):
-            x = dot(picks(row, line), received, 1, 0)
-            state, new = forward_line(
-                k, x, starts_ref[k, m, line : line + 1, :], gain_ref, taps_ref, mix_ref, pad.at[line]
-            )
-            x_ref[m, line] = x.astype(BF16)
-            h_ref[m, line] = state[4]
-            after.append(new)
-        put_next(block_row(order, False), jnp.concatenate(after, axis=0), m, 1, same_ref, swap_ref)
+    def holders(i, carry):
+        ms = [i * GROUP + g for g in range(GROUP)]
+        rows = []
+        for m in ms:
+            received = gathered_rows(pieces, m, k) if k == 0 else moved_rows(in_ref, in_swap_ref, m)
+            rows.append(order_ref[k, m])
+            gather_stage(block_row(rows[-1], k == 0), received, x_ref.at[m])
+        for g, m in enumerate(ms):
+            for line in range(LINES):
+                hidden_stage(
+                    k, x_ref.at[m], starts_ref.at[k, m], h_ref.at[m], active.at[g], gain_ref, taps_ref, pad.at[g], line
+                )
+        after = [mix_stage(k, x_ref.at[m], active.at[g], mix_ref) for g, m in enumerate(ms)]
+        for g, m in enumerate(ms):
+            put_next(block_row(rows[g], False), after[g], m, 1, same_ref, swap_ref)
         return carry
 
-    lax.fori_loop(0, CHIPS, holder, 0)
+    lax.fori_loop(0, CHIPS // GROUP, holders, 0)
 
 
 def turn_kernel(*refs):
@@ -288,32 +303,41 @@
     in_ref, in_swap_ref = refs[:2]
     pieces = refs[2 : 2 + CHIPS]
     gain_ref, taps_ref, mix_ref, order_ref, starts_ref = refs[2 + CHIPS : 7 + CHIPS]
-    same_ref, swap_ref, own_ref, home_ref, sum_ref, pad, rows_ref = refs[7 + CHIPS :]
+    same_ref, swap_ref, own_ref, home_ref, sum_ref = refs[7 + CHIPS : 12 + CHIPS]
+    pad, rows_ref, active, x_ref, grad_ref, slope_ref, h_ref = refs[12 + CHIPS :]
     clear(pad)
     start_sums(sum_ref, rows_ref)
 
-    def holder(m, carry):
-        received = moved_rows(in_ref, in_swap_ref, m)
-        cot = gathered_rows(pieces, m, k)
-        order = order_ref[k, m]
-        row = block_row(order, False)
-        cot_row = block_row(order, True)
-        sums = new_sums()
-        after, grads = [], []
-        for line in range(LINES):
-            x = dot(picks(row, line), received, 1, 0)
-            state, new = forward_line(
-                k, x, starts_ref[k, m, line : line + 1, :], gain_ref, taps_ref, mix_ref, pad.at[line]
-            )
-            after.append(new)
-            grad = dot(picks(cot_row, line), cot, 1, 0).astype(BF16)
-            grads.append(backward_line(k, grad, state, gain_ref, taps_ref, mix_ref, pad.at[line], sums))
-        put_home(row, jnp.concatenate(after, axis=0), m, own_ref, home_ref)
-        put_next(row, jnp.concatenate(grads, axis=0), m, -1, same_ref, swap_ref)
-        add_sums(sum_ref, rows_ref, sums)
+    def holders(i, carry):
+        ms = [i * GROUP + g for g in range(GROUP)]
+        rows = []
+        for g, m in enumerate(ms):
+            order = order_ref[k, m]
+            rows.append(block_row(order, False))
+            gather_stage(rows[-1], moved_rows(in_ref, in_swap_ref, m), x_ref.at[g])
+            gather_stage(block_row(order, True), gathered_rows(pieces, m, k), grad_ref.at[g])
+        for g, m in enumerate(ms):
+            for line in range(LINES):
+                hidden_stage(
+                    k, x_ref.at[g], starts_ref.at[k, m], h_ref.at[g], active.at[g], gain_ref, taps_ref, pad.at[g], line
+                )
+        for g, m in enumerate(ms):
+            after = mix_stage(k, x_ref.at[g], active.at[g], mix_ref)
+            slope_stage(k, grad_ref.at[g], h_ref.at[g], slope_ref.at[g], mix_ref)
+            put_home(rows[g], after, m, own_ref, home_ref)
+        for g, m in enumerate(ms):
+            sums = [None] * (TAPS + 1)
+            grads = [
+                backward_line(
+                    k, grad_ref.at[g], x_ref.at[g], starts_ref.at[k, m], slope_ref.at[g], gain_ref, taps_ref, pad.at[g], line, sums
+                )
+                for line in range(LINES)
+            ]
+            add_sums(sum_ref, rows_ref, active.at[g], grad_ref.at[g], sums)
+            put_next(rows[g], jnp.concatenate(grads, axis=0), m, -1, same_ref, swap_ref)
         return carry
 
-    lax.fori_loop(0, CHIPS, holder, 0)
+    lax.fori_loop(0, CHIPS // GROUP, holders, 0)
     end_sums(sum_ref, rows_ref)
 
 
@@ -339,10 +363,11 @@
 def backward_kernel(k, *refs):
     in_ref, in_swap_ref, x_ref, h_ref, gain_ref, taps_ref, mix_ref, order_ref, starts_ref = refs[:9]
     if k == 1:
-        same_ref, swap_ref, sum_ref, pad, rows_ref = refs[9:]
+        same_ref, swap_ref, sum_ref, pad, rows_ref, active, grad_ref, slope_ref = refs[9:]
     else:
         sum1_ref, sum2_ref, first_ref, second_ref = refs[9:13]
-        imitated_ref, own_ref, home_ref, keep_ref, send_ref, pad, rows_ref, sum_ref, small_ref = refs[13:]
+        imitated_ref, own_ref, home_ref, keep_ref, send_ref = refs[13:18]
+        pad, rows_ref, active, grad_ref, slope_ref, sum_ref, small_ref = refs[18:]
         zone, core = place_of()
         for m in range(CHIPS):
             for ref, first in ((first_ref, 2 * m - core), (second_ref, 2 * m + 1 - 3 * core)):
@@ -351,28 +376,32 @@
     clear(pad)
     start_sums(sum_ref, rows_ref)
 
-    def holder(m, carry):
-        received = moved_rows(in_ref, in_swap_ref, m)
-        row = block_row(order_ref[k, m], False)
-        sums = new_sums()
-        grads = []
-        for line in range(LINES):
-            grad = dot(picks(row, line), received, 1, 0).astype(BF16)
-            hidden = h_ref[m, line]
-            inverse, scaled, masked, keep = norm(
-                x_ref[m, line].astype(F32), gain_ref[k : k + 1, :], starts_ref[k, m, line : line + 1, :]
-            )
-            gate = sigmoid(hidden)
-            state = (inverse, scaled, masked, keep, hidden, gate, (hidden * gate).astype(BF16))
-            grads.append(backward_line(k, grad, state, gain_ref, taps_ref, mix_ref, pad.at[line], sums))
-        if k == 1:
-            put_next(row, jnp.concatenate(grads, axis=0), m, -1, same_ref, swap_ref)
-        else:
-            put_home(row, jnp.concatenate(grads, axis=0), m, own_ref, home_ref)
-        add_sums(sum_ref, rows_ref, sums)
+    def holders(i, carry):
+        ms = [i * GROUP + g for g in range(GROUP)]
+        rows = []
+        for g, m in enumerate(ms):
+            rows.append(block_row(order_ref[k, m], False))
+            gather_stage(rows[-1], moved_rows(in_ref, in_swap_ref, m), grad_ref.at[g])
+        for g, m in enumerate(ms):
+            activity_stage(h_ref.at[m], active.at[g])
+            slope_stage(k, grad_ref.at[g], h_ref.at[m], slope_ref.at[g], mix_ref)
+        for g, m in enumerate(ms):
+            sums = [None] * (TAPS + 1)
+            grads = [
+                backward_line(
+                    k, grad_ref.at[g], x_ref.at[m], starts_ref.at[k, m], slope_ref.at[g], gain_ref, taps_ref, pad.at[g], line, sums
+                )
+                for line in range(LINES)
+            ]
+            add_sums(sum_ref, rows_ref, active.at[g], grad_ref.at[g], sums)
+            values = jnp.concatenate(grads, axis=0)
+            if k == 1:
+                put_next(rows[g], values, m, -1, same_ref, swap_ref)
+            else:
+                put_home(rows[g], values, m, own_ref, home_ref)
         return carry
 
-    lax.fori_loop(0, CHIPS, holder, 0)
+    lax.fori_loop(0, CHIPS // GROUP, holders, 0)
     end_sums(sum_ref, rows_ref)
     if k == 0:
         share_out((sum_ref, sum1_ref, sum2_ref), small_ref, keep_ref, send_ref)
@@ -421,11 +450,10 @@
 
 
 def from_chips(values):
-    got = {
-        back: lax.ppermute(values, "line", [(i, (i + 2 * back) % NL) for i in range(NL)])
-        for back in (2, 1, 3)
-    }
-    return [values, got[1], got[2], got[3]]
+    got = [values]
+    for back in range(1, CHIPS):
+        got.append(lax.ppermute(values, "line", [(i, (i + 2 * back) % NL) for i in range(NL)]))
+    return got
 
 
 def to_ring(values, turn, ring, stride):
@@ -455,8 +483,10 @@
     tables = (shape(3, CHIPS, 1, CELLS, dtype=I32), shape(3, CHIPS, LINES, CH, dtype=F32))
     state = (shape(CHIPS, LINES, LINE, CH), shape(CHIPS, LINES, LINE, CH, dtype=F32))
     sums = shape(ROWS, CH, dtype=F32)
-    pad = (LINES, LINE + 16, CH)
+    pad = (GROUP, LINES, LINE + 16, CH)
+    lines = pltpu.VMEM((GROUP, LINES, LINE, CH), BF16)
     parts = (TAPS + 1, 8, CH)
+    back = (pad, parts, lines, lines, lines)
 
     keep, keep_cot, send, extra = call(
         prep_kernel,
@@ -472,26 +502,26 @@
     pieces = from_chips(piece)
     pieces_cot = from_chips(piece_cot)
     order, starts, same, moved, x0, h0 = call(
-        functools.partial(forward_kernel, 0), (*tables, moving, moving, *state), 7, scratch=(pad,)
+        functools.partial(forward_kernel, 0), (*tables, moving, moving, *state), 7, scratch=(pad, lines)
     )(*pieces, *weights)
     given = (*weights, order, starts)
     same, moved, x1, h1 = call(
-        functools.partial(forward_kernel, 1), (moving, moving, *state), 7, scratch=(pad,)
+        functools.partial(forward_kernel, 1), (moving, moving, *state), 7, scratch=(pad, lines)
     )(same, swap(moved), *given)
     same, moved, first, second, sums2 = call(
-        turn_kernel, (moving, moving, quarter, quarter, sums), 11, scratch=(pad, parts)
+        turn_kernel, (moving, moving, quarter, quarter, sums), 11, scratch=(pad, parts, lines, lines, lines, lines, (GROUP, LINES, LINE, CH))
     )(same, swap(moved), *pieces_cot, *given)
     second = swap(second)
     moved = swap(moved)
     same, moved, sums1 = call(
-        functools.partial(backward_kernel, 1), (moving, moving, sums), 9, scratch=(pad, parts)
+        functools.partial(backward_kernel, 1), (moving, moving, sums), 9, scratch=back
     )(same, moved, x1, h1, *given)
     share = shape(RING, SHARE, CH, dtype=F32)
     imitated, own, home, keep, send = call(
         functools.partial(backward_kernel, 0),
         (shape(1, CELLS, CH), quarter, quarter, share, share),
         13,
-        scratch=(pad, parts, (ROWS, CH), (NL, 8, CH)),
+        scratch=(*back, (ROWS, CH), (NL, 8, CH)),
     )(same, swap(moved), x0, h0, *given, sums1, sums2, first, second)
     grad_scale = float(dp_size * NL * CELLS) ** (-0.5)
     got = swap(send)

time: 121 us -> 108 us (0.89)
  Pallas kernels: 40.1 us -> 27.3 us
    pallas_call x1, Pallas kernels: 7.03 us -> 3.44 us  [block(): call(functools.partial(forward_kernel, 1), (moving, moving, *state), 7, s...]
    pallas_call x1, Pallas kernels: 7.06 us -> 3.49 us  [block(): call(functools.partial(forward_kernel, 0), (*tables, moving, moving, *sta...]
    pallas_call x1, Pallas kernels: 10.7 us -> 7.33 us  [block(): call(turn_kernel, (moving, moving, quarter, quarter, sums), 11, scratch=(...]
where the time goes in v5:
time: 108 us
  starting transfers between devices  45.4 us (42%)
  waiting for transfers between devices  33.4 us (31%)
  Pallas kernels  27.3 us (25%)
    ppermute x6, waiting for transfers between devices, from_chips(): lax.ppermute(values, 'line', [(i, (i + 2 * back) % NL) for i in range(NL)])  16.4 us
    ppermute x9, starting transfers between devices, swap(): return lax.ppermute(values, 'line', [(i, i ^ 1) for i in range(NL)])  15.4 us
    ppermute x10, starting transfers between devices, to_ring(): return lax.ppermute(values, 'dp', pairs)  15.1 us
    ppermute x6, starting transfers between devices, from_chips(): lax.ppermute(values, 'line', [(i, (i + 2 * back) % NL) for i in range(NL)])  14.9 us
    ppermute x10, waiting for transfers between devices, to_ring(): return lax.ppermute(values, 'dp', pairs)  10.2 us
    pallas_call x1, Pallas kernels, block(): call(turn_kernel, (moving, moving, quarter, quarter, sums), 11, scratch=(...  7.33 us
    ppermute x9, waiting for transfers between devices, swap(): return lax.ppermute(values, 'line', [(i, i ^ 1) for i in range(NL)])  6.77 us
    pallas_call x1, Pallas kernels, block(): call(functools.partial(backward_kernel, 0), (shape(1, CELLS, CH), quarter...  5.36 us
  transfers between devices with their start and end apart: 25, of which 17 were waited for; matrix products, arithmetic and copies ran while one was open for 0% of the time, Pallas kernels for 0%

profile of v5, /device:TPU:1, one launch (start us, length us, event | category | flops | bytes accessed | tf_op | source)
XLA Modules:
  0.0 107.7 jit_solution(12273016117562594961)
XLA Ops:
  0.6 1.8 %shard_map.110 = (bf16[4,64,128]{2,1,0:T(8,128)(2,1)}, bf16[4,64,128]{2,1,0:T(8,128)(2,1)}, bf16[8,64,128]{2,1,0:T(8,128)(2,1)}, bf16[48,128]{1,0:T(8,128)(2,1)}) custom-call(bf16[1,512,128]{2,1,0:T(8,128)(2,1)} %fields_ref.1, bf16[1,512,128]{2,1,0:T(8,128)(2,1)} %cot_ref.1, s32[3,512]{1,0:T(4,128)} %table_ref.1, s32[3,4]{1,0:T(4,128)} %begin_ref.1), custom_call_target="tpu_custom_call" | custom-call | tf_op jit(solution)/shard_map/pallas_call | solution.py:491
  2.4 3.3 %collective-permute-start = (bf16[8,64,128]{2,1,0:T(8,128)(2,1)}, bf16[8,64,128]{2,1,0:T(8,128)(2,1)S(1)}, u32[]{:S(2)}, u32[]{:S(2)}) collective-permute-start(bf16[8,64,128]{2,1,0:T(8,128)(2,1)} %get-tuple-element.37), channel_id=1, source_target_pairs={{0,32},{32,0},{64,96},{96,64},{128,160},{160,128},{192,224},{224,1... | collective-permute-start | bytes 393224 | tf_op jit(solution)/shard_map/ppermute | solution.py:449
  7.6 4.4 %collective-permute-start.3 = (bf16[560,128]{1,0:T(8,128)(2,1)S(1)}, bf16[560,128]{1,0:T(8,128)(2,1)S(1)}, u32[]{:S(2)}, u32[]{:S(2)}) collective-permute-start(bf16[560,128]{1,0:T(8,128)(2,1)S(1)} %pad_maximum_fusion.refs_0_), channel_id=1, source_target_pairs={{0,192},{32,224},{64,0},{96,32},{128,64},{160,96},{192,128},{224,1... | collective-permute-start | bytes 430088 | tf_op jit(solution)/shard_map/ppermute | solution.py:455
  13.0 2.3 %collective-permute-start.1 = (bf16[560,128]{1,0:T(8,128)(2,1)S(1)}, bf16[560,128]{1,0:T(8,128)(2,1)S(1)}, u32[]{:S(2)}, u32[]{:S(2)}) collective-permute-start(bf16[560,128]{1,0:T(8,128)(2,1)S(1)} %pad_maximum_fusion.refs_0_), channel_id=1, source_target_pairs={{0,64},{32,96},{64,128},{96,160},{128,192},{160,224},{192,0},{224,... | collective-permute-start | bytes 430088 | tf_op jit(solution)/shard_map/ppermute | solution.py:455
  15.3 3.4 %collective-permute-done.3.refs_3_ = bf16[560,128]{1,0:T(8,128)(2,1)S(1)} collective-permute-done((bf16[560,128]{1,0:T(8,128)(2,1)S(1)}, bf16[560,128]{1,0:T(8,128)(2,1)S(1)}, u32[]{:S(2)}, u32[]{:S(2)}) %collective-permute-start.3) | collective-permute-done | bytes 143392 | tf_op jit(solution)/shard_map/ppermute | solution.py:455
  18.7 5.4 %collective-permute-done.2.refs_2_ = bf16[560,128]{1,0:T(8,128)(2,1)S(1)} collective-permute-done((bf16[560,128]{1,0:T(8,128)(2,1)S(1)}, bf16[560,128]{1,0:T(8,128)(2,1)S(1)}, u32[]{:S(2)}, u32[]{:S(2)}) %collective-permute-start.2) | collective-permute-done | bytes 143392 | tf_op jit(solution)/shard_map/ppermute | solution.py:455
  24.1 3.5 %shard_map.111 = (s32[3,4,1,512]{3,2,1,0:T(1,128)S(1)}, f32[3,4,4,128]{3,2,1,0:T(4,128)S(1)}, bf16[4,4,64,128]{3,2,1,0:T(8,128)(2,1)S(1)}, bf16[4,4,64,128]{3,2,...) custom-call(bf16[560,128]{1,0:T(8,128)(2,1)S(1)} %pad_maximum_fusion.refs_0_, ...), custom_call_target="tpu_custom_call" | custom-call | tf_op jit(solution)/shard_map/pallas_call | solution.py:504
  27.6 2.5 %collective-permute-start.4 = (bf16[4,4,64,128]{3,2,1,0:T(8,128)(2,1)S(1)}, bf16[4,4,64,128]{3,2,1,0:T(8,128)(2,1)S(1)}, u32[]{:S(2)}, u32[]{:S(2)}) collective-permute-start(bf16[4,4,64,128]{3,2,1,0:T(8,128)(2,1)S(1)} %get-tuple-element.40), channel_id=1, source_target_pairs={{0,32},{32,0},{64,96},{96,64},{128,160},{160,128},{192,224},{224,1... | collective-permute-start | bytes 786440 | tf_op jit(solution)/shard_map/ppermute | solution.py:449
  31.2 3.4 %shard_map.112 = (bf16[4,4,64,128]{3,2,1,0:T(8,128)(2,1)S(1)}, bf16[4,4,64,128]{3,2,1,0:T(8,128)(2,1)S(1)}, bf16[4,4,128,128]{3,2,1,0:T(8,128)(2,1)S(1)}, f32[4,4,128,128]{3,2,1,0:T(8,128)S(1)}) custom-call(bf16[4,4,64,128]{3,2,1,0:T(8,128)(2,1)S(1)} %get-tuple-element.39.refs_0_, bf16[4,4,64,128]{3,2,1,0:T(8,128)(2,1)S(1)} %collective-permute-done.4.refs_1_, ...), custom_call_target="tpu_custom_call" | custom-call | tf_op jit(solution)/shard_map/pallas_call | solution.py:508
  35.2 3.4 %collective-permute-start.8 = (bf16[512,128]{1,0:T(8,128)(2,1)S(1)}, bf16[512,128]{1,0:T(8,128)(2,1)S(1)}, u32[]{:S(2)}, u32[]{:S(2)}) collective-permute-start(bf16[512,128]{1,0:T(8,128)(2,1)S(1)} %pad_maximum_fusion.1.refs_2_), channel_id=1, source_target_pairs={{0,192},{32,224},{64,0},{96,32},{128,64},{160,96},{192,128},{224,1... | collective-permute-start | bytes 393224 | tf_op jit(solution)/shard_map/ppermute | solution.py:455
  38.5 1.8 %collective-permute-start.7 = (bf16[512,128]{1,0:T(8,128)(2,1)S(1)}, bf16[512,128]{1,0:T(8,128)(2,1)S(1)}, u32[]{:S(2)}, u32[]{:S(2)}) collective-permute-start(bf16[512,128]{1,0:T(8,128)(2,1)S(1)} %pad_maximum_fusion.1.refs_2_), channel_id=1, source_target_pairs={{0,128},{32,160},{64,192},{96,224},{128,0},{160,32},{192,64},{224,... | collective-permute-start | bytes 393224 | tf_op jit(solution)/shard_map/ppermute | solution.py:455
  40.4 2.0 %collective-permute-start.6 = (bf16[512,128]{1,0:T(8,128)(2,1)S(1)}, bf16[512,128]{1,0:T(8,128)(2,1)S(1)}, u32[]{:S(2)}, u32[]{:S(2)}) collective-permute-start(bf16[512,128]{1,0:T(8,128)(2,1)S(1)} %pad_maximum_fusion.1.refs_2_), channel_id=1, source_target_pairs={{0,64},{32,96},{64,128},{96,160},{128,192},{160,224},{192,0},{224,... | collective-permute-start | bytes 393224 | tf_op jit(solution)/shard_map/ppermute | solution.py:455
  42.4 7.1 %collective-permute-done.7.refs_4_ = bf16[512,128]{1,0:T(8,128)(2,1)S(1)} collective-permute-done((bf16[512,128]{1,0:T(8,128)(2,1)S(1)}, bf16[512,128]{1,0:T(8,128)(2,1)S(1)}, u32[]{:S(2)}, u32[]{:S(2)}) %collective-permute-start.7) | collective-permute-done | bytes 131104 | tf_op jit(solution)/shard_map/ppermute | solution.py:455
  50.0 7.3 %shard_map.113 = (bf16[4,4,64,128]{3,2,1,0:T(8,128)(2,1)S(1)}, bf16[4,4,64,128]{3,2,1,0:T(8,128)(2,1)S(1)}, bf16[4,64,128]{2,1,0:T(8,128)(2,1)S(1)}, bf16[4,64,128]{2,1,0:T(8,128)(2,1)S(1)}, f32[144,128]{1,0:T(8,128)S(1)}) custom-call(bf16[4,4,64,128]{3,2,1,0:T(8,128)(2,1)S(1)} %get-tuple-element.43.refs_0_, ...), custom_call_target="tpu_custom_call" | custom-call | tf_op jit(solution)/shard_map/pallas_call | solution.py:511
  57.4 2.0 %collective-permute-start.9 = (bf16[4,4,64,128]{3,2,1,0:T(8,128)(2,1)S(1)}, bf16[4,4,64,128]{3,2,1,0:T(8,128)(2,1)S(1)}, u32[]{:S(2)}, u32[]{:S(2)}) collective-permute-start(bf16[4,4,64,128]{3,2,1,0:T(8,128)(2,1)S(1)} %get-tuple-element.47), channel_id=1, source_target_pairs={{0,32},{32,0},{64,96},{96,64},{128,160},{160,128},{192,224},{224,1... | collective-permute-start | bytes 786440 | tf_op jit(solution)/shard_map/ppermute | solution.py:449
  60.5 5.2 %shard_map.114 = (bf16[4,4,64,128]{3,2,1,0:T(8,128)(2,1)S(1)}, bf16[4,4,64,128]{3,2,1,0:T(8,128)(2,1)S(1)}, f32[144,128]{1,0:T(8,128)S(1)}) custom-call(bf16[4,4,64,128]{3,2,1,0:T(8,128)(2,1)S(1)} %get-tuple-element.46.refs_0_, bf16[4,4,64,128]{3,2,1,0:T(8,128)(2,1)S(1)} %collective-permute-done.9.refs_1_, ...), custom_call_target="tpu_custom_call" | custom-call | tf_op jit(solution)/shard_map/pallas_call | solution.py:516
  67.4 5.4 %shard_map.115 = (bf16[1,512,128]{2,1,0:T(8,128)(2,1)}, bf16[4,64,128]{2,1,0:T(8,128)(2,1)S(1)}, bf16[4,64,128]{2,1,0:T(8,128)(2,1)S(1)}, f32[4,56,128]{2,1,0:T(8,128)S(1)}, f32[4,56,128]{2,1,0:T(8,128)S(1)}) custom-call(bf16[4,4,64,128]{3,2,1,0:T(8,128)(2,1)S(1)} %get-tuple-element.50.refs_0_, bf16[4,4,64,128]{3,2,1,0:T(8,128)(2,1)S(1)} %collective-permute-done.10.refs_1_, ...), custom_call_target="tpu_custom_call" | custom-call | tf_op jit(solution)/shard_map/pallas_call | solution.py:520
  75.6 2.6 %collective-permute-start.15 = (f32[56,128]{1,0:T(8,128)S(1)}, f32[56,128]{1,0:T(8,128)S(1)}, u32[]{:S(2)}, u32[]{:S(2)}) collective-permute-start(f32[56,128]{1,0:T(8,128)S(1)} %get-tuple-element.70), channel_id=1, source_target_pairs={{0,2},{1,3},{2,0},{3,1},{4,6},{5,7},{6,4},{7,5},{8,10},{9,11},{10,... | collective-permute-start | bytes 86024 | tf_op jit(solution)/shard_map/ppermute | solution.py:464
  81.2 2.6 %collective-permute-start.18 = (f32[56,128]{1,0:T(8,128)S(1)}, f32[56,128]{1,0:T(8,128)S(1)}, u32[]{:S(2)}, u32[]{:S(2)}) collective-permute-start(f32[56,128]{1,0:T(8,128)S(1)} %fusion.2), channel_id=1, source_target_pairs={{0,12},{1,13},{2,14},{3,15},{4,0},{5,1},{6,2},{7,3},{8,4},{9,5},{1... | collective-permute-start | bytes 86024 | tf_op jit(solution)/shard_map/ppermute | solution.py:464
  84.9 3.1 %collective-permute-done.17 = f32[56,128]{1,0:T(8,128)S(1)} collective-permute-done((f32[56,128]{1,0:T(8,128)S(1)}, f32[56,128]{1,0:T(8,128)S(1)}, u32[]{:S(2)}, u32[]{:S(2)}) %collective-permute-start.17) | collective-permute-done | bytes 28704 | tf_op jit(solution)/shard_map/ppermute | solution.py:464
  88.3 3.7 %collective-permute-start.19 = (f32[56,128]{1,0:T(8,128)S(1)}, f32[56,128]{1,0:T(8,128)S(1)}, u32[]{:S(2)}, u32[]{:S(2)}) collective-permute-start(f32[56,128]{1,0:T(8,128)S(1)} %add_add_fusion), channel_id=1, source_target_pairs={{0,16},{1,17},{2,18},{3,19},{4,20},{5,21},{6,22},{7,23},{8,24},{9,... | collective-permute-start | bytes 86024 | tf_op jit(solution)/shard_map/ppermute | solution.py:464
  93.3 2.0 %collective-permute-start.22 = (f32[56,128]{1,0:T(8,128)S(1)}, f32[56,128]{1,0:T(8,128)S(1)}, u32[]{:S(2)}, u32[]{:S(2)}) collective-permute-start(f32[56,128]{1,0:T(8,128)S(1)} %add_multiply_fusion), channel_id=1, source_target_pairs={{0,3},{1,0},{2,1},{3,2},{4,7},{5,4},{6,5},{7,6},{8,11},{9,8},{10,9... | collective-permute-start | bytes 86024 | tf_op jit(solution)/shard_map/ppermute | solution.py:464
  96.3 3.3 %collective-permute-done.21 = f32[56,128]{1,0:T(8,128)S(1)} collective-permute-done((f32[56,128]{1,0:T(8,128)S(1)}, f32[56,128]{1,0:T(8,128)S(1)}, u32[]{:S(2)}, u32[]{:S(2)}) %collective-permute-start.21) | collective-permute-done | bytes 28704 | tf_op jit(solution)/shard_map/ppermute | solution.py:464
  99.5 6.1 %collective-permute-start.23 = (f32[4,56,128]{2,1,0:T(8,128)S(1)}, f32[4,56,128]{2,1,0:T(8,128)S(1)}, u32[]{:S(2)}, u32[]{:S(2)}) collective-permute-start(f32[4,56,128]{2,1,0:T(8,128)S(1)} %pad_maximum_fusion.2.own_ref), channel_id=1, source_target_pairs={{0,32},{32,0},{64,96},{96,64},{128,160},{160,128},{192,224},{224,1... | collective-permute-start | bytes 344072 | tf_op jit(solution)/shard_map/ppermute | solution.py:449
  (54 shorter events, 19.5 us)
Async XLA Ops:
  2.4 4.5 %collective-permute-start = (bf16[8,64,128]{2,1,0:T(8,128)(2,1)}, bf16[8,64,128]{2,1,0:T(8,128)(2,1)S(1)}, u32[]{:S(2)}, u32[]{:S(2)}) collective-permute-start(bf16[8,64,128]{2,1,0:T(8,128)(2,1)} %get-tuple-element.37), channel_id=1, source_target_pairs={{0,32},{32,0},{64,96},{96,64},{128,160},{160,128},{192,224},{224,1... | collective-permute-start | bytes 393224 | tf_op jit(solution)/shard_map/ppermute | solution.py:449
  7.6 11.0 %collective-permute-start.3 = (bf16[560,128]{1,0:T(8,128)(2,1)S(1)}, bf16[560,128]{1,0:T(8,128)(2,1)S(1)}, u32[]{:S(2)}, u32[]{:S(2)}) collective-permute-start(bf16[560,128]{1,0:T(8,128)(2,1)S(1)} %pad_maximum_fusion.refs_0_), channel_id=1, source_target_pairs={{0,192},{32,224},{64,0},{96,32},{128,64},{160,96},{192,128},{224,1... | collective-permute-start | bytes 430088 | tf_op jit(solution)/shard_map/ppermute | solution.py:455
  12.0 12.1 %collective-permute-start.2 = (bf16[560,128]{1,0:T(8,128)(2,1)S(1)}, bf16[560,128]{1,0:T(8,128)(2,1)S(1)}, u32[]{:S(2)}, u32[]{:S(2)}) collective-permute-start(bf16[560,128]{1,0:T(8,128)(2,1)S(1)} %pad_maximum_fusion.refs_0_), channel_id=1, source_target_pairs={{0,128},{32,160},{64,192},{96,224},{128,0},{160,32},{192,64},{224,... | collective-permute-start | bytes 430088 | tf_op jit(solution)/shard_map/ppermute | solution.py:455
  13.0 11.1 %collective-permute-start.1 = (bf16[560,128]{1,0:T(8,128)(2,1)S(1)}, bf16[560,128]{1,0:T(8,128)(2,1)S(1)}, u32[]{:S(2)}, u32[]{:S(2)}) collective-permute-start(bf16[560,128]{1,0:T(8,128)(2,1)S(1)} %pad_maximum_fusion.refs_0_), channel_id=1, source_target_pairs={{0,64},{32,96},{64,128},{96,160},{128,192},{160,224},{192,0},{224,... | collective-permute-start | bytes 430088 | tf_op jit(solution)/shard_map/ppermute | solution.py:455
  27.6 3.6 %collective-permute-start.4 = (bf16[4,4,64,128]{3,2,1,0:T(8,128)(2,1)S(1)}, bf16[4,4,64,128]{3,2,1,0:T(8,128)(2,1)S(1)}, u32[]{:S(2)}, u32[]{:S(2)}) collective-permute-start(bf16[4,4,64,128]{3,2,1,0:T(8,128)(2,1)S(1)} %get-tuple-element.40), channel_id=1, source_target_pairs={{0,32},{32,0},{64,96},{96,64},{128,160},{160,128},{192,224},{224,1... | collective-permute-start | bytes 786440 | tf_op jit(solution)/shard_map/ppermute | solution.py:449
  34.7 15.3 %collective-permute-start.5 = (bf16[4,4,64,128]{3,2,1,0:T(8,128)(2,1)S(1)}, bf16[4,4,64,128]{3,2,1,0:T(8,128)(2,1)S(1)}, u32[]{:S(2)}, u32[]{:S(2)}) collective-permute-start(bf16[4,4,64,128]{3,2,1,0:T(8,128)(2,1)S(1)} %get-tuple-element.44), channel_id=1, source_target_pairs={{0,32},{32,0},{64,96},{96,64},{128,160},{160,128},{192,224},{224,1... | collective-permute-start | bytes 786440 | tf_op jit(solution)/shard_map/ppermute | solution.py:449
  35.2 7.2 %collective-permute-start.8 = (bf16[512,128]{1,0:T(8,128)(2,1)S(1)}, bf16[512,128]{1,0:T(8,128)(2,1)S(1)}, u32[]{:S(2)}, u32[]{:S(2)}) collective-permute-start(bf16[512,128]{1,0:T(8,128)(2,1)S(1)} %pad_maximum_fusion.1.refs_2_), channel_id=1, source_target_pairs={{0,192},{32,224},{64,0},{96,32},{128,64},{160,96},{192,128},{224,1... | collective-permute-start | bytes 393224 | tf_op jit(solution)/shard_map/ppermute | solution.py:455
  38.5 10.9 %collective-permute-start.7 = (bf16[512,128]{1,0:T(8,128)(2,1)S(1)}, bf16[512,128]{1,0:T(8,128)(2,1)S(1)}, u32[]{:S(2)}, u32[]{:S(2)}) collective-permute-start(bf16[512,128]{1,0:T(8,128)(2,1)S(1)} %pad_maximum_fusion.1.refs_2_), channel_id=1, source_target_pairs={{0,128},{32,160},{64,192},{96,224},{128,0},{160,32},{192,64},{224,... | collective-permute-start | bytes 393224 | tf_op jit(solution)/shard_map/ppermute | solution.py:455
  40.4 9.6 %collective-permute-start.6 = (bf16[512,128]{1,0:T(8,128)(2,1)S(1)}, bf16[512,128]{1,0:T(8,128)(2,1)S(1)}, u32[]{:S(2)}, u32[]{:S(2)}) collective-permute-start(bf16[512,128]{1,0:T(8,128)(2,1)S(1)} %pad_maximum_fusion.1.refs_2_), channel_id=1, source_target_pairs={{0,64},{32,96},{64,128},{96,160},{128,192},{160,224},{192,0},{224,... | collective-permute-start | bytes 393224 | tf_op jit(solution)/shard_map/ppermute | solution.py:455
  57.4 3.2 %collective-permute-start.9 = (bf16[4,4,64,128]{3,2,1,0:T(8,128)(2,1)S(1)}, bf16[4,4,64,128]{3,2,1,0:T(8,128)(2,1)S(1)}, u32[]{:S(2)}, u32[]{:S(2)}) collective-permute-start(bf16[4,4,64,128]{3,2,1,0:T(8,128)(2,1)S(1)} %get-tuple-element.47), channel_id=1, source_target_pairs={{0,32},{32,0},{64,96},{96,64},{128,160},{160,128},{192,224},{224,1... | collective-permute-start | bytes 786440 | tf_op jit(solution)/shard_map/ppermute | solution.py:449
  65.7 1.7 %collective-permute-start.10 = (bf16[4,4,64,128]{3,2,1,0:T(8,128)(2,1)S(1)}, bf16[4,4,64,128]{3,2,1,0:T(8,128)(2,1)S(1)}, u32[]{:S(2)}, u32[]{:S(2)}) collective-permute-start(bf16[4,4,64,128]{3,2,1,0:T(8,128)(2,1)S(1)} %get-tuple-element.51), channel_id=1, source_target_pairs={{0,32},{32,0},{64,96},{96,64},{128,160},{160,128},{192,224},{224,1... | collective-permute-start | bytes 786440 | tf_op jit(solution)/shard_map/ppermute | solution.py:449
  66.2 1.3 %collective-permute-start.11 = (bf16[4,64,128]{2,1,0:T(8,128)(2,1)S(1)}, bf16[4,64,128]{2,1,0:T(8,128)(2,1)S(1)}, u32[]{:S(2)}, u32[]{:S(2)}) collective-permute-start(bf16[4,64,128]{2,1,0:T(8,128)(2,1)S(1)} %get-tuple-element.57), channel_id=1, source_target_pairs={{0,32},{32,0},{64,96},{96,64},{128,160},{160,128},{192,224},{224,1... | collective-permute-start | bytes 196616 | tf_op jit(solution)/shard_map/ppermute | solution.py:449
  72.8 1.3 %collective-permute-start.12 = (f32[4,56,128]{2,1,0:T(8,128)S(1)}, f32[4,56,128]{2,1,0:T(8,128)S(1)}, u32[]{:S(2)}, u32[]{:S(2)}) collective-permute-start(f32[4,56,128]{2,1,0:T(8,128)S(1)} %get-tuple-element.60), channel_id=1, source_target_pairs={{0,32},{32,0},{64,96},{96,64},{128,160},{160,128},{192,224},{224,1... | collective-permute-start | bytes 344072 | tf_op jit(solution)/shard_map/ppermute | solution.py:449
  74.2 5.1 %collective-permute-start.13 = (f32[56,128]{1,0:T(8,128)S(1)}, f32[56,128]{1,0:T(8,128)S(1)}, u32[]{:S(2)}, u32[]{:S(2)}) collective-permute-start(f32[56,128]{1,0:T(8,128)S(1)} %get-tuple-element.69), channel_id=1, source_target_pairs={{0,1},{1,2},{2,3},{3,0},{4,5},{5,6},{6,7},{7,4},{8,9},{9,10},{10,1... | collective-permute-start | bytes 86024 | tf_op jit(solution)/shard_map/ppermute | solution.py:464
  75.6 4.2 %collective-permute-start.15 = (f32[56,128]{1,0:T(8,128)S(1)}, f32[56,128]{1,0:T(8,128)S(1)}, u32[]{:S(2)}, u32[]{:S(2)}) collective-permute-start(f32[56,128]{1,0:T(8,128)S(1)} %get-tuple-element.70), channel_id=1, source_target_pairs={{0,2},{1,3},{2,0},{3,1},{4,6},{5,7},{6,4},{7,5},{8,10},{9,11},{10,... | collective-permute-start | bytes 86024 | tf_op jit(solution)/shard_map/ppermute | solution.py:464
  78.2 3.0 %collective-permute-start.14 = (f32[56,128]{1,0:T(8,128)S(1)}, f32[56,128]{1,0:T(8,128)S(1)}, u32[]{:S(2)}, u32[]{:S(2)}) collective-permute-start(f32[56,128]{1,0:T(8,128)S(1)} %get-tuple-element.71), channel_id=1, source_target_pairs={{0,3},{1,0},{2,1},{3,2},{4,7},{5,4},{6,5},{7,6},{8,11},{9,8},{10,9... | collective-permute-start | bytes 86024 | tf_op jit(solution)/shard_map/ppermute | solution.py:464
  81.2 3.7 %collective-permute-start.18 = (f32[56,128]{1,0:T(8,128)S(1)}, f32[56,128]{1,0:T(8,128)S(1)}, u32[]{:S(2)}, u32[]{:S(2)}) collective-permute-start(f32[56,128]{1,0:T(8,128)S(1)} %fusion.2), channel_id=1, source_target_pairs={{0,12},{1,13},{2,14},{3,15},{4,0},{5,1},{6,2},{7,3},{8,4},{9,5},{1... | collective-permute-start | bytes 86024 | tf_op jit(solution)/shard_map/ppermute | solution.py:464
  83.8 4.2 %collective-permute-start.17 = (f32[56,128]{1,0:T(8,128)S(1)}, f32[56,128]{1,0:T(8,128)S(1)}, u32[]{:S(2)}, u32[]{:S(2)}) collective-permute-start(f32[56,128]{1,0:T(8,128)S(1)} %fusion.2), channel_id=1, source_target_pairs={{0,8},{1,9},{2,10},{3,11},{4,12},{5,13},{6,14},{7,15},{8,0},{9,1},... | collective-permute-start | bytes 86024 | tf_op jit(solution)/shard_map/ppermute | solution.py:464
  84.3 4.0 %collective-permute-start.16 = (f32[56,128]{1,0:T(8,128)S(1)}, f32[56,128]{1,0:T(8,128)S(1)}, u32[]{:S(2)}, u32[]{:S(2)}) collective-permute-start(f32[56,128]{1,0:T(8,128)S(1)} %fusion.2), channel_id=1, source_target_pairs={{0,4},{1,5},{2,6},{3,7},{4,8},{5,9},{6,10},{7,11},{8,12},{9,13},{1... | collective-permute-start | bytes 86024 | tf_op jit(solution)/shard_map/ppermute | solution.py:464
  88.3 5.0 %collective-permute-start.19 = (f32[56,128]{1,0:T(8,128)S(1)}, f32[56,128]{1,0:T(8,128)S(1)}, u32[]{:S(2)}, u32[]{:S(2)}) collective-permute-start(f32[56,128]{1,0:T(8,128)S(1)} %add_add_fusion), channel_id=1, source_target_pairs={{0,16},{1,17},{2,18},{3,19},{4,20},{5,21},{6,22},{7,23},{8,24},{9,... | collective-permute-start | bytes 86024 | tf_op jit(solution)/shard_map/ppermute | solution.py:464
  93.3 3.0 %collective-permute-start.22 = (f32[56,128]{1,0:T(8,128)S(1)}, f32[56,128]{1,0:T(8,128)S(1)}, u32[]{:S(2)}, u32[]{:S(2)}) collective-permute-start(f32[56,128]{1,0:T(8,128)S(1)} %add_multiply_fusion), channel_id=1, source_target_pairs={{0,3},{1,0},{2,1},{3,2},{4,7},{5,4},{6,5},{7,6},{8,11},{9,8},{10,9... | collective-permute-start | bytes 86024 | tf_op jit(solution)/shard_map/ppermute | solution.py:464
  95.3 4.2 %collective-permute-start.21 = (f32[56,128]{1,0:T(8,128)S(1)}, f32[56,128]{1,0:T(8,128)S(1)}, u32[]{:S(2)}, u32[]{:S(2)}) collective-permute-start(f32[56,128]{1,0:T(8,128)S(1)} %add_multiply_fusion), channel_id=1, source_target_pairs={{0,2},{1,3},{2,0},{3,1},{4,6},{5,7},{6,4},{7,5},{8,10},{9,11},{10,... | collective-permute-start | bytes 86024 | tf_op jit(solution)/shard_map/ppermute | solution.py:464
  95.3 4.2 %collective-permute-start.20 = (f32[56,128]{1,0:T(8,128)S(1)}, f32[56,128]{1,0:T(8,128)S(1)}, u32[]{:S(2)}, u32[]{:S(2)}) collective-permute-start(f32[56,128]{1,0:T(8,128)S(1)} %add_multiply_fusion), channel_id=1, source_target_pairs={{0,1},{1,2},{2,3},{3,0},{4,5},{5,6},{6,7},{7,4},{8,9},{9,10},{10,1... | collective-permute-start | bytes 86024 | tf_op jit(solution)/shard_map/ppermute | solution.py:464
  99.5 7.3 %collective-permute-start.23 = (f32[4,56,128]{2,1,0:T(8,128)S(1)}, f32[4,56,128]{2,1,0:T(8,128)S(1)}, u32[]{:S(2)}, u32[]{:S(2)}) collective-permute-start(f32[4,56,128]{2,1,0:T(8,128)S(1)} %pad_maximum_fusion.2.own_ref), channel_id=1, source_target_pairs={{0,32},{32,0},{64,96},{96,64},{128,160},{160,128},{192,224},{224,1... | collective-permute-start | bytes 344072 | tf_op jit(solution)/shard_map/ppermute | solution.py:449
  (7 other events, 59.8 us)

commit v6 on v5

--- a/solution.py
+++ b/solution.py
@@ -127,8 +127,11 @@
     inverse = lax.rsqrt(jnp.mean(x * x, axis=-1, keepdims=True) + EPSILON)
     scaled = x * inverse
     normed = (scaled * gain).astype(BF16).astype(F32)
-    keep = lax.broadcasted_iota(I32, (LINE, CH), 0).astype(F32) >= start
-    return inverse, scaled, jnp.where(keep, normed, 0.0), keep
+    return inverse, jnp.where(kept(start), normed, 0.0)
+
+
+def kept(start):
+    return lax.broadcasted_iota(I32, (LINE, CH), 0).astype(F32) >= start
 
 
 def conv(pad, masked, taps):
@@ -148,12 +151,16 @@
         out[line] = dot(picks(row, line), received, 1, 0).astype(BF16)
 
 
-def hidden_stage(k, x_at, start_at, h_at, active, gain_ref, taps_ref, pads, line):
+def hidden_stage(k, x_at, start_at, saved, gain_ref, taps_ref, pads, line):
+    active, masked_at, inverse_at, slope_at = saved
     x = x_at[line].astype(F32)
-    masked = norm(x, gain_ref[k : k + 1, :], start_at[line : line + 1, :])[2]
+    inverse, masked = norm(x, gain_ref[k : k + 1, :], start_at[line : line + 1, :])
     hidden = conv(pads.at[line], masked, taps_ref[k])
-    h_at[line] = hidden
-    active[line] = (hidden * sigmoid(hidden)).astype(BF16)
+    gate = sigmoid(hidden)
+    active[line] = (hidden * gate).astype(BF16)
+    masked_at[line] = masked.astype(BF16)
+    inverse_at[line] = jnp.broadcast_to(inverse, (LINE, CH))
+    slope_at[line] = gate * (1.0 + hidden * (1.0 - gate))
 
 
 def mix_stage(k, x_at, active, mix_ref):
@@ -161,26 +168,21 @@
     return (x_at[...].reshape(CELLS, CH).astype(F32) + mixed).astype(BF16)
 
 
-def activity_stage(h_at, active):
-    for line in range(LINES):
-        hidden = h_at[line]
-        active[line] = (hidden * sigmoid(hidden)).astype(BF16)
-
-
-def slope_stage(k, grad_at, h_at, slope_at, mix_ref):
+def slope_stage(k, grad_at, slope_at, out, mix_ref):
     grad_act = dot(grad_at[...].reshape(CELLS, CH), mix_ref[k], 1, 1).reshape(LINES, LINE, CH)
     for line in range(LINES):
-        hidden = h_at[line]
-        gate = sigmoid(hidden)
-        slope_at[line] = (grad_act[line] * (gate * (1.0 + hidden * (1.0 - gate)))).astype(BF16)
-
-
-def backward_line(k, grad_at, x_at, start_at, slope_at, gain_ref, taps_ref, pads, line, sums):
+        out[line] = (grad_act[line] * slope_at[line]).astype(BF16)
+
+
+def backward_line(k, grad_at, x_at, start_at, saved, hidden_at, gain_ref, taps_ref, pads, line, sums):
     gain = gain_ref[k : k + 1, :]
     taps = taps_ref[k]
-    inverse, scaled, masked, keep = norm(x_at[line].astype(F32), gain, start_at[line : line + 1, :])
+    masked = saved[1][line].astype(F32)
+    inverse = saved[2][line]
+    scaled = x_at[line].astype(F32) * inverse
+    keep = kept(start_at[line : line + 1, :])
     total = None
-    for t, (first, moved) in enumerate(shifts(pads.at[line], slope_at[line].astype(F32))):
+    for t, (first, moved) in enumerate(shifts(pads.at[line], hidden_at[line].astype(F32))):
         u = t if t == 0 else (t + 1 if t % 2 else t - 1)
         size = moved.shape[0]
         term = taps[u : u + 1, :] * moved
@@ -193,6 +195,10 @@
     weighted = cells * gain
     moved = inverse * (weighted - scaled * jnp.mean(weighted * scaled, axis=-1, keepdims=True))
     return (grad_at[line].astype(F32) + moved).astype(BF16)
+
+
+def at(saved, index):
+    return [ref.at[index] for ref in saved]
 
 
 def add_sums(sum_ref, rows_ref, active, grad_at, sums):
@@ -271,11 +277,11 @@
 def forward_kernel(k, *refs):
     if k == 0:
         pieces, refs = refs[:CHIPS], refs[CHIPS:]
-        gain_ref, taps_ref, mix_ref, order_ref, starts_ref, same_ref, swap_ref, x_ref, h_ref, pad, active = refs
+        gain_ref, taps_ref, mix_ref, order_ref, starts_ref, same_ref, swap_ref, x_ref, *saved, pad = refs
         read_tables(pieces, order_ref, starts_ref)
     else:
-        (in_ref, in_swap_ref, gain_ref, taps_ref, mix_ref, order_ref, starts_ref) = refs[:7]
-        same_ref, swap_ref, x_ref, h_ref, pad, active = refs[7:]
+        in_ref, in_swap_ref, gain_ref, taps_ref, mix_ref, order_ref, starts_ref = refs[:7]
+        same_ref, swap_ref, x_ref, *saved, pad = refs[7:]
     clear(pad)
 
     def holders(i, carry):
@@ -288,9 +294,9 @@
         for g, m in enumerate(ms):
             for line in range(LINES):
                 hidden_stage(
-                    k, x_ref.at[m], starts_ref.at[k, m], h_ref.at[m], active.at[g], gain_ref, taps_ref, pad.at[g], line
+                    k, x_ref.at[m], starts_ref.at[k, m], at(saved, m), gain_ref, taps_ref, pad.at[g], line
                 )
-        after = [mix_stage(k, x_ref.at[m], active.at[g], mix_ref) for g, m in enumerate(ms)]
+        after = [mix_stage(k, x_ref.at[m], saved[0].at[m], mix_ref) for m in ms]
         for g, m in enumerate(ms):
             put_next(block_row(rows[g], False), after[g], m, 1, same_ref, swap_ref)
         return carry
@@ -304,7 +310,7 @@
     pieces = refs[2 : 2 + CHIPS]
     gain_ref, taps_ref, mix_ref, order_ref, starts_ref = refs[2 + CHIPS : 7 + CHIPS]
     same_ref, swap_ref, own_ref, home_ref, sum_ref = refs[7 + CHIPS : 12 + CHIPS]
-    pad, rows_ref, active, x_ref, grad_ref, slope_ref, h_ref = refs[12 + CHIPS :]
+    pad, rows_ref, grad_ref, hidden_ref, x_ref, *saved = refs[12 + CHIPS :]
     clear(pad)
     start_sums(sum_ref, rows_ref)
 
@@ -319,21 +325,31 @@
         for g, m in enumerate(ms):
             for line in range(LINES):
                 hidden_stage(
-                    k, x_ref.at[g], starts_ref.at[k, m], h_ref.at[g], active.at[g], gain_ref, taps_ref, pad.at[g], line
+                    k, x_ref.at[g], starts_ref.at[k, m], at(saved, g), gain_ref, taps_ref, pad.at[g], line
                 )
         for g, m in enumerate(ms):
-            after = mix_stage(k, x_ref.at[g], active.at[g], mix_ref)
-            slope_stage(k, grad_ref.at[g], h_ref.at[g], slope_ref.at[g], mix_ref)
+            after = mix_stage(k, x_ref.at[g], saved[0].at[g], mix_ref)
+            slope_stage(k, grad_ref.at[g], saved[3].at[g], hidden_ref.at[g], mix_ref)
             put_home(rows[g], after, m, own_ref, home_ref)
         for g, m in enumerate(ms):
             sums = [None] * (TAPS + 1)
             grads = [
                 backward_line(
-                    k, grad_ref.at[g], x_ref.at[g], starts_ref.at[k, m], slope_ref.at[g], gain_ref, taps_ref, pad.at[g], line, sums
+                    k,
+                    grad_ref.at[g],
+                    x_ref.at[g],
+                    starts_ref.at[k, m],
+                    at(saved, g),
+                    hidden_ref.at[g],
+                    gain_ref,
+                    taps_ref,
+                    pad.at[g],
+                    line,
+                    sums,
                 )
                 for line in range(LINES)
             ]
-            add_sums(sum_ref, rows_ref, active.at[g], grad_ref.at[g], sums)
+            add_sums(sum_ref, rows_ref, saved[0].at[g], grad_ref.at[g], sums)
             put_next(rows[g], jnp.concatenate(grads, axis=0), m, -1, same_ref, swap_ref)
         return carry
 
@@ -361,13 +377,15 @@
 
 
 def backward_kernel(k, *refs):
-    in_ref, in_swap_ref, x_ref, h_ref, gain_ref, taps_ref, mix_ref, order_ref, starts_ref = refs[:9]
+    in_ref, in_swap_ref, x_ref = refs[:3]
+    saved = refs[3:7]
+    gain_ref, taps_ref, mix_ref, order_ref, starts_ref = refs[7:12]
     if k == 1:
-        same_ref, swap_ref, sum_ref, pad, rows_ref, active, grad_ref, slope_ref = refs[9:]
+        same_ref, swap_ref, sum_ref, pad, rows_ref, grad_ref, hidden_ref = refs[12:]
     else:
-        sum1_ref, sum2_ref, first_ref, second_ref = refs[9:13]
-        imitated_ref, own_ref, home_ref, keep_ref, send_ref = refs[13:18]
-        pad, rows_ref, active, grad_ref, slope_ref, sum_ref, small_ref = refs[18:]
+        sum1_ref, sum2_ref, first_ref, second_ref = refs[12:16]
+        imitated_ref, own_ref, home_ref, keep_ref, send_ref = refs[16:21]
+        pad, rows_ref, grad_ref, hidden_ref, sum_ref, small_ref = refs[21:]
         zone, core = place_of()
         for m in range(CHIPS):
             for ref, first in ((first_ref, 2 * m - core), (second_ref, 2 * m + 1 - 3 * core)):
@@ -383,17 +401,26 @@
             rows.append(block_row(order_ref[k, m], False))
             gather_stage(rows[-1], moved_rows(in_ref, in_swap_ref, m), grad_ref.at[g])
         for g, m in enumerate(ms):
-            activity_stage(h_ref.at[m], active.at[g])
-            slope_stage(k, grad_ref.at[g], h_ref.at[m], slope_ref.at[g], mix_ref)
+            slope_stage(k, grad_ref.at[g], saved[3].at[m], hidden_ref.at[g], mix_ref)
         for g, m in enumerate(ms):
             sums = [None] * (TAPS + 1)
             grads = [
                 backward_line(
-                    k, grad_ref.at[g], x_ref.at[m], starts_ref.at[k, m], slope_ref.at[g], gain_ref, taps_ref, pad.at[g], line, sums
+                    k,
+                    grad_ref.at[g],
+                    x_ref.at[m],
+                    starts_ref.at[k, m],
+                    at(saved, m),
+                    hidden_ref.at[g],
+                    gain_ref,
+                    taps_ref,
+                    pad.at[g],
+                    line,
+                    sums,
                 )
                 for line in range(LINES)
             ]
-            add_sums(sum_ref, rows_ref, active.at[g], grad_ref.at[g], sums)
+            add_sums(sum_ref, rows_ref, saved[0].at[m], grad_ref.at[g], sums)
             values = jnp.concatenate(grads, axis=0)
             if k == 1:
                 put_next(rows[g], values, m, -1, same_ref, swap_ref)
@@ -466,11 +493,11 @@
 
 def sum_over_dp(parts):
     size = lax.axis_size("dp")
-    part = sum((to_ring(parts[turn], turn, RING, 1) for turn in (1, 3, 2)), parts[0])
+    part = sum([to_ring(parts[turn], turn, RING, 1) for turn in range(1, RING)], parts[0])
     stride = RING
     while stride < size:
         ring = RING if size % (stride * RING) == 0 else 2
-        part = sum((to_ring(part, turn, ring, stride) for turn in range(1, ring)), part)
+        part = sum([to_ring(part, turn, ring, stride) for turn in range(1, ring)], part)
         stride *= ring
     return part
 
@@ -481,12 +508,14 @@
     quarter = shape(CHIPS, Q, CH)
     moving = shape(CHIPS, CHIPS, Q, CH)
     tables = (shape(3, CHIPS, 1, CELLS, dtype=I32), shape(3, CHIPS, LINES, CH, dtype=F32))
-    state = (shape(CHIPS, LINES, LINE, CH), shape(CHIPS, LINES, LINE, CH, dtype=F32))
+    kinds = (BF16, BF16, BF16, F32, F32)
+    state = [shape(CHIPS, LINES, LINE, CH, dtype=kind) for kind in kinds]
     sums = shape(ROWS, CH, dtype=F32)
     pad = (GROUP, LINES, LINE + 16, CH)
     lines = pltpu.VMEM((GROUP, LINES, LINE, CH), BF16)
     parts = (TAPS + 1, 8, CH)
-    back = (pad, parts, lines, lines, lines)
+    back = (pad, parts, lines, lines)
+    wide = (GROUP, LINES, LINE, CH)
 
     keep, keep_cot, send, extra = call(
         prep_kernel,
@@ -501,28 +530,28 @@
     piece_cot = jnp.concatenate([keep_cot.reshape(HALF, CH), got[CHIPS:].reshape(HALF, CH)])
     pieces = from_chips(piece)
     pieces_cot = from_chips(piece_cot)
-    order, starts, same, moved, x0, h0 = call(
-        functools.partial(forward_kernel, 0), (*tables, moving, moving, *state), 7, scratch=(pad, lines)
+    order, starts, same, moved, *saved0 = call(
+        functools.partial(forward_kernel, 0), (*tables, moving, moving, *state), 7, scratch=(pad,)
     )(*pieces, *weights)
     given = (*weights, order, starts)
-    same, moved, x1, h1 = call(
-        functools.partial(forward_kernel, 1), (moving, moving, *state), 7, scratch=(pad, lines)
+    same, moved, *saved1 = call(
+        functools.partial(forward_kernel, 1), (moving, moving, *state), 7, scratch=(pad,)
     )(same, swap(moved), *given)
     same, moved, first, second, sums2 = call(
-        turn_kernel, (moving, moving, quarter, quarter, sums), 11, scratch=(pad, parts, lines, lines, lines, lines, (GROUP, LINES, LINE, CH))
+        turn_kernel, (moving, moving, quarter, quarter, sums), 11, scratch=(*back, lines, lines, lines, wide, wide)
     )(same, swap(moved), *pieces_cot, *given)
     second = swap(second)
     moved = swap(moved)
     same, moved, sums1 = call(
-        functools.partial(backward_kernel, 1), (moving, moving, sums), 9, scratch=back
-    )(same, moved, x1, h1, *given)
+        functools.partial(backward_kernel, 1), (moving, moving, sums), 12, scratch=back
+    )(same, moved, *saved1, *given)
     share = shape(RING, SHARE, CH, dtype=F32)
     imitated, own, home, keep, send = call(
         functools.partial(backward_kernel, 0),
         (shape(1, CELLS, CH), quarter, quarter, share, share),
-        13,
+        16,
         scratch=(*back, (ROWS, CH), (NL, 8, CH)),
-    )(same, swap(moved), x0, h0, *given, sums1, sums2, first, second)
+    )(same, swap(moved), *saved0, *given, sums1, sums2, first, second)
     grad_scale = float(dp_size * NL * CELLS) ** (-0.5)
     got = swap(send)
     home = swap(home)

time: 108 us -> 107 us (level)
  Pallas kernels: 27.3 us -> 26.2 us
where the time goes in v6:
time: 107 us
  starting transfers between devices  44.8 us (42%)
  waiting for transfers between devices  34 us (32%)
  Pallas kernels  26.2 us (24%)
    ppermute x6, waiting for transfers between devices, from_chips(): lax.ppermute(values, 'line', [(i, (i + 2 * back) % NL) for i in range(NL)])  16.4 us
    ppermute x9, starting transfers between devices, swap(): return lax.ppermute(values, 'line', [(i, i ^ 1) for i in range(NL)])  15.5 us
    ppermute x6, starting transfers between devices, from_chips(): lax.ppermute(values, 'line', [(i, (i + 2 * back) % NL) for i in range(NL)])  14.9 us
    ppermute x10, starting transfers between devices, to_ring(): return lax.ppermute(values, 'dp', pairs)  14.5 us
    ppermute x10, waiting for transfers between devices, to_ring(): return lax.ppermute(values, 'dp', pairs)  10.8 us
    ppermute x9, waiting for transfers between devices, swap(): return lax.ppermute(values, 'line', [(i, i ^ 1) for i in range(NL)])  6.77 us
    pallas_call x1, Pallas kernels, block(): call(turn_kernel, (moving, moving, quarter, quarter, sums), 11, scratch=(...  6.7 us
    pallas_call x1, Pallas kernels, block(): call(functools.partial(backward_kernel, 0), (shape(1, CELLS, CH), quarter...  5.02 us
  transfers between devices with their start and end apart: 25, of which 17 were waited for; matrix products, arithmetic and copies ran while one was open for 0% of the time, Pallas kernels for 0%

profile of v6, /device:TPU:1, one launch (start us, length us, event | category | flops | bytes accessed | tf_op | source)
XLA Modules:
  0.0 106.6 jit_solution(9197434207715417355)
XLA Ops:
  0.6 1.8 %shard_map.110 = (bf16[4,64,128]{2,1,0:T(8,128)(2,1)}, bf16[4,64,128]{2,1,0:T(8,128)(2,1)}, bf16[8,64,128]{2,1,0:T(8,128)(2,1)}, bf16[48,128]{1,0:T(8,128)(2,1)}) custom-call(bf16[1,512,128]{2,1,0:T(8,128)(2,1)} %fields_ref.1, bf16[1,512,128]{2,1,0:T(8,128)(2,1)} %cot_ref.1, s32[3,512]{1,0:T(4,128)} %table_ref.1, s32[3,4]{1,0:T(4,128)} %begin_ref.1), custom_call_target="tpu_custom_call" | custom-call | tf_op jit(solution)/shard_map/pallas_call | solution.py:520
  2.4 3.3 %collective-permute-start = (bf16[8,64,128]{2,1,0:T(8,128)(2,1)}, bf16[8,64,128]{2,1,0:T(8,128)(2,1)S(1)}, u32[]{:S(2)}, u32[]{:S(2)}) collective-permute-start(bf16[8,64,128]{2,1,0:T(8,128)(2,1)} %get-tuple-element.43), channel_id=1, source_target_pairs={{0,32},{32,0},{64,96},{96,64},{128,160},{160,128},{192,224},{224,1... | collective-permute-start | bytes 393224 | tf_op jit(solution)/shard_map/ppermute | solution.py:476
  7.6 4.4 %collective-permute-start.3 = (bf16[560,128]{1,0:T(8,128)(2,1)S(1)}, bf16[560,128]{1,0:T(8,128)(2,1)S(1)}, u32[]{:S(2)}, u32[]{:S(2)}) collective-permute-start(bf16[560,128]{1,0:T(8,128)(2,1)S(1)} %pad_maximum_fusion.refs_0_), channel_id=1, source_target_pairs={{0,192},{32,224},{64,0},{96,32},{128,64},{160,96},{192,128},{224,1... | collective-permute-start | bytes 430088 | tf_op jit(solution)/shard_map/ppermute | solution.py:482
  13.0 2.3 %collective-permute-start.1 = (bf16[560,128]{1,0:T(8,128)(2,1)S(1)}, bf16[560,128]{1,0:T(8,128)(2,1)S(1)}, u32[]{:S(2)}, u32[]{:S(2)}) collective-permute-start(bf16[560,128]{1,0:T(8,128)(2,1)S(1)} %pad_maximum_fusion.refs_0_), channel_id=1, source_target_pairs={{0,64},{32,96},{64,128},{96,160},{128,192},{160,224},{192,0},{224,... | collective-permute-start | bytes 430088 | tf_op jit(solution)/shard_map/ppermute | solution.py:482
  15.3 3.4 %collective-permute-done.3.refs_3_ = bf16[560,128]{1,0:T(8,128)(2,1)S(1)} collective-permute-done((bf16[560,128]{1,0:T(8,128)(2,1)S(1)}, bf16[560,128]{1,0:T(8,128)(2,1)S(1)}, u32[]{:S(2)}, u32[]{:S(2)}) %collective-permute-start.3) | collective-permute-done | bytes 143392 | tf_op jit(solution)/shard_map/ppermute | solution.py:482
  18.7 5.4 %collective-permute-done.2.refs_2_ = bf16[560,128]{1,0:T(8,128)(2,1)S(1)} collective-permute-done((bf16[560,128]{1,0:T(8,128)(2,1)S(1)}, bf16[560,128]{1,0:T(8,128)(2,1)S(1)}, u32[]{:S(2)}, u32[]{:S(2)}) %collective-permute-start.2) | collective-permute-done | bytes 143392 | tf_op jit(solution)/shard_map/ppermute | solution.py:482
  24.1 3.7 %shard_map.111 = (s32[3,4,1,512]{3,2,1,0:T(1,128)S(1)}, f32[3,4,4,128]{3,2,1,0:T(4,128)S(1)}, bf16[4,4,64,128]{3,2,1,0:T(8,128)(2,1)S(1)}, bf16[4,4,64,128]{3,2,...) custom-call(bf16[560,128]{1,0:T(8,128)(2,1)S(1)} %pad_maximum_fusion, ...), custom_call_target="tpu_custom_call" | custom-call | tf_op jit(solution)/shard_map/pallas_call | solution.py:533
  27.8 2.5 %collective-permute-start.4 = (bf16[4,4,64,128]{3,2,1,0:T(8,128)(2,1)S(1)}, bf16[4,4,64,128]{3,2,1,0:T(8,128)(2,1)S(1)}, u32[]{:S(2)}, u32[]{:S(2)}) collective-permute-start(bf16[4,4,64,128]{3,2,1,0:T(8,128)(2,1)S(1)} %get-tuple-element.46), channel_id=1, source_target_pairs={{0,32},{32,0},{64,96},{96,64},{128,160},{160,128},{192,224},{224,1... | collective-permute-start | bytes 786440 | tf_op jit(solution)/shard_map/ppermute | solution.py:476
  31.4 3.7 %shard_map.112 = (bf16[4,4,64,128]{3,2,1,0:T(8,128)(2,1)S(1)}, bf16[4,4,64,128]{3,2,1,0:T(8,128)(2,1)S(1)}, bf16[4,4,128,128]{3,2,1,0:T(8,128)(2,1)S(1)}, bf16[4...) custom-call(bf16[4,4,64,128]{3,2,1,0:T(8,128)(2,1)S(1)} %get-tuple-e, ...), custom_call_target="tpu_custom_call" | custom-call | tf_op jit(solution)/shard_map/pallas_call | solution.py:537
  35.6 3.4 %collective-permute-start.8 = (bf16[512,128]{1,0:T(8,128)(2,1)S(1)}, bf16[512,128]{1,0:T(8,128)(2,1)S(1)}, u32[]{:S(2)}, u32[]{:S(2)}) collective-permute-start(bf16[512,128]{1,0:T(8,128)(2,1)S(1)} %pad_maximum_fusion.1.refs_2_), channel_id=1, source_target_pairs={{0,192},{32,224},{64,0},{96,32},{128,64},{160,96},{192,128},{224,1... | collective-permute-start | bytes 393224 | tf_op jit(solution)/shard_map/ppermute | solution.py:482
  39.0 1.8 %collective-permute-start.7 = (bf16[512,128]{1,0:T(8,128)(2,1)S(1)}, bf16[512,128]{1,0:T(8,128)(2,1)S(1)}, u32[]{:S(2)}, u32[]{:S(2)}) collective-permute-start(bf16[512,128]{1,0:T(8,128)(2,1)S(1)} %pad_maximum_fusion.1.refs_2_), channel_id=1, source_target_pairs={{0,128},{32,160},{64,192},{96,224},{128,0},{160,32},{192,64},{224,... | collective-permute-start | bytes 393224 | tf_op jit(solution)/shard_map/ppermute | solution.py:482
  40.8 2.0 %collective-permute-start.6 = (bf16[512,128]{1,0:T(8,128)(2,1)S(1)}, bf16[512,128]{1,0:T(8,128)(2,1)S(1)}, u32[]{:S(2)}, u32[]{:S(2)}) collective-permute-start(bf16[512,128]{1,0:T(8,128)(2,1)S(1)} %pad_maximum_fusion.1.refs_2_), channel_id=1, source_target_pairs={{0,64},{32,96},{64,128},{96,160},{128,192},{160,224},{192,0},{224,... | collective-permute-start | bytes 393224 | tf_op jit(solution)/shard_map/ppermute | solution.py:482
  42.8 7.1 %collective-permute-done.7.refs_4_ = bf16[512,128]{1,0:T(8,128)(2,1)S(1)} collective-permute-done((bf16[512,128]{1,0:T(8,128)(2,1)S(1)}, bf16[512,128]{1,0:T(8,128)(2,1)S(1)}, u32[]{:S(2)}, u32[]{:S(2)}) %collective-permute-start.7) | collective-permute-done | bytes 131104 | tf_op jit(solution)/shard_map/ppermute | solution.py:482
  50.4 6.7 %shard_map.113 = (bf16[4,4,64,128]{3,2,1,0:T(8,128)(2,1)S(1)}, bf16[4,4,64,128]{3,2,1,0:T(8,128)(2,1)S(1)}, bf16[4,64,128]{2,1,0:T(8,128)(2,1)S(1)}, bf16[4,64,128]{2,1,0:T(8,128)(2,1)S(1)}, f32[144,128]{1,0:T(8,128)S(1)}) custom-call(bf16[4,4,64,128]{3,2,1,0:T(8,128)(2,1)S(1)} %get-tuple-element.49.refs_0_, ...), custom_call_target="tpu_custom_call" | custom-call | tf_op jit(solution)/shard_map/pallas_call | solution.py:540
  57.1 2.0 %collective-permute-start.9 = (bf16[4,4,64,128]{3,2,1,0:T(8,128)(2,1)S(1)}, bf16[4,4,64,128]{3,2,1,0:T(8,128)(2,1)S(1)}, u32[]{:S(2)}, u32[]{:S(2)}) collective-permute-start(bf16[4,4,64,128]{3,2,1,0:T(8,128)(2,1)S(1)} %get-tuple-element.53), channel_id=1, source_target_pairs={{0,32},{32,0},{64,96},{96,64},{128,160},{160,128},{192,224},{224,1... | collective-permute-start | bytes 786440 | tf_op jit(solution)/shard_map/ppermute | solution.py:476
  60.3 4.6 %shard_map.114 = (bf16[4,4,64,128]{3,2,1,0:T(8,128)(2,1)S(1)}, bf16[4,4,64,128]{3,2,1,0:T(8,128)(2,1)S(1)}, f32[144,128]{1,0:T(8,128)S(1)}) custom-call(bf16[4,4,64,128]{3,2,1,0:T(8,128)(2,1)S(1)} %get-tuple-element.52.refs_0_, bf16[4,4,64,128]{3,2,1,0:T(8,128)(2,1)S(1)} %collective-permute-done.9.refs_1_, ...), custom_call_target="tpu_custom_call" | custom-call | tf_op jit(solution)/shard_map/pallas_call | solution.py:545
  66.7 5.0 %shard_map.115 = (bf16[1,512,128]{2,1,0:T(8,128)(2,1)}, bf16[4,64,128]{2,1,0:T(8,128)(2,1)S(1)}, bf16[4,64,128]{2,1,0:T(8,128)(2,1)S(1)}, f32[4,56,128]{2,1,0:T(8,128)S(1)}, f32[4,56,128]{2,1,0:T(8,128)S(1)}) custom-call(bf16[4,4,64,128]{3,2,1,0:T(8,128)(2,1)S(1)} %get-tuple-element.59.refs_0_, bf16[4,4,64,128]{3,2,1,0:T(8,128)(2,1)S(1)} %collective-permute-done.10.refs_1_, ...), custom_call_target="tpu_custom_call" | custom-call | tf_op jit(solution)/shard_map/pallas_call | solution.py:549
  76.0 1.6 %collective-permute-start.14 = (f32[56,128]{1,0:T(8,128)S(1)}, f32[56,128]{1,0:T(8,128)S(1)}, u32[]{:S(2)}, u32[]{:S(2)}) collective-permute-start(f32[56,128]{1,0:T(8,128)S(1)} %get-tuple-element.83), channel_id=1, source_target_pairs={{0,2},{1,3},{2,0},{3,1},{4,6},{5,7},{6,4},{7,5},{8,10},{9,11},{10,... | collective-permute-start | bytes 86024 | tf_op jit(solution)/shard_map/ppermute | solution.py:491
  77.6 2.7 %collective-permute-done.14 = f32[56,128]{1,0:T(8,128)S(1)} collective-permute-done((f32[56,128]{1,0:T(8,128)S(1)}, f32[56,128]{1,0:T(8,128)S(1)}, u32[]{:S(2)}, u32[]{:S(2)}) %collective-permute-start.14) | collective-permute-done | bytes 28704 | tf_op jit(solution)/shard_map/ppermute | solution.py:491
  80.2 2.8 %collective-permute-start.18 = (f32[56,128]{1,0:T(8,128)S(1)}, f32[56,128]{1,0:T(8,128)S(1)}, u32[]{:S(2)}, u32[]{:S(2)}) collective-permute-start(f32[56,128]{1,0:T(8,128)S(1)} %fusion.2), channel_id=1, source_target_pairs={{0,12},{1,13},{2,14},{3,15},{4,0},{5,1},{6,2},{7,3},{8,4},{9,5},{1... | collective-permute-start | bytes 86024 | tf_op jit(solution)/shard_map/ppermute | solution.py:491
  84.1 3.1 %collective-permute-done.17 = f32[56,128]{1,0:T(8,128)S(1)} collective-permute-done((f32[56,128]{1,0:T(8,128)S(1)}, f32[56,128]{1,0:T(8,128)S(1)}, u32[]{:S(2)}, u32[]{:S(2)}) %collective-permute-start.17) | collective-permute-done | bytes 28704 | tf_op jit(solution)/shard_map/ppermute | solution.py:491
  87.6 3.7 %collective-permute-start.19 = (f32[56,128]{1,0:T(8,128)S(1)}, f32[56,128]{1,0:T(8,128)S(1)}, u32[]{:S(2)}, u32[]{:S(2)}) collective-permute-start(f32[56,128]{1,0:T(8,128)S(1)} %add_add_fusion), channel_id=1, source_target_pairs={{0,16},{1,17},{2,18},{3,19},{4,20},{5,21},{6,22},{7,23},{8,24},{9,... | collective-permute-start | bytes 86024 | tf_op jit(solution)/shard_map/ppermute | solution.py:491
  95.2 2.9 %collective-permute-done.21 = f32[56,128]{1,0:T(8,128)S(1)} collective-permute-done((f32[56,128]{1,0:T(8,128)S(1)}, f32[56,128]{1,0:T(8,128)S(1)}, u32[]{:S(2)}, u32[]{:S(2)}) %collective-permute-start.21) | collective-permute-done | bytes 28704 | tf_op jit(solution)/shard_map/ppermute | solution.py:491
  98.4 6.1 %collective-permute-start.23 = (f32[4,56,128]{2,1,0:T(8,128)S(1)}, f32[4,56,128]{2,1,0:T(8,128)S(1)}, u32[]{:S(2)}, u32[]{:S(2)}) collective-permute-start(f32[4,56,128]{2,1,0:T(8,128)S(1)} %pad_maximum_fusion.2.own_ref), channel_id=1, source_target_pairs={{0,32},{32,0},{64,96},{96,64},{128,160},{160,128},{192,224},{224,1... | collective-permute-start | bytes 344072 | tf_op jit(solution)/shard_map/ppermute | solution.py:476
  (54 shorter events, 20.1 us)
Async XLA Ops:
  2.4 4.5 %collective-permute-start = (bf16[8,64,128]{2,1,0:T(8,128)(2,1)}, bf16[8,64,128]{2,1,0:T(8,128)(2,1)S(1)}, u32[]{:S(2)}, u32[]{:S(2)}) collective-permute-start(bf16[8,64,128]{2,1,0:T(8,128)(2,1)} %get-tuple-element.43), channel_id=1, source_target_pairs={{0,32},{32,0},{64,96},{96,64},{128,160},{160,128},{192,224},{224,1... | collective-permute-start | bytes 393224 | tf_op jit(solution)/shard_map/ppermute | solution.py:476
  7.6 11.0 %collective-permute-start.3 = (bf16[560,128]{1,0:T(8,128)(2,1)S(1)}, bf16[560,128]{1,0:T(8,128)(2,1)S(1)}, u32[]{:S(2)}, u32[]{:S(2)}) collective-permute-start(bf16[560,128]{1,0:T(8,128)(2,1)S(1)} %pad_maximum_fusion.refs_0_), channel_id=1, source_target_pairs={{0,192},{32,224},{64,0},{96,32},{128,64},{160,96},{192,128},{224,1... | collective-permute-start | bytes 430088 | tf_op jit(solution)/shard_map/ppermute | solution.py:482
  12.0 12.1 %collective-permute-start.2 = (bf16[560,128]{1,0:T(8,128)(2,1)S(1)}, bf16[560,128]{1,0:T(8,128)(2,1)S(1)}, u32[]{:S(2)}, u32[]{:S(2)}) collective-permute-start(bf16[560,128]{1,0:T(8,128)(2,1)S(1)} %pad_maximum_fusion.refs_0_), channel_id=1, source_target_pairs={{0,128},{32,160},{64,192},{96,224},{128,0},{160,32},{192,64},{224,... | collective-permute-start | bytes 430088 | tf_op jit(solution)/shard_map/ppermute | solution.py:482
  13.0 11.1 %collective-permute-start.1 = (bf16[560,128]{1,0:T(8,128)(2,1)S(1)}, bf16[560,128]{1,0:T(8,128)(2,1)S(1)}, u32[]{:S(2)}, u32[]{:S(2)}) collective-permute-start(bf16[560,128]{1,0:T(8,128)(2,1)S(1)} %pad_maximum_fusion.refs_0_), channel_id=1, source_target_pairs={{0,64},{32,96},{64,128},{96,160},{128,192},{160,224},{192,0},{224,... | collective-permute-start | bytes 430088 | tf_op jit(solution)/shard_map/ppermute | solution.py:482
  27.8 3.6 %collective-permute-start.4 = (bf16[4,4,64,128]{3,2,1,0:T(8,128)(2,1)S(1)}, bf16[4,4,64,128]{3,2,1,0:T(8,128)(2,1)S(1)}, u32[]{:S(2)}, u32[]{:S(2)}) collective-permute-start(bf16[4,4,64,128]{3,2,1,0:T(8,128)(2,1)S(1)} %get-tuple-element.46), channel_id=1, source_target_pairs={{0,32},{32,0},{64,96},{96,64},{128,160},{160,128},{192,224},{224,1... | collective-permute-start | bytes 786440 | tf_op jit(solution)/shard_map/ppermute | solution.py:476
  35.1 15.3 %collective-permute-start.5 = (bf16[4,4,64,128]{3,2,1,0:T(8,128)(2,1)S(1)}, bf16[4,4,64,128]{3,2,1,0:T(8,128)(2,1)S(1)}, u32[]{:S(2)}, u32[]{:S(2)}) collective-permute-start(bf16[4,4,64,128]{3,2,1,0:T(8,128)(2,1)S(1)} %get-tuple-element.50), channel_id=1, source_target_pairs={{0,32},{32,0},{64,96},{96,64},{128,160},{160,128},{192,224},{224,1... | collective-permute-start | bytes 786440 | tf_op jit(solution)/shard_map/ppermute | solution.py:476
  35.6 7.2 %collective-permute-start.8 = (bf16[512,128]{1,0:T(8,128)(2,1)S(1)}, bf16[512,128]{1,0:T(8,128)(2,1)S(1)}, u32[]{:S(2)}, u32[]{:S(2)}) collective-permute-start(bf16[512,128]{1,0:T(8,128)(2,1)S(1)} %pad_maximum_fusion.1.refs_2_), channel_id=1, source_target_pairs={{0,192},{32,224},{64,0},{96,32},{128,64},{160,96},{192,128},{224,1... | collective-permute-start | bytes 393224 | tf_op jit(solution)/shard_map/ppermute | solution.py:482
  39.0 10.9 %collective-permute-start.7 = (bf16[512,128]{1,0:T(8,128)(2,1)S(1)}, bf16[512,128]{1,0:T(8,128)(2,1)S(1)}, u32[]{:S(2)}, u32[]{:S(2)}) collective-permute-start(bf16[512,128]{1,0:T(8,128)(2,1)S(1)} %pad_maximum_fusion.1.refs_2_), channel_id=1, source_target_pairs={{0,128},{32,160},{64,192},{96,224},{128,0},{160,32},{192,64},{224,... | collective-permute-start | bytes 393224 | tf_op jit(solution)/shard_map/ppermute | solution.py:482
  40.8 9.6 %collective-permute-start.6 = (bf16[512,128]{1,0:T(8,128)(2,1)S(1)}, bf16[512,128]{1,0:T(8,128)(2,1)S(1)}, u32[]{:S(2)}, u32[]{:S(2)}) collective-permute-start(bf16[512,128]{1,0:T(8,128)(2,1)S(1)} %pad_maximum_fusion.1.refs_2_), channel_id=1, source_target_pairs={{0,64},{32,96},{64,128},{96,160},{128,192},{160,224},{192,0},{224,... | collective-permute-start | bytes 393224 | tf_op jit(solution)/shard_map/ppermute | solution.py:482
  57.1 3.2 %collective-permute-start.9 = (bf16[4,4,64,128]{3,2,1,0:T(8,128)(2,1)S(1)}, bf16[4,4,64,128]{3,2,1,0:T(8,128)(2,1)S(1)}, u32[]{:S(2)}, u32[]{:S(2)}) collective-permute-start(bf16[4,4,64,128]{3,2,1,0:T(8,128)(2,1)S(1)} %get-tuple-element.53), channel_id=1, source_target_pairs={{0,32},{32,0},{64,96},{96,64},{128,160},{160,128},{192,224},{224,1... | collective-permute-start | bytes 786440 | tf_op jit(solution)/shard_map/ppermute | solution.py:476
  65.0 1.7 %collective-permute-start.10 = (bf16[4,4,64,128]{3,2,1,0:T(8,128)(2,1)S(1)}, bf16[4,4,64,128]{3,2,1,0:T(8,128)(2,1)S(1)}, u32[]{:S(2)}, u32[]{:S(2)}) collective-permute-start(bf16[4,4,64,128]{3,2,1,0:T(8,128)(2,1)S(1)} %get-tuple-element.60), channel_id=1, source_target_pairs={{0,32},{32,0},{64,96},{96,64},{128,160},{160,128},{192,224},{224,1... | collective-permute-start | bytes 786440 | tf_op jit(solution)/shard_map/ppermute | solution.py:476
  65.4 1.3 %collective-permute-start.11 = (bf16[4,64,128]{2,1,0:T(8,128)(2,1)S(1)}, bf16[4,64,128]{2,1,0:T(8,128)(2,1)S(1)}, u32[]{:S(2)}, u32[]{:S(2)}) collective-permute-start(bf16[4,64,128]{2,1,0:T(8,128)(2,1)S(1)} %get-tuple-element.69), channel_id=1, source_target_pairs={{0,32},{32,0},{64,96},{96,64},{128,160},{160,128},{192,224},{224,1... | collective-permute-start | bytes 196616 | tf_op jit(solution)/shard_map/ppermute | solution.py:476
  71.7 1.3 %collective-permute-start.12 = (f32[4,56,128]{2,1,0:T(8,128)S(1)}, f32[4,56,128]{2,1,0:T(8,128)S(1)}, u32[]{:S(2)}, u32[]{:S(2)}) collective-permute-start(f32[4,56,128]{2,1,0:T(8,128)S(1)} %get-tuple-element.72), channel_id=1, source_target_pairs={{0,32},{32,0},{64,96},{96,64},{128,160},{160,128},{192,224},{224,1... | collective-permute-start | bytes 344072 | tf_op jit(solution)/shard_map/ppermute | solution.py:476
  73.1 4.5 %collective-permute-start.13 = (f32[56,128]{1,0:T(8,128)S(1)}, f32[56,128]{1,0:T(8,128)S(1)}, u32[]{:S(2)}, u32[]{:S(2)}) collective-permute-start(f32[56,128]{1,0:T(8,128)S(1)} %get-tuple-element.81), channel_id=1, source_target_pairs={{0,1},{1,2},{2,3},{3,0},{4,5},{5,6},{6,7},{7,4},{8,9},{9,10},{10,1... | collective-permute-start | bytes 86024 | tf_op jit(solution)/shard_map/ppermute | solution.py:491
  74.5 3.1 %collective-permute-start.15 = (f32[56,128]{1,0:T(8,128)S(1)}, f32[56,128]{1,0:T(8,128)S(1)}, u32[]{:S(2)}, u32[]{:S(2)}) collective-permute-start(f32[56,128]{1,0:T(8,128)S(1)} %get-tuple-element.82), channel_id=1, source_target_pairs={{0,3},{1,0},{2,1},{3,2},{4,7},{5,4},{6,5},{7,6},{8,11},{9,8},{10,9... | collective-permute-start | bytes 86024 | tf_op jit(solution)/shard_map/ppermute | solution.py:491
  76.0 4.2 %collective-permute-start.14 = (f32[56,128]{1,0:T(8,128)S(1)}, f32[56,128]{1,0:T(8,128)S(1)}, u32[]{:S(2)}, u32[]{:S(2)}) collective-permute-start(f32[56,128]{1,0:T(8,128)S(1)} %get-tuple-element.83), channel_id=1, source_target_pairs={{0,2},{1,3},{2,0},{3,1},{4,6},{5,7},{6,4},{7,5},{8,10},{9,11},{10,... | collective-permute-start | bytes 86024 | tf_op jit(solution)/shard_map/ppermute | solution.py:491
  80.2 3.9 %collective-permute-start.18 = (f32[56,128]{1,0:T(8,128)S(1)}, f32[56,128]{1,0:T(8,128)S(1)}, u32[]{:S(2)}, u32[]{:S(2)}) collective-permute-start(f32[56,128]{1,0:T(8,128)S(1)} %fusion.2), channel_id=1, source_target_pairs={{0,12},{1,13},{2,14},{3,15},{4,0},{5,1},{6,2},{7,3},{8,4},{9,5},{1... | collective-permute-start | bytes 86024 | tf_op jit(solution)/shard_map/ppermute | solution.py:491
  83.0 4.2 %collective-permute-start.17 = (f32[56,128]{1,0:T(8,128)S(1)}, f32[56,128]{1,0:T(8,128)S(1)}, u32[]{:S(2)}, u32[]{:S(2)}) collective-permute-start(f32[56,128]{1,0:T(8,128)S(1)} %fusion.2), channel_id=1, source_target_pairs={{0,8},{1,9},{2,10},{3,11},{4,12},{5,13},{6,14},{7,15},{8,0},{9,1},... | collective-permute-start | bytes 86024 | tf_op jit(solution)/shard_map/ppermute | solution.py:491
  83.5 4.0 %collective-permute-start.16 = (f32[56,128]{1,0:T(8,128)S(1)}, f32[56,128]{1,0:T(8,128)S(1)}, u32[]{:S(2)}, u32[]{:S(2)}) collective-permute-start(f32[56,128]{1,0:T(8,128)S(1)} %fusion.2), channel_id=1, source_target_pairs={{0,4},{1,5},{2,6},{3,7},{4,8},{5,9},{6,10},{7,11},{8,12},{9,13},{1... | collective-permute-start | bytes 86024 | tf_op jit(solution)/shard_map/ppermute | solution.py:491
  87.6 5.0 %collective-permute-start.19 = (f32[56,128]{1,0:T(8,128)S(1)}, f32[56,128]{1,0:T(8,128)S(1)}, u32[]{:S(2)}, u32[]{:S(2)}) collective-permute-start(f32[56,128]{1,0:T(8,128)S(1)} %add_add_fusion), channel_id=1, source_target_pairs={{0,16},{1,17},{2,18},{3,19},{4,20},{5,21},{6,22},{7,23},{8,24},{9,... | collective-permute-start | bytes 86024 | tf_op jit(solution)/shard_map/ppermute | solution.py:491
  92.5 2.7 %collective-permute-start.22 = (f32[56,128]{1,0:T(8,128)S(1)}, f32[56,128]{1,0:T(8,128)S(1)}, u32[]{:S(2)}, u32[]{:S(2)}) collective-permute-start(f32[56,128]{1,0:T(8,128)S(1)} %add_multiply_fusion), channel_id=1, source_target_pairs={{0,3},{1,0},{2,1},{3,2},{4,7},{5,4},{6,5},{7,6},{8,11},{9,8},{10,9... | collective-permute-start | bytes 86024 | tf_op jit(solution)/shard_map/ppermute | solution.py:491
  93.9 4.2 %collective-permute-start.21 = (f32[56,128]{1,0:T(8,128)S(1)}, f32[56,128]{1,0:T(8,128)S(1)}, u32[]{:S(2)}, u32[]{:S(2)}) collective-permute-start(f32[56,128]{1,0:T(8,128)S(1)} %add_multiply_fusion), channel_id=1, source_target_pairs={{0,2},{1,3},{2,0},{3,1},{4,6},{5,7},{6,4},{7,5},{8,10},{9,11},{10,... | collective-permute-start | bytes 86024 | tf_op jit(solution)/shard_map/ppermute | solution.py:491
  94.4 4.0 %collective-permute-start.20 = (f32[56,128]{1,0:T(8,128)S(1)}, f32[56,128]{1,0:T(8,128)S(1)}, u32[]{:S(2)}, u32[]{:S(2)}) collective-permute-start(f32[56,128]{1,0:T(8,128)S(1)} %add_multiply_fusion), channel_id=1, source_target_pairs={{0,1},{1,2},{2,3},{3,0},{4,5},{5,6},{6,7},{7,4},{8,9},{9,10},{10,1... | collective-permute-start | bytes 86024 | tf_op jit(solution)/shard_map/ppermute | solution.py:491
  98.4 7.4 %collective-permute-start.23 = (f32[4,56,128]{2,1,0:T(8,128)S(1)}, f32[4,56,128]{2,1,0:T(8,128)S(1)}, u32[]{:S(2)}, u32[]{:S(2)}) collective-permute-start(f32[4,56,128]{2,1,0:T(8,128)S(1)} %pad_maximum_fusion.2.own_ref), channel_id=1, source_target_pairs={{0,32},{32,0},{64,96},{96,64},{128,160},{160,128},{192,224},{224,1... | collective-permute-start | bytes 344072 | tf_op jit(solution)/shard_map/ppermute | solution.py:476
  (7 other events, 60.0 us)

commit v7 on v6

--- a/solution.py
+++ b/solution.py
@@ -357,23 +357,18 @@
     end_sums(sum_ref, rows_ref)
 
 
-def ring_of():
-    return jnp.bitwise_and(lax.axis_index("dp"), RING - 1)
-
-
 def share_out(sum_refs, small_ref, keep_ref, send_ref):
     _, core = place_of()
-    here = ring_of()
     for r in range(NL):
         for k, ref in enumerate(sum_refs):
             small_ref[r, 2 * k : 2 * k + 2, :] = ref[CH + 2 * r : CH + 2 * r + 2, :]
         small_ref[r, 6:8, :] = jnp.zeros((2, CH), F32)
     for side, out in ((core, keep_ref), (1 - core, send_ref)):
-        for ahead in range(RING):
-            r = 2 * jnp.bitwise_and(here + ahead, RING - 1) + side
+        for piece in range(CHIPS):
+            r = 2 * piece + side
             for k, ref in enumerate(sum_refs):
-                out[ahead, k * 16 : (k + 1) * 16, :] = ref[pl.ds(pl.multiple_of(r * 16, 16), 16), :]
-            out[ahead, 48:SHARE, :] = small_ref[r]
+                out[piece, k * 16 : (k + 1) * 16, :] = ref[pl.ds(pl.multiple_of(r * 16, 16), 16), :]
+            out[piece, 48:SHARE, :] = small_ref[r]
 
 
 def backward_kernel(k, *refs):
@@ -436,16 +431,15 @@
 
 def finish_kernel(own_ref, other_ref, grad_ref, home_ref, mix_ref, taps_ref, gain_ref, out_ref, tail_ref):
     _, core = place_of()
-    here = ring_of()
     for m in range(CHIPS):
         for ref, b in ((grad_ref, 2 * m + core), (home_ref, 2 * m + 1 - core)):
             out_ref[0, pl.ds(pl.multiple_of(b * Q, Q), Q), :] = ref[m]
     for ref, side in ((own_ref, core), (other_ref, 1 - core)):
-        for back in range(RING):
-            r = 2 * jnp.bitwise_and(here - back + RING, RING - 1) + side
+        for piece in range(CHIPS):
+            r = 2 * piece + side
             for k in range(3):
-                mix_ref[k, pl.ds(pl.multiple_of(r * 16, 16), 16), :] = ref[back, k * 16 : (k + 1) * 16, :]
-            tail_ref[r] = ref[back, 48:SHARE, :]
+                mix_ref[k, pl.ds(pl.multiple_of(r * 16, 16), 16), :] = ref[piece, k * 16 : (k + 1) * 16, :]
+            tail_ref[r] = ref[piece, 48:SHARE, :]
     for k in range(3):
         for r in range(NL):
             pair = tail_ref[r, 2 * k : 2 * k + 2, :]
@@ -491,13 +485,15 @@
     return lax.ppermute(values, "dp", pairs)
 
 
-def sum_over_dp(parts):
+def sum_over_dp(part):
     size = lax.axis_size("dp")
-    part = sum([to_ring(parts[turn], turn, RING, 1) for turn in range(1, RING)], parts[0])
-    stride = RING
+    stride = 1
     while stride < size:
         ring = RING if size % (stride * RING) == 0 else 2
-        part = sum([to_ring(part, turn, ring, stride) for turn in range(1, ring)], part)
+        own = lax.reduce_precision(part, exponent_bits=8, mantissa_bits=7)
+        sent = own.astype(BF16)
+        got = [to_ring(sent, turn, ring, stride).astype(F32) for turn in range(1, ring)]
+        part = own + got[0] if ring == 2 else (own + got[1]) + (got[0] + got[2])
         stride *= ring
     return part
 
@@ -545,7 +541,7 @@
     same, moved, sums1 = call(
         functools.partial(backward_kernel, 1), (moving, moving, sums), 12, scratch=back
     )(same, moved, *saved1, *given)
-    share = shape(RING, SHARE, CH, dtype=F32)
+    share = shape(CHIPS, SHARE, CH, dtype=F32)
     imitated, own, home, keep, send = call(
         functools.partial(backward_kernel, 0),
         (shape(1, CELLS, CH), quarter, quarter, share, share),
@@ -555,8 +551,7 @@
     grad_scale = float(dp_size * NL * CELLS) ** (-0.5)
     got = swap(send)
     home = swap(home)
-    part = sum_over_dp(keep + got) * grad_scale
-    shares = jnp.stack([part] + [to_ring(part, turn, RING, 1) for turn in range(1, RING)])
+    shares = sum_over_dp(keep + got) * grad_scale
     mix_grad, kernel_grad, gain_grad, field_grad = call(
         finish_kernel,
         (

time: 107 us -> 100 us (0.935)
  starting transfers between devices: 44.8 us -> 41.2 us
  waiting for transfers between devices: 34 us -> 31.2 us
    ppermute x10 -> x7, waiting for transfers between devices: 10.8 us -> 7.98 us  [to_ring(): return lax.ppermute(values, 'dp', pairs)]
    ppermute x9, starting transfers between devices: 15.5 us -> 13.6 us  [swap(): return lax.ppermute(values, 'line', [(i, i ^ 1) for i in range(NL)])]
    ppermute x10 -> x7, starting transfers between devices: 14.5 us -> 12.7 us  [to_ring(): return lax.ppermute(values, 'dp', pairs)]
  transfers between devices with their start and end apart: 25 -> 22, of which waited for: 17 -> 14; matrix products, arithmetic and copies ran while one was open for 0% -> 0% of each run, Pallas kernels for 0% -> 0%
where the time goes in v7:
time: 100 us
  starting transfers between devices  41.2 us (41%)
  waiting for transfers between devices  31.2 us (31%)
  Pallas kernels  26.2 us (26%)
    ppermute x6, waiting for transfers between devices, from_chips(): lax.ppermute(values, 'line', [(i, (i + 2 * back) % NL) for i in range(NL)])  16.4 us
    ppermute x6, starting transfers between devices, from_chips(): lax.ppermute(values, 'line', [(i, (i + 2 * back) % NL) for i in range(NL)])  14.9 us
    ppermute x9, starting transfers between devices, swap(): return lax.ppermute(values, 'line', [(i, i ^ 1) for i in range(NL)])  13.6 us
    ppermute x7, starting transfers between devices, to_ring(): return lax.ppermute(values, 'dp', pairs)  12.7 us
    ppermute x7, waiting for transfers between devices, to_ring(): return lax.ppermute(values, 'dp', pairs)  7.98 us
    ppermute x9, waiting for transfers between devices, swap(): return lax.ppermute(values, 'line', [(i, i ^ 1) for i in range(NL)])  6.77 us
    pallas_call x1, Pallas kernels, block(): call(turn_kernel, (moving, moving, quarter, quarter, sums), 11, scratch=(...  6.7 us
    pallas_call x1, Pallas kernels, block(): call(functools.partial(backward_kernel, 0), (shape(1, CELLS, CH), quarter...  5.01 us
  transfers between devices with their start and end apart: 22, of which 14 were waited for; matrix products, arithmetic and copies ran while one was open for 0% of the time, Pallas kernels for 0%

profile of v7, /device:TPU:1, one launch (start us, length us, event | category | flops | bytes accessed | tf_op | source)
XLA Modules:
  0.0 100.2 jit_solution(6761960634698929986)
XLA Ops:
  0.6 1.8 %shard_map.110 = (bf16[4,64,128]{2,1,0:T(8,128)(2,1)}, bf16[4,64,128]{2,1,0:T(8,128)(2,1)}, bf16[8,64,128]{2,1,0:T(8,128)(2,1)}, bf16[48,128]{1,0:T(8,128)(2,1)}) custom-call(bf16[1,512,128]{2,1,0:T(8,128)(2,1)} %fields_ref.1, bf16[1,512,128]{2,1,0:T(8,128)(2,1)} %cot_ref.1, s32[3,512]{1,0:T(4,128)} %table_ref.1, s32[3,4]{1,0:T(4,128)} %begin_ref.1), custom_call_target="tpu_custom_call" | custom-call | tf_op jit(solution)/shard_map/pallas_call | solution.py:516
  2.4 3.3 %collective-permute-start = (bf16[8,64,128]{2,1,0:T(8,128)(2,1)}, bf16[8,64,128]{2,1,0:T(8,128)(2,1)S(1)}, u32[]{:S(2)}, u32[]{:S(2)}) collective-permute-start(bf16[8,64,128]{2,1,0:T(8,128)(2,1)} %get-tuple-element.43), channel_id=1, source_target_pairs={{0,32},{32,0},{64,96},{96,64},{128,160},{160,128},{192,224},{224,1... | collective-permute-start | bytes 393224 | tf_op jit(solution)/shard_map/ppermute | solution.py:470
  7.6 4.4 %collective-permute-start.3 = (bf16[560,128]{1,0:T(8,128)(2,1)S(1)}, bf16[560,128]{1,0:T(8,128)(2,1)S(1)}, u32[]{:S(2)}, u32[]{:S(2)}) collective-permute-start(bf16[560,128]{1,0:T(8,128)(2,1)S(1)} %pad_maximum_fusion.refs_0_), channel_id=1, source_target_pairs={{0,192},{32,224},{64,0},{96,32},{128,64},{160,96},{192,128},{224,1... | collective-permute-start | bytes 430088 | tf_op jit(solution)/shard_map/ppermute | solution.py:476
  13.0 2.3 %collective-permute-start.1 = (bf16[560,128]{1,0:T(8,128)(2,1)S(1)}, bf16[560,128]{1,0:T(8,128)(2,1)S(1)}, u32[]{:S(2)}, u32[]{:S(2)}) collective-permute-start(bf16[560,128]{1,0:T(8,128)(2,1)S(1)} %pad_maximum_fusion.refs_0_), channel_id=1, source_target_pairs={{0,64},{32,96},{64,128},{96,160},{128,192},{160,224},{192,0},{224,... | collective-permute-start | bytes 430088 | tf_op jit(solution)/shard_map/ppermute | solution.py:476
  15.3 3.4 %collective-permute-done.3.refs_3_ = bf16[560,128]{1,0:T(8,128)(2,1)S(1)} collective-permute-done((bf16[560,128]{1,0:T(8,128)(2,1)S(1)}, bf16[560,128]{1,0:T(8,128)(2,1)S(1)}, u32[]{:S(2)}, u32[]{:S(2)}) %collective-permute-start.3) | collective-permute-done | bytes 143392 | tf_op jit(solution)/shard_map/ppermute | solution.py:476
  18.7 5.4 %collective-permute-done.2.refs_2_ = bf16[560,128]{1,0:T(8,128)(2,1)S(1)} collective-permute-done((bf16[560,128]{1,0:T(8,128)(2,1)S(1)}, bf16[560,128]{1,0:T(8,128)(2,1)S(1)}, u32[]{:S(2)}, u32[]{:S(2)}) %collective-permute-start.2) | collective-permute-done | bytes 143392 | tf_op jit(solution)/shard_map/ppermute | solution.py:476
  24.1 3.7 %shard_map.111 = (s32[3,4,1,512]{3,2,1,0:T(1,128)S(1)}, f32[3,4,4,128]{3,2,1,0:T(4,128)S(1)}, bf16[4,4,64,128]{3,2,1,0:T(8,128)(2,1)S(1)}, bf16[4,4,64,128]{3,2,...) custom-call(bf16[560,128]{1,0:T(8,128)(2,1)S(1)} %pad_maximum_fusion, ...), custom_call_target="tpu_custom_call" | custom-call | tf_op jit(solution)/shard_map/pallas_call | solution.py:529
  27.8 2.5 %collective-permute-start.4 = (bf16[4,4,64,128]{3,2,1,0:T(8,128)(2,1)S(1)}, bf16[4,4,64,128]{3,2,1,0:T(8,128)(2,1)S(1)}, u32[]{:S(2)}, u32[]{:S(2)}) collective-permute-start(bf16[4,4,64,128]{3,2,1,0:T(8,128)(2,1)S(1)} %get-tuple-element.46), channel_id=1, source_target_pairs={{0,32},{32,0},{64,96},{96,64},{128,160},{160,128},{192,224},{224,1... | collective-permute-start | bytes 786440 | tf_op jit(solution)/shard_map/ppermute | solution.py:470
  31.4 3.7 %shard_map.112 = (bf16[4,4,64,128]{3,2,1,0:T(8,128)(2,1)S(1)}, bf16[4,4,64,128]{3,2,1,0:T(8,128)(2,1)S(1)}, bf16[4,4,128,128]{3,2,1,0:T(8,128)(2,1)S(1)}, bf16[4...) custom-call(bf16[4,4,64,128]{3,2,1,0:T(8,128)(2,1)S(1)} %get-tuple-e, ...), custom_call_target="tpu_custom_call" | custom-call | tf_op jit(solution)/shard_map/pallas_call | solution.py:533
  35.6 3.4 %collective-permute-start.8 = (bf16[512,128]{1,0:T(8,128)(2,1)S(1)}, bf16[512,128]{1,0:T(8,128)(2,1)S(1)}, u32[]{:S(2)}, u32[]{:S(2)}) collective-permute-start(bf16[512,128]{1,0:T(8,128)(2,1)S(1)} %pad_maximum_fusion.1.refs_2_), channel_id=1, source_target_pairs={{0,192},{32,224},{64,0},{96,32},{128,64},{160,96},{192,128},{224,1... | collective-permute-start | bytes 393224 | tf_op jit(solution)/shard_map/ppermute | solution.py:476
  39.0 1.8 %collective-permute-start.7 = (bf16[512,128]{1,0:T(8,128)(2,1)S(1)}, bf16[512,128]{1,0:T(8,128)(2,1)S(1)}, u32[]{:S(2)}, u32[]{:S(2)}) collective-permute-start(bf16[512,128]{1,0:T(8,128)(2,1)S(1)} %pad_maximum_fusion.1.refs_2_), channel_id=1, source_target_pairs={{0,128},{32,160},{64,192},{96,224},{128,0},{160,32},{192,64},{224,... | collective-permute-start | bytes 393224 | tf_op jit(solution)/shard_map/ppermute | solution.py:476
  40.8 2.0 %collective-permute-start.6 = (bf16[512,128]{1,0:T(8,128)(2,1)S(1)}, bf16[512,128]{1,0:T(8,128)(2,1)S(1)}, u32[]{:S(2)}, u32[]{:S(2)}) collective-permute-start(bf16[512,128]{1,0:T(8,128)(2,1)S(1)} %pad_maximum_fusion.1.refs_2_), channel_id=1, source_target_pairs={{0,64},{32,96},{64,128},{96,160},{128,192},{160,224},{192,0},{224,... | collective-permute-start | bytes 393224 | tf_op jit(solution)/shard_map/ppermute | solution.py:476
  42.8 7.1 %collective-permute-done.7.refs_4_ = bf16[512,128]{1,0:T(8,128)(2,1)S(1)} collective-permute-done((bf16[512,128]{1,0:T(8,128)(2,1)S(1)}, bf16[512,128]{1,0:T(8,128)(2,1)S(1)}, u32[]{:S(2)}, u32[]{:S(2)}) %collective-permute-start.7) | collective-permute-done | bytes 131104 | tf_op jit(solution)/shard_map/ppermute | solution.py:476
  50.4 6.7 %shard_map.113 = (bf16[4,4,64,128]{3,2,1,0:T(8,128)(2,1)S(1)}, bf16[4,4,64,128]{3,2,1,0:T(8,128)(2,1)S(1)}, bf16[4,64,128]{2,1,0:T(8,128)(2,1)S(1)}, bf16[4,64,128]{2,1,0:T(8,128)(2,1)S(1)}, f32[144,128]{1,0:T(8,128)S(1)}) custom-call(bf16[4,4,64,128]{3,2,1,0:T(8,128)(2,1)S(1)} %get-tuple-element.49.refs_0_, ...), custom_call_target="tpu_custom_call" | custom-call | tf_op jit(solution)/shard_map/pallas_call | solution.py:536
  57.1 2.0 %collective-permute-start.9 = (bf16[4,4,64,128]{3,2,1,0:T(8,128)(2,1)S(1)}, bf16[4,4,64,128]{3,2,1,0:T(8,128)(2,1)S(1)}, u32[]{:S(2)}, u32[]{:S(2)}) collective-permute-start(bf16[4,4,64,128]{3,2,1,0:T(8,128)(2,1)S(1)} %get-tuple-element.53), channel_id=1, source_target_pairs={{0,32},{32,0},{64,96},{96,64},{128,160},{160,128},{192,224},{224,1... | collective-permute-start | bytes 786440 | tf_op jit(solution)/shard_map/ppermute | solution.py:470
  60.3 4.6 %shard_map.114 = (bf16[4,4,64,128]{3,2,1,0:T(8,128)(2,1)S(1)}, bf16[4,4,64,128]{3,2,1,0:T(8,128)(2,1)S(1)}, f32[144,128]{1,0:T(8,128)S(1)}) custom-call(bf16[4,4,64,128]{3,2,1,0:T(8,128)(2,1)S(1)} %get-tuple-element.52.refs_0_, bf16[4,4,64,128]{3,2,1,0:T(8,128)(2,1)S(1)} %collective-permute-done.9.refs_1_, ...), custom_call_target="tpu_custom_call" | custom-call | tf_op jit(solution)/shard_map/pallas_call | solution.py:541
  66.7 5.0 %shard_map.115 = (bf16[1,512,128]{2,1,0:T(8,128)(2,1)}, bf16[4,64,128]{2,1,0:T(8,128)(2,1)S(1)}, bf16[4,64,128]{2,1,0:T(8,128)(2,1)S(1)}, f32[4,56,128]{2,1,0:T(8,128)S(1)}, f32[4,56,128]{2,1,0:T(8,128)S(1)}) custom-call(bf16[4,4,64,128]{3,2,1,0:T(8,128)(2,1)S(1)} %get-tuple-element.59.refs_0_, bf16[4,4,64,128]{3,2,1,0:T(8,128)(2,1)S(1)} %collective-permute-done.10.refs_1_, ...), custom_call_target="tpu_custom_call" | custom-call | tf_op jit(solution)/shard_map/pallas_call | solution.py:545
  73.1 2.8 %collective-permute-start.15 = (bf16[4,56,128]{2,1,0:T(8,128)(2,1)S(1)}, bf16[4,56,128]{2,1,0:T(8,128)(2,1)S(1)}, u32[]{:S(2)}, u32[]{:S(2)}) collective-permute-start(bf16[4,56,128]{2,1,0:T(8,128)(2,1)S(1)} %fusion), channel_id=1, source_target_pairs={{0,3},{1,0},{2,1},{3,2},{4,7},{5,4},{6,5},{7,6},{8,11},{9,8},{10,9... | collective-permute-start | bytes 172040 | tf_op jit(solution)/shard_map/ppermute | solution.py:485
  77.5 2.9 %collective-permute-done.14 = bf16[4,56,128]{2,1,0:T(8,128)(2,1)S(1)} collective-permute-done((bf16[4,56,128]{2,1,0:T(8,128)(2,1)S(1)}, bf16[4,56,128]{2,1,0:T(8,128)(2,1)S(1)}, u32[]{:S(2)}, u32[]{:S(2)}) %collective-permute-start.14) | collective-permute-done | bytes 57376 | tf_op jit(solution)/shard_map/ppermute | solution.py:485
  80.9 2.8 %collective-permute-start.18 = (bf16[4,56,128]{2,1,0:T(8,128)(2,1)S(1)}, bf16[4,56,128]{2,1,0:T(8,128)(2,1)S(1)}, u32[]{:S(2)}, u32[]{:S(2)}) collective-permute-start(bf16[4,56,128]{2,1,0:T(8,128)(2,1)S(1)} %get-tuple-element.79), channel_id=1, source_target_pairs={{0,12},{1,13},{2,14},{3,15},{4,0},{5,1},{6,2},{7,3},{8,4},{9,5},{1... | collective-permute-start | bytes 172040 | tf_op jit(solution)/shard_map/ppermute | solution.py:485
  83.6 1.7 %collective-permute-start.16 = (bf16[4,56,128]{2,1,0:T(8,128)(2,1)S(1)}, bf16[4,56,128]{2,1,0:T(8,128)(2,1)S(1)}, u32[]{:S(2)}, u32[]{:S(2)}) collective-permute-start(bf16[4,56,128]{2,1,0:T(8,128)(2,1)S(1)} %get-tuple-element.79), channel_id=1, source_target_pairs={{0,8},{1,9},{2,10},{3,11},{4,12},{5,13},{6,14},{7,15},{8,0},{9,1},... | collective-permute-start | bytes 172040 | tf_op jit(solution)/shard_map/ppermute | solution.py:485
  85.4 3.1 %collective-permute-done.17 = bf16[4,56,128]{2,1,0:T(8,128)(2,1)S(1)} collective-permute-done((bf16[4,56,128]{2,1,0:T(8,128)(2,1)S(1)}, bf16[4,56,128]{2,1,0:T(8,128)(2,1)S(1)}, u32[]{:S(2)}, u32[]{:S(2)}) %collective-permute-start.17) | collective-permute-done | bytes 57376 | tf_op jit(solution)/shard_map/ppermute | solution.py:485
  88.5 3.7 %collective-permute-start.19 = (bf16[4,56,128]{2,1,0:T(8,128)(2,1)S(1)}, bf16[4,56,128]{2,1,0:T(8,128)(2,1)S(1)}, u32[]{:S(2)}, u32[]{:S(2)}) collective-permute-start(bf16[4,56,128]{2,1,0:T(8,128)(2,1)S(1)} %fusion.1), channel_id=1, source_target_pairs={{0,16},{1,17},{2,18},{3,19},{4,20},{5,21},{6,22},{7,23},{8,24},{9,... | collective-permute-start | bytes 172040 | tf_op jit(solution)/shard_map/ppermute | solution.py:485
  93.9 4.3 %collective-permute-start.20 = (f32[4,56,128]{2,1,0:T(8,128)S(1)}, f32[4,56,128]{2,1,0:T(8,128)S(1)}, u32[]{:S(2)}, u32[]{:S(2)}) collective-permute-start(f32[4,56,128]{2,1,0:T(8,128)S(1)} %add_multiply_fusion.own_ref), channel_id=1, source_target_pairs={{0,32},{32,0},{64,96},{96,64},{128,160},{160,128},{192,224},{224,1... | collective-permute-start | bytes 344072 | tf_op jit(solution)/shard_map/ppermute | solution.py:470
  (46 shorter events, 15.1 us)
Async XLA Ops:
  2.4 4.5 %collective-permute-start = (bf16[8,64,128]{2,1,0:T(8,128)(2,1)}, bf16[8,64,128]{2,1,0:T(8,128)(2,1)S(1)}, u32[]{:S(2)}, u32[]{:S(2)}) collective-permute-start(bf16[8,64,128]{2,1,0:T(8,128)(2,1)} %get-tuple-element.43), channel_id=1, source_target_pairs={{0,32},{32,0},{64,96},{96,64},{128,160},{160,128},{192,224},{224,1... | collective-permute-start | bytes 393224 | tf_op jit(solution)/shard_map/ppermute | solution.py:470
  7.6 16.5 %copy-start.1 = (f32[3,15,128]{2,1,0:T(8,128)S(1)}, f32[3,15,128]{2,1,0:T(8,128)}, u32[]{:S(2)}) copy-start(f32[3,15,128]{2,1,0:T(8,128)} %refs_8_.5) | copy-start | bytes 69124
  7.6 16.5 %copy-start.2 = (f32[3,128]{1,0:T(4,128)S(1)}, f32[3,128]{1,0:T(4,128)}, u32[]{:S(2)}) copy-start(f32[3,128]{1,0:T(4,128)} %refs_7_.5) | copy-start | bytes 4612
  7.6 11.0 %collective-permute-start.3 = (bf16[560,128]{1,0:T(8,128)(2,1)S(1)}, bf16[560,128]{1,0:T(8,128)(2,1)S(1)}, u32[]{:S(2)}, u32[]{:S(2)}) collective-permute-start(bf16[560,128]{1,0:T(8,128)(2,1)S(1)} %pad_maximum_fusion.refs_0_), channel_id=1, source_target_pairs={{0,192},{32,224},{64,0},{96,32},{128,64},{160,96},{192,128},{224,1... | collective-permute-start | bytes 430088 | tf_op jit(solution)/shard_map/ppermute | solution.py:476
  12.0 12.1 %collective-permute-start.2 = (bf16[560,128]{1,0:T(8,128)(2,1)S(1)}, bf16[560,128]{1,0:T(8,128)(2,1)S(1)}, u32[]{:S(2)}, u32[]{:S(2)}) collective-permute-start(bf16[560,128]{1,0:T(8,128)(2,1)S(1)} %pad_maximum_fusion.refs_0_), channel_id=1, source_target_pairs={{0,128},{32,160},{64,192},{96,224},{128,0},{160,32},{192,64},{224,... | collective-permute-start | bytes 430088 | tf_op jit(solution)/shard_map/ppermute | solution.py:476
  13.0 11.1 %collective-permute-start.1 = (bf16[560,128]{1,0:T(8,128)(2,1)S(1)}, bf16[560,128]{1,0:T(8,128)(2,1)S(1)}, u32[]{:S(2)}, u32[]{:S(2)}) collective-permute-start(bf16[560,128]{1,0:T(8,128)(2,1)S(1)} %pad_maximum_fusion.refs_0_), channel_id=1, source_target_pairs={{0,64},{32,96},{64,128},{96,160},{128,192},{160,224},{192,0},{224,... | collective-permute-start | bytes 430088 | tf_op jit(solution)/shard_map/ppermute | solution.py:476
  27.8 3.6 %collective-permute-start.4 = (bf16[4,4,64,128]{3,2,1,0:T(8,128)(2,1)S(1)}, bf16[4,4,64,128]{3,2,1,0:T(8,128)(2,1)S(1)}, u32[]{:S(2)}, u32[]{:S(2)}) collective-permute-start(bf16[4,4,64,128]{3,2,1,0:T(8,128)(2,1)S(1)} %get-tuple-element.46), channel_id=1, source_target_pairs={{0,32},{32,0},{64,96},{96,64},{128,160},{160,128},{192,224},{224,1... | collective-permute-start | bytes 786440 | tf_op jit(solution)/shard_map/ppermute | solution.py:470
  35.1 15.3 %collective-permute-start.5 = (bf16[4,4,64,128]{3,2,1,0:T(8,128)(2,1)S(1)}, bf16[4,4,64,128]{3,2,1,0:T(8,128)(2,1)S(1)}, u32[]{:S(2)}, u32[]{:S(2)}) collective-permute-start(bf16[4,4,64,128]{3,2,1,0:T(8,128)(2,1)S(1)} %get-tuple-element.50), channel_id=1, source_target_pairs={{0,32},{32,0},{64,96},{96,64},{128,160},{160,128},{192,224},{224,1... | collective-permute-start | bytes 786440 | tf_op jit(solution)/shard_map/ppermute | solution.py:470
  35.6 7.2 %collective-permute-start.8 = (bf16[512,128]{1,0:T(8,128)(2,1)S(1)}, bf16[512,128]{1,0:T(8,128)(2,1)S(1)}, u32[]{:S(2)}, u32[]{:S(2)}) collective-permute-start(bf16[512,128]{1,0:T(8,128)(2,1)S(1)} %pad_maximum_fusion.1.refs_2_), channel_id=1, source_target_pairs={{0,192},{32,224},{64,0},{96,32},{128,64},{160,96},{192,128},{224,1... | collective-permute-start | bytes 393224 | tf_op jit(solution)/shard_map/ppermute | solution.py:476
  39.0 10.9 %collective-permute-start.7 = (bf16[512,128]{1,0:T(8,128)(2,1)S(1)}, bf16[512,128]{1,0:T(8,128)(2,1)S(1)}, u32[]{:S(2)}, u32[]{:S(2)}) collective-permute-start(bf16[512,128]{1,0:T(8,128)(2,1)S(1)} %pad_maximum_fusion.1.refs_2_), channel_id=1, source_target_pairs={{0,128},{32,160},{64,192},{96,224},{128,0},{160,32},{192,64},{224,... | collective-permute-start | bytes 393224 | tf_op jit(solution)/shard_map/ppermute | solution.py:476
  40.8 9.6 %collective-permute-start.6 = (bf16[512,128]{1,0:T(8,128)(2,1)S(1)}, bf16[512,128]{1,0:T(8,128)(2,1)S(1)}, u32[]{:S(2)}, u32[]{:S(2)}) collective-permute-start(bf16[512,128]{1,0:T(8,128)(2,1)S(1)} %pad_maximum_fusion.1.refs_2_), channel_id=1, source_target_pairs={{0,64},{32,96},{64,128},{96,160},{128,192},{160,224},{192,0},{224,... | collective-permute-start | bytes 393224 | tf_op jit(solution)/shard_map/ppermute | solution.py:476
  57.1 3.2 %collective-permute-start.9 = (bf16[4,4,64,128]{3,2,1,0:T(8,128)(2,1)S(1)}, bf16[4,4,64,128]{3,2,1,0:T(8,128)(2,1)S(1)}, u32[]{:S(2)}, u32[]{:S(2)}) collective-permute-start(bf16[4,4,64,128]{3,2,1,0:T(8,128)(2,1)S(1)} %get-tuple-element.53), channel_id=1, source_target_pairs={{0,32},{32,0},{64,96},{96,64},{128,160},{160,128},{192,224},{224,1... | collective-permute-start | bytes 786440 | tf_op jit(solution)/shard_map/ppermute | solution.py:470
  65.0 1.7 %collective-permute-start.10 = (bf16[4,4,64,128]{3,2,1,0:T(8,128)(2,1)S(1)}, bf16[4,4,64,128]{3,2,1,0:T(8,128)(2,1)S(1)}, u32[]{:S(2)}, u32[]{:S(2)}) collective-permute-start(bf16[4,4,64,128]{3,2,1,0:T(8,128)(2,1)S(1)} %get-tuple-element.60), channel_id=1, source_target_pairs={{0,32},{32,0},{64,96},{96,64},{128,160},{160,128},{192,224},{224,1... | collective-permute-start | bytes 786440 | tf_op jit(solution)/shard_map/ppermute | solution.py:470
  65.4 1.3 %collective-permute-start.11 = (bf16[4,64,128]{2,1,0:T(8,128)(2,1)S(1)}, bf16[4,64,128]{2,1,0:T(8,128)(2,1)S(1)}, u32[]{:S(2)}, u32[]{:S(2)}) collective-permute-start(bf16[4,64,128]{2,1,0:T(8,128)(2,1)S(1)} %get-tuple-element.69), channel_id=1, source_target_pairs={{0,32},{32,0},{64,96},{96,64},{128,160},{160,128},{192,224},{224,1... | collective-permute-start | bytes 196616 | tf_op jit(solution)/shard_map/ppermute | solution.py:470
  71.7 1.3 %collective-permute-start.12 = (f32[4,56,128]{2,1,0:T(8,128)S(1)}, f32[4,56,128]{2,1,0:T(8,128)S(1)}, u32[]{:S(2)}, u32[]{:S(2)}) collective-permute-start(f32[4,56,128]{2,1,0:T(8,128)S(1)} %get-tuple-element.72), channel_id=1, source_target_pairs={{0,32},{32,0},{64,96},{96,64},{128,160},{160,128},{192,224},{224,1... | collective-permute-start | bytes 344072 | tf_op jit(solution)/shard_map/ppermute | solution.py:470
  73.1 4.5 %collective-permute-start.15 = (bf16[4,56,128]{2,1,0:T(8,128)(2,1)S(1)}, bf16[4,56,128]{2,1,0:T(8,128)(2,1)S(1)}, u32[]{:S(2)}, u32[]{:S(2)}) collective-permute-start(bf16[4,56,128]{2,1,0:T(8,128)(2,1)S(1)} %fusion), channel_id=1, source_target_pairs={{0,3},{1,0},{2,1},{3,2},{4,7},{5,4},{6,5},{7,6},{8,11},{9,8},{10,9... | collective-permute-start | bytes 172040 | tf_op jit(solution)/shard_map/ppermute | solution.py:485
  75.9 4.6 %collective-permute-start.14 = (bf16[4,56,128]{2,1,0:T(8,128)(2,1)S(1)}, bf16[4,56,128]{2,1,0:T(8,128)(2,1)S(1)}, u32[]{:S(2)}, u32[]{:S(2)}) collective-permute-start(bf16[4,56,128]{2,1,0:T(8,128)(2,1)S(1)} %fusion), channel_id=1, source_target_pairs={{0,1},{1,2},{2,3},{3,0},{4,5},{5,6},{6,7},{7,4},{8,9},{9,10},{10,1... | collective-permute-start | bytes 172040 | tf_op jit(solution)/shard_map/ppermute | solution.py:485
  75.9 4.9 %collective-permute-start.13 = (bf16[4,56,128]{2,1,0:T(8,128)(2,1)S(1)}, bf16[4,56,128]{2,1,0:T(8,128)(2,1)S(1)}, u32[]{:S(2)}, u32[]{:S(2)}) collective-permute-start(bf16[4,56,128]{2,1,0:T(8,128)(2,1)S(1)} %fusion), channel_id=1, source_target_pairs={{0,2},{1,3},{2,0},{3,1},{4,6},{5,7},{6,4},{7,5},{8,10},{9,11},{10,... | collective-permute-start | bytes 172040 | tf_op jit(solution)/shard_map/ppermute | solution.py:485
  80.9 4.5 %collective-permute-start.18 = (bf16[4,56,128]{2,1,0:T(8,128)(2,1)S(1)}, bf16[4,56,128]{2,1,0:T(8,128)(2,1)S(1)}, u32[]{:S(2)}, u32[]{:S(2)}) collective-permute-start(bf16[4,56,128]{2,1,0:T(8,128)(2,1)S(1)} %get-tuple-element.79), channel_id=1, source_target_pairs={{0,12},{1,13},{2,14},{3,15},{4,0},{5,1},{6,2},{7,3},{8,4},{9,5},{1... | collective-permute-start | bytes 172040 | tf_op jit(solution)/shard_map/ppermute | solution.py:485
  83.6 4.9 %collective-permute-start.17 = (bf16[4,56,128]{2,1,0:T(8,128)(2,1)S(1)}, bf16[4,56,128]{2,1,0:T(8,128)(2,1)S(1)}, u32[]{:S(2)}, u32[]{:S(2)}) collective-permute-start(bf16[4,56,128]{2,1,0:T(8,128)(2,1)S(1)} %get-tuple-element.79), channel_id=1, source_target_pairs={{0,4},{1,5},{2,6},{3,7},{4,8},{5,9},{6,10},{7,11},{8,12},{9,13},{1... | collective-permute-start | bytes 172040 | tf_op jit(solution)/shard_map/ppermute | solution.py:485
  83.6 4.9 %collective-permute-start.16 = (bf16[4,56,128]{2,1,0:T(8,128)(2,1)S(1)}, bf16[4,56,128]{2,1,0:T(8,128)(2,1)S(1)}, u32[]{:S(2)}, u32[]{:S(2)}) collective-permute-start(bf16[4,56,128]{2,1,0:T(8,128)(2,1)S(1)} %get-tuple-element.79), channel_id=1, source_target_pairs={{0,8},{1,9},{2,10},{3,11},{4,12},{5,13},{6,14},{7,15},{8,0},{9,1},... | collective-permute-start | bytes 172040 | tf_op jit(solution)/shard_map/ppermute | solution.py:485
  88.5 5.3 %collective-permute-start.19 = (bf16[4,56,128]{2,1,0:T(8,128)(2,1)S(1)}, bf16[4,56,128]{2,1,0:T(8,128)(2,1)S(1)}, u32[]{:S(2)}, u32[]{:S(2)}) collective-permute-start(bf16[4,56,128]{2,1,0:T(8,128)(2,1)S(1)} %fusion.1), channel_id=1, source_target_pairs={{0,16},{1,17},{2,18},{3,19},{4,20},{5,21},{6,22},{7,23},{8,24},{9,... | collective-permute-start | bytes 172040 | tf_op jit(solution)/shard_map/ppermute | solution.py:485
  93.9 5.5 %collective-permute-start.20 = (f32[4,56,128]{2,1,0:T(8,128)S(1)}, f32[4,56,128]{2,1,0:T(8,128)S(1)}, u32[]{:S(2)}, u32[]{:S(2)}) collective-permute-start(f32[4,56,128]{2,1,0:T(8,128)S(1)} %add_multiply_fusion.own_ref), channel_id=1, source_target_pairs={{0,32},{32,0},{64,96},{96,64},{128,160},{160,128},{192,224},{224,1... | collective-permute-start | bytes 344072 | tf_op jit(solution)/shard_map/ppermute | solution.py:470
  98.1 1.3 %collective-permute-start.21 = (bf16[4,64,128]{2,1,0:T(8,128)(2,1)S(1)}, bf16[4,64,128]{2,1,0:T(8,128)(2,1)S(1)}, u32[]{:S(2)}, u32[]{:S(2)}) collective-permute-start(bf16[4,64,128]{2,1,0:T(8,128)(2,1)S(1)} %get-tuple-element.74), channel_id=1, source_target_pairs={{0,32},{32,0},{64,96},{96,64},{128,160},{160,128},{192,224},{224,1... | collective-permute-start | bytes 196616 | tf_op jit(solution)/shard_map/ppermute | solution.py:470
  (4 other events, 25.8 us)

commit v8 on v7

--- a/solution.py
+++ b/solution.py
@@ -216,7 +216,7 @@
     sum_ref[CH:ROWS, :] = jnp.sum(rows_ref[...], axis=1)
 
 
-def prep_kernel(fields_ref, cot_ref, table_ref, begin_ref, keep_ref, keep_cot_ref, send_ref, extra_ref, order_ref, starts_ref, sem):
+def prep_kernel(fields_ref, cot_ref, table_ref, begin_ref, keep_ref, keep_cot_ref, send_ref, order_ref, starts_ref, sem):
     _, core = place_of()
     copies = [
         pltpu.make_async_copy(table_ref, order_ref, sem.at[0]),
@@ -226,7 +226,7 @@
         here = pl.ds(pl.multiple_of((2 * m + core) * Q, Q), Q)
         there = pl.ds(pl.multiple_of((2 * m + 1 - core) * Q, Q), Q)
         for source, own, first in ((fields_ref, keep_ref, 0), (cot_ref, keep_cot_ref, CHIPS)):
-            for rows, target in ((here, own.at[m]), (there, send_ref.at[first + m])):
+            for rows, target in ((here, own.at[pl.ds(m * Q, Q), :]), (there, send_ref.at[first + m])):
                 copies.append(pltpu.make_async_copy(source.at[0, rows, :], target, sem.at[len(copies)]))
     for copy in copies:
         copy.start()
@@ -241,7 +241,7 @@
     for k in range(3):
         rows += [jnp.broadcast_to(starts[k : k + 1, line : line + 1], (1, CH)) for line in range(LINES)]
     rows.append(jnp.zeros((EXTRA - len(rows), CH), F32))
-    extra_ref[...] = jnp.concatenate(rows, axis=0).astype(BF16)
+    keep_ref[HALF : HALF + EXTRA, :] = jnp.concatenate(rows, axis=0).astype(BF16)
     for copy in copies[2:]:
         copy.wait()
 
@@ -513,17 +513,17 @@
     back = (pad, parts, lines, lines)
     wide = (GROUP, LINES, LINE, CH)
 
-    keep, keep_cot, send, extra = call(
+    keep, keep_cot, send = call(
         prep_kernel,
-        (quarter, quarter, shape(NL, Q, CH), shape(EXTRA, CH)),
+        (shape(HALF + EXTRA, CH), shape(HALF, CH), shape(NL, Q, CH)),
         4,
         scratch=(pltpu.VMEM((3, CELLS), I32), pltpu.VMEM((3, LINES), I32), pltpu.SemaphoreType.DMA((18,))),
         space=pltpu.HBM,
         grant=None,
     )(fields, cotangent, line_order, line_starts)
     got = swap(send)
-    piece = jnp.concatenate([keep.reshape(HALF, CH), got[:CHIPS].reshape(HALF, CH), extra])
-    piece_cot = jnp.concatenate([keep_cot.reshape(HALF, CH), got[CHIPS:].reshape(HALF, CH)])
+    piece = jnp.concatenate([keep[:HALF], got[:CHIPS].reshape(HALF, CH), keep[HALF:]])
+    piece_cot = jnp.concatenate([keep_cot, got[CHIPS:].reshape(HALF, CH)])
     pieces = from_chips(piece)
     pieces_cot = from_chips(piece_cot)
     order, starts, same, moved, *saved0 = call(

time: 100 us -> 100 us (level)
  waiting for transfers between devices: 31.2 us -> 30.1 us
    slice x1 -> x3, local copies, waits for them, and re-layouts: 0.01 us -> 1.56 us  [the longest x1 0.84 us: block(): keep[:HALF]]
    ppermute x9, waiting for transfers between devices: 6.77 us -> 5.58 us  [swap(): return lax.ppermute(values, 'line', [(i, i ^ 1) for i in range(NL)])]
  transfers between devices with their start and end apart: 22 -> 22, of which waited for: 14 -> 12; matrix products, arithmetic and copies ran while one was open for 0% -> 2% of each run, Pallas kernels for 0% -> 0%
where the time goes in v8:
time: 100 us; the launch traced here: 99.9 us
  starting transfers between devices  41 us (41%)
  waiting for transfers between devices  30.1 us (30%)
  Pallas kernels  26.2 us (26%)
  local copies, waits for them, and re-layouts  1.58 us (2%)
    ppermute x6, waiting for transfers between devices, from_chips(): lax.ppermute(values, 'line', [(i, (i + 2 * back) % NL) for i in range(NL)])  16.6 us
    ppermute x6, starting transfers between devices, from_chips(): lax.ppermute(values, 'line', [(i, (i + 2 * back) % NL) for i in range(NL)])  14.9 us
    ppermute x9, starting transfers between devices, swap(): return lax.ppermute(values, 'line', [(i, i ^ 1) for i in range(NL)])  13.5 us
    ppermute x7, starting transfers between devices, to_ring(): return lax.ppermute(values, 'dp', pairs)  12.6 us
    ppermute x7, waiting for transfers between devices, to_ring(): return lax.ppermute(values, 'dp', pairs)  7.98 us
    pallas_call x1, Pallas kernels, block(): call(turn_kernel, (moving, moving, quarter, quarter, sums), 11, scratch=(...  6.7 us
    ppermute x9, waiting for transfers between devices, swap(): return lax.ppermute(values, 'line', [(i, i ^ 1) for i in range(NL)])  5.58 us
    pallas_call x1, Pallas kernels, block(): call(functools.partial(backward_kernel, 0), (shape(1, CELLS, CH), quarter...  5.01 us
  transfers between devices with their start and end apart: 22, of which 12 were waited for; matrix products, arithmetic and copies ran while one was open for 2% of the time, Pallas kernels for 0%

profile of v8, /device:TPU:1, one launch (start us, length us, event | category | flops | bytes accessed | tf_op | source)
XLA Modules:
  0.0 99.9 jit_solution(16588307057434876991)
XLA Ops:
  0.6 1.8 %shard_map.110 = (bf16[304,128]{1,0:T(8,128)(2,1)}, bf16[256,128]{1,0:T(8,128)(2,1)}, bf16[8,64,128]{2,1,0:T(8,128)(2,1)}) custom-call(bf16[1,512,128]{2,1,0:T(8,128)(2,1)} %fields_ref.1, bf16[1,512,128]{2,1,0:T(8,128)(2,1)} %cot_ref.1, s32[3,512]{1,0:T(4,128)} %table_ref.1, s32[3,4]{1,0:T(4,128)} %begin_ref.1), custom_call_target="tpu_custom_call" | custom-call | tf_op jit(solution)/shard_map/pallas_call | solution.py:516
  2.4 3.3 %collective-permute-start = (bf16[8,64,128]{2,1,0:T(8,128)(2,1)}, bf16[8,64,128]{2,1,0:T(8,128)(2,1)S(1)}, u32[]{:S(2)}, u32[]{:S(2)}) collective-permute-start(bf16[8,64,128]{2,1,0:T(8,128)(2,1)} %get-tuple-element.42), channel_id=1, source_target_pairs={{0,32},{32,0},{64,96},{96,64},{128,160},{160,128},{192,224},{224,1... | collective-permute-start | bytes 393224 | tf_op jit(solution)/shard_map/ppermute | solution.py:470
  7.3 4.4 %collective-permute-start.3 = (bf16[560,128]{1,0:T(8,128)(2,1)S(1)}, bf16[560,128]{1,0:T(8,128)(2,1)S(1)}, u32[]{:S(2)}, u32[]{:S(2)}) collective-permute-start(bf16[560,128]{1,0:T(8,128)(2,1)S(1)} %pad_maximum_fusion.refs_0_), channel_id=1, source_target_pairs={{0,192},{32,224},{64,0},{96,32},{128,64},{160,96},{192,128},{224,1... | collective-permute-start | bytes 430088 | tf_op jit(solution)/shard_map/ppermute | solution.py:476
  12.7 2.3 %collective-permute-start.1 = (bf16[560,128]{1,0:T(8,128)(2,1)S(1)}, bf16[560,128]{1,0:T(8,128)(2,1)S(1)}, u32[]{:S(2)}, u32[]{:S(2)}) collective-permute-start(bf16[560,128]{1,0:T(8,128)(2,1)S(1)} %pad_maximum_fusion.refs_0_), channel_id=1, source_target_pairs={{0,64},{32,96},{64,128},{96,160},{128,192},{160,224},{192,0},{224,... | collective-permute-start | bytes 430088 | tf_op jit(solution)/shard_map/ppermute | solution.py:476
  15.0 3.4 %collective-permute-done.3.refs_3_ = bf16[560,128]{1,0:T(8,128)(2,1)S(1)} collective-permute-done((bf16[560,128]{1,0:T(8,128)(2,1)S(1)}, bf16[560,128]{1,0:T(8,128)(2,1)S(1)}, u32[]{:S(2)}, u32[]{:S(2)}) %collective-permute-start.3) | collective-permute-done | bytes 143392 | tf_op jit(solution)/shard_map/ppermute | solution.py:476
  18.4 5.6 %collective-permute-done.2.refs_2_ = bf16[560,128]{1,0:T(8,128)(2,1)S(1)} collective-permute-done((bf16[560,128]{1,0:T(8,128)(2,1)S(1)}, bf16[560,128]{1,0:T(8,128)(2,1)S(1)}, u32[]{:S(2)}, u32[]{:S(2)}) %collective-permute-start.2) | collective-permute-done | bytes 143392 | tf_op jit(solution)/shard_map/ppermute | solution.py:476
  24.0 3.7 %shard_map.111 = (s32[3,4,1,512]{3,2,1,0:T(1,128)S(1)}, f32[3,4,4,128]{3,2,1,0:T(4,128)S(1)}, bf16[4,4,64,128]{3,2,1,0:T(8,128)(2,1)S(1)}, bf16[4,4,64,128]{3,2,...) custom-call(bf16[560,128]{1,0:T(8,128)(2,1)S(1)} %pad_maximum_fusion, ...), custom_call_target="tpu_custom_call" | custom-call | tf_op jit(solution)/shard_map/pallas_call | solution.py:529
  27.7 2.0 %collective-permute-start.4 = (bf16[4,4,64,128]{3,2,1,0:T(8,128)(2,1)S(1)}, bf16[4,4,64,128]{3,2,1,0:T(8,128)(2,1)S(1)}, u32[]{:S(2)}, u32[]{:S(2)}) collective-permute-start(bf16[4,4,64,128]{3,2,1,0:T(8,128)(2,1)S(1)} %get-tuple-element.44), channel_id=1, source_target_pairs={{0,32},{32,0},{64,96},{96,64},{128,160},{160,128},{192,224},{224,1... | collective-permute-start | bytes 786440 | tf_op jit(solution)/shard_map/ppermute | solution.py:470
  30.9 3.7 %shard_map.112 = (bf16[4,4,64,128]{3,2,1,0:T(8,128)(2,1)S(1)}, bf16[4,4,64,128]{3,2,1,0:T(8,128)(2,1)S(1)}, bf16[4,4,128,128]{3,2,1,0:T(8,128)(2,1)S(1)}, bf16[4...) custom-call(bf16[4,4,64,128]{3,2,1,0:T(8,128)(2,1)S(1)} %get-tuple-e, ...), custom_call_target="tpu_custom_call" | custom-call | tf_op jit(solution)/shard_map/pallas_call | solution.py:533
  35.0 3.6 %collective-permute-start.8 = (bf16[512,128]{1,0:T(8,128)(2,1)S(1)}, bf16[512,128]{1,0:T(8,128)(2,1)S(1)}, u32[]{:S(2)}, u32[]{:S(2)}) collective-permute-start(bf16[512,128]{1,0:T(8,128)(2,1)S(1)} %pad_maximum_fusion.1.refs_2_), channel_id=1, source_target_pairs={{0,192},{32,224},{64,0},{96,32},{128,64},{160,96},{192,128},{224,1... | collective-permute-start | bytes 393224 | tf_op jit(solution)/shard_map/ppermute | solution.py:476
  40.2 2.0 %collective-permute-start.6 = (bf16[512,128]{1,0:T(8,128)(2,1)S(1)}, bf16[512,128]{1,0:T(8,128)(2,1)S(1)}, u32[]{:S(2)}, u32[]{:S(2)}) collective-permute-start(bf16[512,128]{1,0:T(8,128)(2,1)S(1)} %pad_maximum_fusion.1.refs_2_), channel_id=1, source_target_pairs={{0,64},{32,96},{64,128},{96,160},{128,192},{160,224},{192,0},{224,... | collective-permute-start | bytes 393224 | tf_op jit(solution)/shard_map/ppermute | solution.py:476
  42.3 7.5 %collective-permute-done.7.refs_4_ = bf16[512,128]{1,0:T(8,128)(2,1)S(1)} collective-permute-done((bf16[512,128]{1,0:T(8,128)(2,1)S(1)}, bf16[512,128]{1,0:T(8,128)(2,1)S(1)}, u32[]{:S(2)}, u32[]{:S(2)}) %collective-permute-start.7) | collective-permute-done | bytes 131104 | tf_op jit(solution)/shard_map/ppermute | solution.py:476
  49.8 6.7 %shard_map.113 = (bf16[4,4,64,128]{3,2,1,0:T(8,128)(2,1)S(1)}, bf16[4,4,64,128]{3,2,1,0:T(8,128)(2,1)S(1)}, bf16[4,64,128]{2,1,0:T(8,128)(2,1)S(1)}, bf16[4,64,128]{2,1,0:T(8,128)(2,1)S(1)}, f32[144,128]{1,0:T(8,128)S(1)}) custom-call(bf16[4,4,64,128]{3,2,1,0:T(8,128)(2,1)S(1)} %get-tuple-element.47.refs_0_, ...), custom_call_target="tpu_custom_call" | custom-call | tf_op jit(solution)/shard_map/pallas_call | solution.py:536
  56.5 2.4 %collective-permute-start.9 = (bf16[4,4,64,128]{3,2,1,0:T(8,128)(2,1)S(1)}, bf16[4,4,64,128]{3,2,1,0:T(8,128)(2,1)S(1)}, u32[]{:S(2)}, u32[]{:S(2)}) collective-permute-start(bf16[4,4,64,128]{3,2,1,0:T(8,128)(2,1)S(1)} %get-tuple-element.51), channel_id=1, source_target_pairs={{0,32},{32,0},{64,96},{96,64},{128,160},{160,128},{192,224},{224,1... | collective-permute-start | bytes 786440 | tf_op jit(solution)/shard_map/ppermute | solution.py:470
  60.1 4.6 %shard_map.114 = (bf16[4,4,64,128]{3,2,1,0:T(8,128)(2,1)S(1)}, bf16[4,4,64,128]{3,2,1,0:T(8,128)(2,1)S(1)}, f32[144,128]{1,0:T(8,128)S(1)}) custom-call(bf16[4,4,64,128]{3,2,1,0:T(8,128)(2,1)S(1)} %get-tuple-element.50.refs_0_, bf16[4,4,64,128]{3,2,1,0:T(8,128)(2,1)S(1)} %collective-permute-done.9.refs_1_, ...), custom_call_target="tpu_custom_call" | custom-call | tf_op jit(solution)/shard_map/pallas_call | solution.py:541
  66.4 5.0 %shard_map.115 = (bf16[1,512,128]{2,1,0:T(8,128)(2,1)}, bf16[4,64,128]{2,1,0:T(8,128)(2,1)S(1)}, bf16[4,64,128]{2,1,0:T(8,128)(2,1)S(1)}, f32[4,56,128]{2,1,0:T(8,128)S(1)}, f32[4,56,128]{2,1,0:T(8,128)S(1)}) custom-call(bf16[4,4,64,128]{3,2,1,0:T(8,128)(2,1)S(1)} %get-tuple-element.57.refs_0_, bf16[4,4,64,128]{3,2,1,0:T(8,128)(2,1)S(1)} %collective-permute-done.10.refs_1_, ...), custom_call_target="tpu_custom_call" | custom-call | tf_op jit(solution)/shard_map/pallas_call | solution.py:545
  72.8 2.5 %collective-permute-start.15 = (bf16[4,56,128]{2,1,0:T(8,128)(2,1)S(1)}, bf16[4,56,128]{2,1,0:T(8,128)(2,1)S(1)}, u32[]{:S(2)}, u32[]{:S(2)}) collective-permute-start(bf16[4,56,128]{2,1,0:T(8,128)(2,1)S(1)} %fusion), channel_id=1, source_target_pairs={{0,3},{1,0},{2,1},{3,2},{4,7},{5,4},{6,5},{7,6},{8,11},{9,8},{10,9... | collective-permute-start | bytes 172040 | tf_op jit(solution)/shard_map/ppermute | solution.py:485
  75.3 1.6 %collective-permute-start.13 = (bf16[4,56,128]{2,1,0:T(8,128)(2,1)S(1)}, bf16[4,56,128]{2,1,0:T(8,128)(2,1)S(1)}, u32[]{:S(2)}, u32[]{:S(2)}) collective-permute-start(bf16[4,56,128]{2,1,0:T(8,128)(2,1)S(1)} %fusion), channel_id=1, source_target_pairs={{0,2},{1,3},{2,0},{3,1},{4,6},{5,7},{6,4},{7,5},{8,10},{9,11},{10,... | collective-permute-start | bytes 172040 | tf_op jit(solution)/shard_map/ppermute | solution.py:485
  77.0 2.9 %collective-permute-done.14 = bf16[4,56,128]{2,1,0:T(8,128)(2,1)S(1)} collective-permute-done((bf16[4,56,128]{2,1,0:T(8,128)(2,1)S(1)}, bf16[4,56,128]{2,1,0:T(8,128)(2,1)S(1)}, u32[]{:S(2)}, u32[]{:S(2)}) %collective-permute-start.14) | collective-permute-done | bytes 57376 | tf_op jit(solution)/shard_map/ppermute | solution.py:485
  80.3 2.8 %collective-permute-start.18 = (bf16[4,56,128]{2,1,0:T(8,128)(2,1)S(1)}, bf16[4,56,128]{2,1,0:T(8,128)(2,1)S(1)}, u32[]{:S(2)}, u32[]{:S(2)}) collective-permute-start(bf16[4,56,128]{2,1,0:T(8,128)(2,1)S(1)} %get-tuple-element.77), channel_id=1, source_target_pairs={{0,12},{1,13},{2,14},{3,15},{4,0},{5,1},{6,2},{7,3},{8,4},{9,5},{1... | collective-permute-start | bytes 172040 | tf_op jit(solution)/shard_map/ppermute | solution.py:485
  83.1 1.7 %collective-permute-start.16 = (bf16[4,56,128]{2,1,0:T(8,128)(2,1)S(1)}, bf16[4,56,128]{2,1,0:T(8,128)(2,1)S(1)}, u32[]{:S(2)}, u32[]{:S(2)}) collective-permute-start(bf16[4,56,128]{2,1,0:T(8,128)(2,1)S(1)} %get-tuple-element.77), channel_id=1, source_target_pairs={{0,8},{1,9},{2,10},{3,11},{4,12},{5,13},{6,14},{7,15},{8,0},{9,1},... | collective-permute-start | bytes 172040 | tf_op jit(solution)/shard_map/ppermute | solution.py:485
  84.8 3.1 %collective-permute-done.17 = bf16[4,56,128]{2,1,0:T(8,128)(2,1)S(1)} collective-permute-done((bf16[4,56,128]{2,1,0:T(8,128)(2,1)S(1)}, bf16[4,56,128]{2,1,0:T(8,128)(2,1)S(1)}, u32[]{:S(2)}, u32[]{:S(2)}) %collective-permute-start.17) | collective-permute-done | bytes 57376 | tf_op jit(solution)/shard_map/ppermute | solution.py:485
  88.0 3.9 %collective-permute-start.19 = (bf16[4,56,128]{2,1,0:T(8,128)(2,1)S(1)}, bf16[4,56,128]{2,1,0:T(8,128)(2,1)S(1)}, u32[]{:S(2)}, u32[]{:S(2)}) collective-permute-start(bf16[4,56,128]{2,1,0:T(8,128)(2,1)S(1)} %fusion.1), channel_id=1, source_target_pairs={{0,16},{1,17},{2,18},{3,19},{4,20},{5,21},{6,22},{7,23},{8,24},{9,... | collective-permute-start | bytes 172040 | tf_op jit(solution)/shard_map/ppermute | solution.py:485
  93.5 4.3 %collective-permute-start.20 = (f32[4,56,128]{2,1,0:T(8,128)S(1)}, f32[4,56,128]{2,1,0:T(8,128)S(1)}, u32[]{:S(2)}, u32[]{:S(2)}) collective-permute-start(f32[4,56,128]{2,1,0:T(8,128)S(1)} %add_multiply_fusion.own_ref), channel_id=1, source_target_pairs={{0,32},{32,0},{64,96},{96,64},{128,160},{160,128},{192,224},{224,1... | collective-permute-start | bytes 344072 | tf_op jit(solution)/shard_map/ppermute | solution.py:470
  (44 shorter events, 14.2 us)
Async XLA Ops:
  2.4 4.8 %collective-permute-start = (bf16[8,64,128]{2,1,0:T(8,128)(2,1)}, bf16[8,64,128]{2,1,0:T(8,128)(2,1)S(1)}, u32[]{:S(2)}, u32[]{:S(2)}) collective-permute-start(bf16[8,64,128]{2,1,0:T(8,128)(2,1)} %get-tuple-element.42), channel_id=1, source_target_pairs={{0,32},{32,0},{64,96},{96,64},{128,160},{160,128},{192,224},{224,1... | collective-permute-start | bytes 393224 | tf_op jit(solution)/shard_map/ppermute | solution.py:470
  7.3 16.7 %copy-start = (bf16[3,128,128]{2,1,0:T(8,128)(2,1)S(1)}, bf16[3,128,128]{2,1,0:T(8,128)(2,1)}, u32[]{:S(2)}) copy-start(bf16[3,128,128]{2,1,0:T(8,128)(2,1)} %refs_9_.3) | copy-start | bytes 294916
  7.3 16.7 %copy-start.1 = (f32[3,15,128]{2,1,0:T(8,128)S(1)}, f32[3,15,128]{2,1,0:T(8,128)}, u32[]{:S(2)}) copy-start(f32[3,15,128]{2,1,0:T(8,128)} %refs_8_.5) | copy-start | bytes 69124
  7.3 11.0 %collective-permute-start.3 = (bf16[560,128]{1,0:T(8,128)(2,1)S(1)}, bf16[560,128]{1,0:T(8,128)(2,1)S(1)}, u32[]{:S(2)}, u32[]{:S(2)}) collective-permute-start(bf16[560,128]{1,0:T(8,128)(2,1)S(1)} %pad_maximum_fusion.refs_0_), channel_id=1, source_target_pairs={{0,192},{32,224},{64,0},{96,32},{128,64},{160,96},{192,128},{224,1... | collective-permute-start | bytes 430088 | tf_op jit(solution)/shard_map/ppermute | solution.py:476
  11.7 12.3 %collective-permute-start.2 = (bf16[560,128]{1,0:T(8,128)(2,1)S(1)}, bf16[560,128]{1,0:T(8,128)(2,1)S(1)}, u32[]{:S(2)}, u32[]{:S(2)}) collective-permute-start(bf16[560,128]{1,0:T(8,128)(2,1)S(1)} %pad_maximum_fusion.refs_0_), channel_id=1, source_target_pairs={{0,128},{32,160},{64,192},{96,224},{128,0},{160,32},{192,64},{224,... | collective-permute-start | bytes 430088 | tf_op jit(solution)/shard_map/ppermute | solution.py:476
  12.7 11.3 %collective-permute-start.1 = (bf16[560,128]{1,0:T(8,128)(2,1)S(1)}, bf16[560,128]{1,0:T(8,128)(2,1)S(1)}, u32[]{:S(2)}, u32[]{:S(2)}) collective-permute-start(bf16[560,128]{1,0:T(8,128)(2,1)S(1)} %pad_maximum_fusion.refs_0_), channel_id=1, source_target_pairs={{0,64},{32,96},{64,128},{96,160},{128,192},{160,224},{192,0},{224,... | collective-permute-start | bytes 430088 | tf_op jit(solution)/shard_map/ppermute | solution.py:476
  27.7 3.2 %collective-permute-start.4 = (bf16[4,4,64,128]{3,2,1,0:T(8,128)(2,1)S(1)}, bf16[4,4,64,128]{3,2,1,0:T(8,128)(2,1)S(1)}, u32[]{:S(2)}, u32[]{:S(2)}) collective-permute-start(bf16[4,4,64,128]{3,2,1,0:T(8,128)(2,1)S(1)} %get-tuple-element.44), channel_id=1, source_target_pairs={{0,32},{32,0},{64,96},{96,64},{128,160},{160,128},{192,224},{224,1... | collective-permute-start | bytes 786440 | tf_op jit(solution)/shard_map/ppermute | solution.py:470
  34.6 15.2 %collective-permute-start.5 = (bf16[4,4,64,128]{3,2,1,0:T(8,128)(2,1)S(1)}, bf16[4,4,64,128]{3,2,1,0:T(8,128)(2,1)S(1)}, u32[]{:S(2)}, u32[]{:S(2)}) collective-permute-start(bf16[4,4,64,128]{3,2,1,0:T(8,128)(2,1)S(1)} %get-tuple-element.48), channel_id=1, source_target_pairs={{0,32},{32,0},{64,96},{96,64},{128,160},{160,128},{192,224},{224,1... | collective-permute-start | bytes 786440 | tf_op jit(solution)/shard_map/ppermute | solution.py:470
  35.0 7.2 %collective-permute-start.8 = (bf16[512,128]{1,0:T(8,128)(2,1)S(1)}, bf16[512,128]{1,0:T(8,128)(2,1)S(1)}, u32[]{:S(2)}, u32[]{:S(2)}) collective-permute-start(bf16[512,128]{1,0:T(8,128)(2,1)S(1)} %pad_maximum_fusion.1.refs_2_), channel_id=1, source_target_pairs={{0,192},{32,224},{64,0},{96,32},{128,64},{160,96},{192,128},{224,1... | collective-permute-start | bytes 393224 | tf_op jit(solution)/shard_map/ppermute | solution.py:476
  38.6 11.1 %collective-permute-start.7 = (bf16[512,128]{1,0:T(8,128)(2,1)S(1)}, bf16[512,128]{1,0:T(8,128)(2,1)S(1)}, u32[]{:S(2)}, u32[]{:S(2)}) collective-permute-start(bf16[512,128]{1,0:T(8,128)(2,1)S(1)} %pad_maximum_fusion.1.refs_2_), channel_id=1, source_target_pairs={{0,128},{32,160},{64,192},{96,224},{128,0},{160,32},{192,64},{224,... | collective-permute-start | bytes 393224 | tf_op jit(solution)/shard_map/ppermute | solution.py:476
  40.2 9.5 %collective-permute-start.6 = (bf16[512,128]{1,0:T(8,128)(2,1)S(1)}, bf16[512,128]{1,0:T(8,128)(2,1)S(1)}, u32[]{:S(2)}, u32[]{:S(2)}) collective-permute-start(bf16[512,128]{1,0:T(8,128)(2,1)S(1)} %pad_maximum_fusion.1.refs_2_), channel_id=1, source_target_pairs={{0,64},{32,96},{64,128},{96,160},{128,192},{160,224},{192,0},{224,... | collective-permute-start | bytes 393224 | tf_op jit(solution)/shard_map/ppermute | solution.py:476
  56.5 3.6 %collective-permute-start.9 = (bf16[4,4,64,128]{3,2,1,0:T(8,128)(2,1)S(1)}, bf16[4,4,64,128]{3,2,1,0:T(8,128)(2,1)S(1)}, u32[]{:S(2)}, u32[]{:S(2)}) collective-permute-start(bf16[4,4,64,128]{3,2,1,0:T(8,128)(2,1)S(1)} %get-tuple-element.51), channel_id=1, source_target_pairs={{0,32},{32,0},{64,96},{96,64},{128,160},{160,128},{192,224},{224,1... | collective-permute-start | bytes 786440 | tf_op jit(solution)/shard_map/ppermute | solution.py:470
  64.7 1.7 %collective-permute-start.10 = (bf16[4,4,64,128]{3,2,1,0:T(8,128)(2,1)S(1)}, bf16[4,4,64,128]{3,2,1,0:T(8,128)(2,1)S(1)}, u32[]{:S(2)}, u32[]{:S(2)}) collective-permute-start(bf16[4,4,64,128]{3,2,1,0:T(8,128)(2,1)S(1)} %get-tuple-element.58), channel_id=1, source_target_pairs={{0,32},{32,0},{64,96},{96,64},{128,160},{160,128},{192,224},{224,1... | collective-permute-start | bytes 786440 | tf_op jit(solution)/shard_map/ppermute | solution.py:470
  65.2 1.3 %collective-permute-start.11 = (bf16[4,64,128]{2,1,0:T(8,128)(2,1)S(1)}, bf16[4,64,128]{2,1,0:T(8,128)(2,1)S(1)}, u32[]{:S(2)}, u32[]{:S(2)}) collective-permute-start(bf16[4,64,128]{2,1,0:T(8,128)(2,1)S(1)} %get-tuple-element.67), channel_id=1, source_target_pairs={{0,32},{32,0},{64,96},{96,64},{128,160},{160,128},{192,224},{224,1... | collective-permute-start | bytes 196616 | tf_op jit(solution)/shard_map/ppermute | solution.py:470
  71.4 1.3 %collective-permute-start.12 = (f32[4,56,128]{2,1,0:T(8,128)S(1)}, f32[4,56,128]{2,1,0:T(8,128)S(1)}, u32[]{:S(2)}, u32[]{:S(2)}) collective-permute-start(f32[4,56,128]{2,1,0:T(8,128)S(1)} %get-tuple-element.70), channel_id=1, source_target_pairs={{0,32},{32,0},{64,96},{96,64},{128,160},{160,128},{192,224},{224,1... | collective-permute-start | bytes 344072 | tf_op jit(solution)/shard_map/ppermute | solution.py:470
  72.8 4.2 %collective-permute-start.15 = (bf16[4,56,128]{2,1,0:T(8,128)(2,1)S(1)}, bf16[4,56,128]{2,1,0:T(8,128)(2,1)S(1)}, u32[]{:S(2)}, u32[]{:S(2)}) collective-permute-start(bf16[4,56,128]{2,1,0:T(8,128)(2,1)S(1)} %fusion), channel_id=1, source_target_pairs={{0,3},{1,0},{2,1},{3,2},{4,7},{5,4},{6,5},{7,6},{8,11},{9,8},{10,9... | collective-permute-start | bytes 172040 | tf_op jit(solution)/shard_map/ppermute | solution.py:485
  75.3 4.6 %collective-permute-start.14 = (bf16[4,56,128]{2,1,0:T(8,128)(2,1)S(1)}, bf16[4,56,128]{2,1,0:T(8,128)(2,1)S(1)}, u32[]{:S(2)}, u32[]{:S(2)}) collective-permute-start(bf16[4,56,128]{2,1,0:T(8,128)(2,1)S(1)} %fusion), channel_id=1, source_target_pairs={{0,1},{1,2},{2,3},{3,0},{4,5},{5,6},{6,7},{7,4},{8,9},{9,10},{10,1... | collective-permute-start | bytes 172040 | tf_op jit(solution)/shard_map/ppermute | solution.py:485
  75.3 4.9 %collective-permute-start.13 = (bf16[4,56,128]{2,1,0:T(8,128)(2,1)S(1)}, bf16[4,56,128]{2,1,0:T(8,128)(2,1)S(1)}, u32[]{:S(2)}, u32[]{:S(2)}) collective-permute-start(bf16[4,56,128]{2,1,0:T(8,128)(2,1)S(1)} %fusion), channel_id=1, source_target_pairs={{0,2},{1,3},{2,0},{3,1},{4,6},{5,7},{6,4},{7,5},{8,10},{9,11},{10,... | collective-permute-start | bytes 172040 | tf_op jit(solution)/shard_map/ppermute | solution.py:485
  80.3 4.5 %collective-permute-start.18 = (bf16[4,56,128]{2,1,0:T(8,128)(2,1)S(1)}, bf16[4,56,128]{2,1,0:T(8,128)(2,1)S(1)}, u32[]{:S(2)}, u32[]{:S(2)}) collective-permute-start(bf16[4,56,128]{2,1,0:T(8,128)(2,1)S(1)} %get-tuple-element.77), channel_id=1, source_target_pairs={{0,12},{1,13},{2,14},{3,15},{4,0},{5,1},{6,2},{7,3},{8,4},{9,5},{1... | collective-permute-start | bytes 172040 | tf_op jit(solution)/shard_map/ppermute | solution.py:485
  83.1 4.9 %collective-permute-start.17 = (bf16[4,56,128]{2,1,0:T(8,128)(2,1)S(1)}, bf16[4,56,128]{2,1,0:T(8,128)(2,1)S(1)}, u32[]{:S(2)}, u32[]{:S(2)}) collective-permute-start(bf16[4,56,128]{2,1,0:T(8,128)(2,1)S(1)} %get-tuple-element.77), channel_id=1, source_target_pairs={{0,4},{1,5},{2,6},{3,7},{4,8},{5,9},{6,10},{7,11},{8,12},{9,13},{1... | collective-permute-start | bytes 172040 | tf_op jit(solution)/shard_map/ppermute | solution.py:485
  83.1 4.9 %collective-permute-start.16 = (bf16[4,56,128]{2,1,0:T(8,128)(2,1)S(1)}, bf16[4,56,128]{2,1,0:T(8,128)(2,1)S(1)}, u32[]{:S(2)}, u32[]{:S(2)}) collective-permute-start(bf16[4,56,128]{2,1,0:T(8,128)(2,1)S(1)} %get-tuple-element.77), channel_id=1, source_target_pairs={{0,8},{1,9},{2,10},{3,11},{4,12},{5,13},{6,14},{7,15},{8,0},{9,1},... | collective-permute-start | bytes 172040 | tf_op jit(solution)/shard_map/ppermute | solution.py:485
  88.0 5.5 %collective-permute-start.19 = (bf16[4,56,128]{2,1,0:T(8,128)(2,1)S(1)}, bf16[4,56,128]{2,1,0:T(8,128)(2,1)S(1)}, u32[]{:S(2)}, u32[]{:S(2)}) collective-permute-start(bf16[4,56,128]{2,1,0:T(8,128)(2,1)S(1)} %fusion.1), channel_id=1, source_target_pairs={{0,16},{1,17},{2,18},{3,19},{4,20},{5,21},{6,22},{7,23},{8,24},{9,... | collective-permute-start | bytes 172040 | tf_op jit(solution)/shard_map/ppermute | solution.py:485
  93.5 5.5 %collective-permute-start.20 = (f32[4,56,128]{2,1,0:T(8,128)S(1)}, f32[4,56,128]{2,1,0:T(8,128)S(1)}, u32[]{:S(2)}, u32[]{:S(2)}) collective-permute-start(f32[4,56,128]{2,1,0:T(8,128)S(1)} %add_multiply_fusion.own_ref), channel_id=1, source_target_pairs={{0,32},{32,0},{64,96},{96,64},{128,160},{160,128},{192,224},{224,1... | collective-permute-start | bytes 344072 | tf_op jit(solution)/shard_map/ppermute | solution.py:470
  97.8 1.3 %collective-permute-start.21 = (bf16[4,64,128]{2,1,0:T(8,128)(2,1)S(1)}, bf16[4,64,128]{2,1,0:T(8,128)(2,1)S(1)}, u32[]{:S(2)}, u32[]{:S(2)}) collective-permute-start(bf16[4,64,128]{2,1,0:T(8,128)(2,1)S(1)} %get-tuple-element.72), channel_id=1, source_target_pairs={{0,32},{32,0},{64,96},{96,64},{128,160},{160,128},{192,224},{224,1... | collective-permute-start | bytes 196616 | tf_op jit(solution)/shard_map/ppermute | solution.py:470
  (2 other events, 20.9 us)
